TPU v7x, 32 devices: a whole 2x2x4 slice. The times are simulated.
32 devices in a mesh: dp: 8 (over z, y), tensor: 4 (over x, core).
Axes of the slice: x: 2, y: 2, z: 4, core: 2. Of those that a mesh axis runs over, the one named last changes fastest.
Arguments:
- tokens: bfloat16 [2048, 4096], P('dp', 'tensor'), may hold values from -24 to 24
- segments: int32 [16, 128], P('dp'), may hold values from 0 to 3, never falling along the last dimension, each value on 1 to 96 neighbouring positions
- w_query: bfloat16 [4096, 4096], P('dp', 'tensor'), may hold values from -1 to 1
- key_weight: bfloat16 [4096, 1024], P('dp', 'tensor'), may hold values from -1 to 1
- value_weight: bfloat16 [4096, 1024], P('dp', 'tensor'), may hold values from -0.09375 to 0.09375
- w_out: bfloat16 [4096, 4096], P('dp', 'tensor'), may hold values from -0.375 to 0.375
- w_gate: bfloat16 [4096, 12288], P('dp', 'tensor'), may hold values from -0.09375 to 0.09375
- w_up: bfloat16 [4096, 12288], P('dp', 'tensor'), may hold values from -0.09375 to 0.09375
- w_down: bfloat16 [4096, 12288], P('dp', 'tensor'), may hold values from -0.0546875 to 0.0546875
- attn_gain: float32 [4096], P(('dp', 'tensor')), may hold values from 0.25 to 1.75
- ffn_gain: float32 [4096], P(('dp', 'tensor')), may hold values from 0.25 to 1.75
- query_norm_gain: float32 [128], replicated, may hold values from 0.6 to 5
- key_gain: float32 [128], replicated, may hold values from 0.6 to 5
- cotangent: bfloat16 [2048, 4096], P('dp', 'tensor'), may hold values from -6 to 6
Outputs:
- block_out: bfloat16 [2048, 4096], P('dp', 'tensor')
- tokens_grad: float32 [2048, 4096], P('dp', 'tensor')
- w_query_grad: float32 [4096, 4096], P('dp', 'tensor')
- w_key_grad: float32 [4096, 1024], P('dp', 'tensor')
- w_value_grad: float32 [4096, 1024], P('dp', 'tensor')
- w_out_grad: float32 [4096, 4096], P('dp', 'tensor')
- w_gate_grad: float32 [4096, 12288], P('dp', 'tensor')
- w_up_grad: float32 [4096, 12288], P('dp', 'tensor')
- w_down_grad: float32 [4096, 12288], P('dp', 'tensor')
- attn_gain_grad: float32 [4096], P(('dp', 'tensor'))
- ffn_gain_grad: float32 [4096], P(('dp', 'tensor'))
- query_gain_grad: float32 [128], replicated
- key_gain_grad: float32 [128], replicated
Inputs may be any that keep to these rules, and one draw needn't show every extreme that they name: `segments`: in each row (one micro-batch) the sequence numbers never fall, every number of 0 to 3 occurs, each sequence holds 1 to 96 rows, and one holds exactly that many.
All inputs are finite; a program needn't handle non-finite values.
Results may differ from a plain program's by a relative error of at most 0.017.
The roundings to bfloat16 on the way count: a program that leaves them out, or rounds other values in their place, can miss the bound.
Values may be sent and summed in bfloat16 or wider, within the bound.
No kernel may reach another device: no remote copies, remote signals or barrier semaphores. Data moves between devices by JAX's collectives and lax.ppermute only.
A program may use at most 384 MiB of HBM per device.

v0:
```python
import jax
import jax.numpy as jnp
from jax import lax
from jax.sharding import PartitionSpec as P

epsilon = 1e-06
rope_base = 1000000.0
masked_score = -1e30


def rope_tables(segment, head_size):
    token_row_count = segment.shape[0]
    starts = jnp.sum((segment[None, :] < segment[:, None]).astype(jnp.int32), axis=1)
    position = (jnp.arange(token_row_count, dtype=jnp.int32) - starts).astype(jnp.float32)
    half_size = head_size // 2
    frequency = jnp.power(rope_base, -2.0 * jnp.arange(half_size, dtype=jnp.float32) / head_size)
    angles = position[:, None] * frequency[None, :]
    angles = jnp.concatenate([angles, angles], axis=1)
    return (jnp.cos(angles)[:, None, :], jnp.sin(angles)[:, None, :])


def visible(segment):
    token_row_count = segment.shape[0]
    row_order = jnp.arange(token_row_count, dtype=jnp.int32)
    return (segment[:, None] == segment[None, :]) & (row_order[:, None] >= row_order[None, :])


def apply_rotary(value_rows, cosine_table, sine_table):
    half_size = value_rows.shape[-1] // 2
    turned = jnp.concatenate([-value_rows[..., half_size:], value_rows[..., :half_size]], axis=-1)
    return value_rows * cosine_table + turned * sine_table


def rotate_back(upstream, cosine_table, sine_table):
    scaled = upstream * sine_table
    half_size = upstream.shape[-1] // 2
    turned = jnp.concatenate([scaled[..., half_size:], -scaled[..., :half_size]], axis=-1)
    return upstream * cosine_table + turned


def norm_back(upstream, normed, inverse, gain_vector):
    scaled = upstream * gain_vector
    return inverse * (scaled - normed * jnp.mean(scaled * normed, axis=-1, keepdims=True))


def project(left_side, right_side):
    return jnp.dot(left_side, right_side, preferred_element_type=jnp.float32)


def project_back(left_side, right_side):
    return lax.dot_general(
        left_side, right_side, (((1,), (1,)), ((), ())), preferred_element_type=jnp.float32
    )


def outer_sum(left_side, right_side):
    return lax.dot_general(
        left_side, right_side, (((0,), (0,)), ((), ())), preferred_element_type=jnp.float32
    )


def fetch_attention(shards):
    return (
        lax.all_gather(shards[0], "dp", axis=0, tiled=True),
        lax.all_gather(shards[1], "dp", axis=0, tiled=True),
        lax.all_gather(shards[2], "dp", axis=0, tiled=True),
        lax.all_gather(shards[3], "dp", axis=0, tiled=True),
    )


def fetch_attention_back(shards):
    return (
        lax.all_gather(shards[0], "dp", axis=0, tiled=True),
        lax.all_gather(shards[1], "dp", axis=0, tiled=True),
        lax.all_gather(shards[2], "dp", axis=0, tiled=True),
        lax.all_gather(shards[3], "dp", axis=0, tiled=True),
    )


def fetch_feedforward(shards):
    return (
        lax.all_gather(shards[4], "dp", axis=0, tiled=True),
        lax.all_gather(shards[5], "dp", axis=0, tiled=True),
        lax.all_gather(shards[6], "dp", axis=0, tiled=True),
    )


def forward_part(
    x_piece, segment, attn_weights, ffn_weights, attn_full, ffn_full, query_norm_gain, key_gain
):
    w_query, key_weight, value_weight, w_out = attn_weights
    w_gate, w_up, w_down = ffn_weights
    head_size = query_norm_gain.shape[0]
    token_row_count = x_piece.shape[0]
    query_heads = w_query.shape[1] // head_size
    kv_heads = key_weight.shape[1] // head_size
    head_groups = query_heads // kv_heads
    x_whole = lax.all_gather(x_piece, "tensor", axis=1, tiled=True)
    x_float = x_whole.astype(jnp.float32)
    inverse_one = lax.rsqrt(jnp.mean(x_float * x_float, axis=1, keepdims=True) + epsilon)
    first_hidden = (x_float * inverse_one * attn_full).astype(jnp.bfloat16)
    query_before_norm = project(first_hidden, w_query).reshape(
        token_row_count, query_heads, head_size
    )
    key_before_norm = project(first_hidden, key_weight).reshape(
        token_row_count, kv_heads, head_size
    )
    value_reduced = (
        project(first_hidden, value_weight)
        .astype(jnp.bfloat16)
        .reshape(token_row_count, kv_heads, head_size)
    )
    cosine_table, sine_table = rope_tables(segment, head_size)
    query_inv = lax.rsqrt(
        jnp.mean(query_before_norm * query_before_norm, axis=2, keepdims=True) + epsilon
    )
    key_inv = lax.rsqrt(
        jnp.mean(key_before_norm * key_before_norm, axis=2, keepdims=True) + epsilon
    )
    query_rotated = apply_rotary(
        query_before_norm * query_inv * query_norm_gain, cosine_table, sine_table
    ).astype(jnp.bfloat16)
    query_rotated = query_rotated.reshape(token_row_count, kv_heads, head_groups, head_size)
    key_rot = apply_rotary(key_before_norm * key_inv * key_gain, cosine_table, sine_table).astype(
        jnp.bfloat16
    )
    allowed = visible(segment)[None, None]
    score_scale = head_size ** (-0.5)
    scores = (
        jnp.einsum("qkgd,skd->kgqs", query_rotated, key_rot, preferred_element_type=jnp.float32)
        * score_scale
    )
    scores = jnp.where(allowed, scores, masked_score)
    top_score = jnp.max(scores, axis=3, keepdims=True)
    exp_scores = jnp.exp(scores - top_score)
    row_totals = jnp.sum(exp_scores, axis=3, keepdims=True)
    probs_low = (exp_scores / row_totals).astype(jnp.bfloat16)
    log_total = top_score + jnp.log(row_totals)
    mixed_heads = jnp.einsum(
        "kgqs,skd->qkgd", probs_low, value_reduced, preferred_element_type=jnp.float32
    )
    mixed_low = mixed_heads.astype(jnp.bfloat16).reshape(token_row_count, query_heads * head_size)
    attn_piece = lax.psum_scatter(
        project_back(mixed_low, w_out), "tensor", scatter_dimension=1, tiled=True
    )
    resid_piece = x_piece.astype(jnp.float32) + attn_piece
    resid_whole = lax.all_gather(resid_piece, "tensor", axis=1, tiled=True)
    inverse_two = lax.rsqrt(jnp.mean(resid_whole * resid_whole, axis=1, keepdims=True) + epsilon)
    hidden_two = (resid_whole * inverse_two * ffn_full).astype(jnp.bfloat16)
    gate_pre = project(hidden_two, w_gate)
    up_proj = project(hidden_two, w_up)
    act_low = (jax.nn.silu(gate_pre) * up_proj).astype(jnp.bfloat16)
    ffn_piece = lax.psum_scatter(
        project_back(act_low, w_down).astype(jnp.bfloat16),
        "tensor",
        scatter_dimension=1,
        tiled=True,
    ).astype(jnp.float32)
    out_piece = (resid_piece + ffn_piece).astype(jnp.bfloat16)
    saved_state = (
        x_float,
        inverse_one,
        first_hidden,
        query_before_norm,
        query_inv,
        key_before_norm,
        key_inv,
        value_reduced,
        query_rotated,
        key_rot,
        cosine_table,
        sine_table,
        allowed,
        log_total,
        mixed_low,
        resid_piece,
        resid_whole,
        inverse_two,
        hidden_two,
        gate_pre,
        up_proj,
        act_low,
    )
    return (out_piece, saved_state)


def feedforward_back(dy_piece, saved_state, ffn_weights, ffn_full, ffn_slice):
    (
        x_float,
        inverse_one,
        first_hidden,
        query_before_norm,
        query_inv,
        key_before_norm,
        key_inv,
        value_reduced,
        query_rotated,
        key_rot,
        cosine_table,
        sine_table,
        allowed,
        log_total,
        mixed_low,
        resid_piece,
        resid_whole,
        inverse_two,
        hidden_two,
        gate_pre,
        up_proj,
        act_low,
    ) = saved_state
    w_gate, w_up, w_down = ffn_weights
    token_row_count = dy_piece.shape[0]
    model_width = x_float.shape[1]
    tensor_size = lax.axis_size("tensor")
    dy_whole = lax.all_gather(dy_piece, "tensor", axis=1, tiled=True)
    d_act = project(dy_whole, w_down)
    grad_down = outer_sum(dy_whole, act_low)
    sigmoid_gate = jax.nn.sigmoid(gate_pre)
    d_gate = (d_act * up_proj * sigmoid_gate * (1.0 + gate_pre * (1.0 - sigmoid_gate))).astype(
        jnp.bfloat16
    )
    d_up = (d_act * (gate_pre * sigmoid_gate)).astype(jnp.bfloat16)
    grad_gate = outer_sum(hidden_two, d_gate)
    grad_up = outer_sum(hidden_two, d_up)
    d_hidden_two = project_back(d_gate, w_gate) + project_back(d_up, w_up)
    normed_two = resid_whole * inverse_two
    ffn_gain_part = jnp.sum(d_hidden_two * normed_two, axis=0)
    stat_two = jnp.sum(d_hidden_two * ffn_full * normed_two, axis=1, keepdims=True)
    d_norm_two, stat_two_sum = (
        lax.psum_scatter(d_hidden_two, "tensor", scatter_dimension=1, tiled=True),
        lax.psum_scatter(
            jnp.broadcast_to(stat_two, (token_row_count, tensor_size)),
            "tensor",
            scatter_dimension=1,
            tiled=True,
        ),
    )
    d_resid = dy_piece.astype(jnp.float32) + inverse_two * (
        d_norm_two * ffn_slice - resid_piece * inverse_two * stat_two_sum / model_width
    )
    return (d_resid, (grad_gate, grad_up, grad_down), ffn_gain_part)


def attention_back(
    d_resid, x_piece, saved_state, attn_weights, attn_full, attn_slice, query_norm_gain, key_gain
):
    (
        x_float,
        inverse_one,
        first_hidden,
        query_before_norm,
        query_inv,
        key_before_norm,
        key_inv,
        value_reduced,
        query_rotated,
        key_rot,
        cosine_table,
        sine_table,
        allowed,
        log_total,
        mixed_low,
        resid_piece,
        resid_whole,
        inverse_two,
        hidden_two,
        gate_pre,
        up_proj,
        act_low,
    ) = saved_state
    w_query, key_weight, value_weight, w_out = attn_weights
    token_row_count = x_piece.shape[0]
    model_width = x_float.shape[1]
    tensor_size = lax.axis_size("tensor")
    head_size = query_norm_gain.shape[0]
    query_heads = query_before_norm.shape[1]
    kv_heads = key_before_norm.shape[1]
    head_groups = query_heads // kv_heads
    score_scale = head_size ** (-0.5)
    d_resid_low = d_resid.astype(jnp.bfloat16)
    d_resid_whole = lax.all_gather(d_resid_low, "tensor", axis=1, tiled=True)
    grad_out = outer_sum(d_resid_whole, mixed_low)
    d_mixed = (
        project(d_resid_whole, w_out)
        .astype(jnp.bfloat16)
        .reshape(token_row_count, kv_heads, head_groups, head_size)
    )
    scores = (
        jnp.einsum("qkgd,skd->kgqs", query_rotated, key_rot, preferred_element_type=jnp.float32)
        * score_scale
    )
    probability = jnp.exp(jnp.where(allowed, scores, masked_score) - log_total)
    d_probs = jnp.einsum(
        "qkgd,skd->kgqs", d_mixed, value_reduced, preferred_element_type=jnp.float32
    )
    row_delta = jnp.sum(probability * d_probs, axis=3, keepdims=True)
    d_scores = (probability * (d_probs - row_delta)).astype(jnp.bfloat16)
    d_value = jnp.einsum(
        "kgqs,qkgd->skd",
        probability.astype(jnp.bfloat16),
        d_mixed,
        preferred_element_type=jnp.float32,
    )
    d_value = d_value.astype(jnp.bfloat16).reshape(token_row_count, kv_heads * head_size)
    d_query_rot = (
        jnp.einsum("kgqs,skd->qkgd", d_scores, key_rot, preferred_element_type=jnp.float32)
        * score_scale
    )
    d_query_rot = d_query_rot.reshape(token_row_count, query_heads, head_size)
    d_key_rot = (
        jnp.einsum("kgqs,qkgd->skd", d_scores, query_rotated, preferred_element_type=jnp.float32)
        * score_scale
    )
    query_normed = query_before_norm * query_inv
    key_normed = key_before_norm * key_inv
    d_query_norm = rotate_back(d_query_rot, cosine_table, sine_table)
    d_key_norm = rotate_back(d_key_rot, cosine_table, sine_table)
    query_gain_part = jnp.sum(d_query_norm * query_normed, axis=(0, 1))
    key_gain_part = jnp.sum(d_key_norm * key_normed, axis=(0, 1))
    d_query_pre = norm_back(d_query_norm, query_normed, query_inv, query_norm_gain).astype(
        jnp.bfloat16
    )
    d_query_pre = d_query_pre.reshape(token_row_count, query_heads * head_size)
    d_key_pre = norm_back(d_key_norm, key_normed, key_inv, key_gain).astype(jnp.bfloat16)
    d_key_pre = d_key_pre.reshape(token_row_count, kv_heads * head_size)
    grad_query = outer_sum(first_hidden, d_query_pre)
    grad_key = outer_sum(first_hidden, d_key_pre)
    grad_value = outer_sum(first_hidden, d_value)
    d_hidden_one = (
        project_back(d_query_pre, w_query)
        + project_back(d_key_pre, key_weight)
        + project_back(d_value, value_weight)
    )
    normed_one = x_float * inverse_one
    attn_gain_part = jnp.sum(d_hidden_one * normed_one, axis=0)
    stat_one = jnp.sum(d_hidden_one * attn_full * normed_one, axis=1, keepdims=True)
    d_norm_one, stat_one_sum = (
        lax.psum_scatter(
            d_hidden_one.astype(jnp.bfloat16), "tensor", scatter_dimension=1, tiled=True
        ).astype(jnp.float32),
        lax.psum_scatter(
            jnp.broadcast_to(stat_one, (token_row_count, tensor_size)).astype(jnp.bfloat16),
            "tensor",
            scatter_dimension=1,
            tiled=True,
        ).astype(jnp.float32),
    )
    d_tokens = d_resid + inverse_one * (
        d_norm_one * attn_slice
        - x_piece.astype(jnp.float32) * inverse_one * stat_one_sum / model_width
    )
    return (
        d_tokens,
        (grad_query, grad_key, grad_value, grad_out),
        (attn_gain_part, query_gain_part, key_gain_part),
    )


def on_device(
    tokens,
    segments,
    w_query,
    key_weight,
    value_weight,
    w_out,
    w_gate,
    w_up,
    w_down,
    attn_gain,
    ffn_gain,
    query_norm_gain,
    key_gain,
    cotangent,
):
    shards = (w_query, key_weight, value_weight, w_out, w_gate, w_up, w_down)
    tensor_size = lax.axis_size("tensor")
    tensor_rank = lax.axis_index("tensor")
    slice_width = tokens.shape[1]
    batch_count = segments.shape[0]
    token_row_count = segments.shape[1]
    head_size = query_norm_gain.shape[0]
    attn_full, ffn_full = (
        lax.all_gather(attn_gain, ("dp", "tensor"), axis=0, tiled=True),
        lax.all_gather(ffn_gain, ("dp", "tensor"), axis=0, tiled=True),
    )
    attn_slice = lax.dynamic_slice_in_dim(attn_full, tensor_rank * slice_width, slice_width)
    ffn_slice = lax.dynamic_slice_in_dim(ffn_full, tensor_rank * slice_width, slice_width)
    weight_owned = tuple((jnp.zeros(piece.shape, jnp.float32) for piece in shards))
    gain_totals = (
        jnp.zeros((slice_width * tensor_size,), jnp.float32),
        jnp.zeros((slice_width * tensor_size,), jnp.float32),
        jnp.zeros((head_size,), jnp.float32),
        jnp.zeros((head_size,), jnp.float32),
    )
    out_pieces = []
    grad_pieces = []
    for batch_index in range(batch_count):
        x_piece = tokens[batch_index * token_row_count : (batch_index + 1) * token_row_count]
        dy_piece = cotangent[batch_index * token_row_count : (batch_index + 1) * token_row_count]
        attn_weights = fetch_attention(shards)
        ffn_weights = fetch_feedforward(shards)
        out_piece, saved_state = forward_part(
            x_piece,
            segments[batch_index],
            attn_weights,
            ffn_weights,
            attn_full,
            ffn_full,
            query_norm_gain,
            key_gain,
        )
        d_resid, ffn_grads, ffn_gain_part = feedforward_back(
            dy_piece, saved_state, ffn_weights, ffn_full, ffn_slice
        )
        back_weights = fetch_attention_back(shards)
        d_tokens, attn_grads, head_parts = attention_back(
            d_resid,
            x_piece,
            saved_state,
            back_weights,
            attn_full,
            attn_slice,
            query_norm_gain,
            key_gain,
        )
        batch_sums = (
            lax.psum_scatter(
                attn_grads[0].astype(jnp.bfloat16), "dp", scatter_dimension=0, tiled=True
            ).astype(jnp.float32),
            lax.psum_scatter(
                attn_grads[1].astype(jnp.bfloat16), "dp", scatter_dimension=0, tiled=True
            ).astype(jnp.float32),
            lax.psum_scatter(
                attn_grads[2].astype(jnp.bfloat16), "dp", scatter_dimension=0, tiled=True
            ).astype(jnp.float32),
            lax.psum_scatter(
                attn_grads[3].astype(jnp.bfloat16), "dp", scatter_dimension=0, tiled=True
            ).astype(jnp.float32),
            lax.psum_scatter(
                ffn_grads[0].astype(jnp.bfloat16), "dp", scatter_dimension=0, tiled=True
            ).astype(jnp.float32),
            lax.psum_scatter(
                ffn_grads[1].astype(jnp.bfloat16), "dp", scatter_dimension=0, tiled=True
            ).astype(jnp.float32),
            lax.psum_scatter(
                ffn_grads[2].astype(jnp.bfloat16), "dp", scatter_dimension=0, tiled=True
            ).astype(jnp.float32),
        )
        weight_owned = tuple((total + grad for total, grad in zip(weight_owned, batch_sums)))
        gain_totals = (
            gain_totals[0] + head_parts[0],
            gain_totals[1] + ffn_gain_part,
            gain_totals[2] + head_parts[1],
            gain_totals[3] + head_parts[2],
        )
        out_pieces.append(out_piece)
        grad_pieces.append(d_tokens)
    device_count = lax.axis_size("dp") * tensor_size
    gain_tiles = jnp.tile(jnp.concatenate([gain_totals[2], gain_totals[3]]), device_count)
    attn_gain_grad, ffn_gain_grad, head_gain_grad = (
        lax.psum_scatter(gain_totals[0], ("dp", "tensor"), scatter_dimension=0, tiled=True),
        lax.psum_scatter(gain_totals[1], ("dp", "tensor"), scatter_dimension=0, tiled=True),
        lax.psum_scatter(gain_tiles, ("dp", "tensor"), scatter_dimension=0, tiled=True),
    )
    return (
        jnp.concatenate(out_pieces, axis=0),
        jnp.concatenate(grad_pieces, axis=0),
        weight_owned[0],
        weight_owned[1],
        weight_owned[2],
        weight_owned[3],
        weight_owned[4],
        weight_owned[5],
        weight_owned[6],
        attn_gain_grad,
        ffn_gain_grad,
        head_gain_grad[:head_size],
        head_gain_grad[head_size:],
    )


def solution(mesh):
    placed = (
        P("dp", "tensor"),
        P("dp", None),
        P("dp", "tensor"),
        P("dp", "tensor"),
        P("dp", "tensor"),
        P("dp", "tensor"),
        P("dp", "tensor"),
        P("dp", "tensor"),
        P("dp", "tensor"),
        P(("dp", "tensor")),
        P(("dp", "tensor")),
        P(),
        P(),
        P("dp", "tensor"),
    )
    return jax.shard_map(
        on_device,
        mesh=mesh,
        in_specs=placed,
        out_specs=(
            P("dp", "tensor"),
            P("dp", "tensor"),
            P("dp", "tensor"),
            P("dp", "tensor"),
            P("dp", "tensor"),
            P("dp", "tensor"),
            P("dp", "tensor"),
            P("dp", "tensor"),
            P("dp", "tensor"),
            P(("dp", "tensor")),
            P(("dp", "tensor")),
            P(),
            P(),
        ),
        check_vma=False,
    )
```

profile of v0, /device:TPU:2, one launch (start us, length us, event | category | flops | bytes accessed | tf_op | source)
XLA Modules:
  0.0 5810.7 jit_solution(13198030857712125721)
XLA Ops:
  12.4 37.0 all-gather
  55.5 43.1 all-gather.22.cloned.1.call-done
  103.8 44.6 all-gather.20.cloned.1.call-done
  152.4 121.4 %all-gather.24.cloned.1.call-done = bf16[4096,1024]{1,0:T(8,128)(2,1)} async-done(((bf16[512,1024]{1,0:T(8,128)(2,1)}), bf16[4096,1024]{1,0:T(8,128)(2,1)}) %all-gather.24.cloned.1.call-update) | async-done | bytes 8388624 | tf_op jit(solution)/shard_map/all_gather | solution.py:64
  278.7 5.2 fusion.87
  287.3 111.6 %all-gather.26.cloned.1.call-done = bf16[4096,1024]{1,0:T(8,128)(2,1)} async-done(((bf16[512,1024]{1,0:T(8,128)(2,1)}), bf16[4096,1024]{1,0:T(8,128)(2,1)}) %all-gather.26.cloned.1.call-update) | async-done | bytes 8388624 | tf_op jit(solution)/shard_map/all_gather | solution.py:67
  398.9 7.6 fusion.104
  411.4 8.3 fusion.101
  419.8 15.4 reduce-scatter.27.cloned.1.call-done
  435.2 34.7 reduce-scatter.23.cloned.1.call-done
  476.8 37.9 all-gather.1
  522.5 480.4 %all-gather.30.cloned.1.call-done = bf16[4096,3072]{1,0:T(8,128)(2,1)} async-done(((bf16[512,3072]{1,0:T(8,128)(2,1)}), bf16[4096,3072]{1,0:T(8,128)(2,1)}) %all-gather.30.cloned.1.call-update) | async-done | bytes 25165840 | tf_op jit(solution)/shard_map/all_gather | solution.py:82
  1002.9 10.1 fusion.102
  1013.0 471.7 %all-gather.32.cloned.1.call-done = bf16[4096,3072]{1,0:T(8,128)(2,1)} async-done(((bf16[512,3072]{1,0:T(8,128)(2,1)}), bf16[4096,3072]{1,0:T(8,128)(2,1)}) %all-gather.32.cloned.1.call-update) | async-done | bytes 25165840 | tf_op jit(solution)/shard_map/all_gather | solution.py:83
  1484.8 11.1 fusion.103
  1495.9 6.6 all-gather.40.cloned.1.call-done
  1502.5 483.0 %all-gather.34.cloned.1.call-done = bf16[4096,3072]{1,0:T(8,128)(2,1)} async-done(((bf16[512,3072]{1,0:T(8,128)(2,1)}), bf16[4096,3072]{1,0:T(8,128)(2,1)}) %all-gather.34.cloned.1.call-update) | async-done | bytes 25165840 | tf_op jit(solution)/shard_map/all_gather | solution.py:84
  1985.5 14.4 multiply_convert_fusion.4
  1999.8 14.6 fusion.107
  2014.5 16.5 multiply_reduce_fusion.1
  2031.0 11.5 fusion.106
  2042.5 11.1 fusion.105
  2053.6 14.7 multiply_convert_fusion.2
  2068.3 14.3 convolution_convert_fusion.12
  2082.7 14.3 fusion.109
  2097.0 15.4 multiply_reduce_fusion
  2113.8 6.0 all-reduce.8
  2121.2 21.7 reduce-scatter.35.cloned.1.call-done
  2142.9 34.4 reduce-scatter.31.cloned.1.call-done
  2185.3 11.5 all-gather.46.cloned.1.call-done
  2207.2 8.4 all-gather.42.cloned.1.call-done
  2240.9 6.4 fusion.108
  2258.4 14.2 convolution_convert_fusion.13
  2283.1 6.7 convolution_convert_fusion.4
  2291.0 6.7 convolution_convert_fusion.5
  2298.6 5.7 convolution_convert_fusion.7
  2304.4 5.8 convolution_convert_fusion.6
  2311.7 11.8 convert_bitcast_fusion
  2325.0 11.7 convert_bitcast_fusion.1
  2338.2 11.8 convolution_convert_fusion
  2351.4 12.0 convolution_convert_fusion.1
  2364.5 11.8 convolution_convert_fusion.2
  2377.4 12.0 convolution_convert_fusion.3
  2389.6 7.9 all-reduce.9
  2406.5 28.1 reduce-scatter.33.cloned.1.call-done
  2436.9 25.7 reduce-scatter.37.cloned.1.call-done
  2465.1 70.5 %reduce-scatter.47.cloned.1.call-done = bf16[512,256]{1,0:T(8,128)(2,1)} async-done(((bf16[4096,256]{1,0:T(8,128)(2,1)}), bf16[512,256]{1,0:T(8,128)(2,1)}) %reduce-scatter.47.cloned.1.call-update) | async-done | bytes 262160 | tf_op jit(solution)/shard_map/reduce_scatter | solution.py:434
  2535.7 70.6 %reduce-scatter.49.cloned.1.call-done = bf16[512,256]{1,0:T(8,128)(2,1)} async-done(((bf16[4096,256]{1,0:T(8,128)(2,1)}), bf16[512,256]{1,0:T(8,128)(2,1)}) %reduce-scatter.49.cloned.1.call-update) | async-done | bytes 262160 | tf_op jit(solution)/shard_map/reduce_scatter | solution.py:434
  2608.1 69.0 %reduce-scatter.45.cloned.1.call-done = bf16[512,256]{1,0:T(8,128)(2,1)} async-done(((bf16[4096,256]{1,0:T(8,128)(2,1)}), bf16[512,256]{1,0:T(8,128)(2,1)}) %reduce-scatter.45.cloned.1.call-update) | async-done | bytes 262160 | tf_op jit(solution)/shard_map/reduce_scatter | solution.py:431
  2677.2 71.0 %reduce-scatter.43.cloned.1.call-done = bf16[512,256]{1,0:T(8,128)(2,1)} async-done(((bf16[4096,256]{1,0:T(8,128)(2,1)}), bf16[512,256]{1,0:T(8,128)(2,1)}) %reduce-scatter.43.cloned.1.call-update) | async-done | bytes 262160 | tf_op jit(solution)/shard_map/reduce_scatter | solution.py:431
  2750.1 149.8 %reduce-scatter.53.cloned.1.call-done = bf16[512,1024]{1,0:T(8,128)(2,1)} async-done(((bf16[4096,1024]{1,0:T(8,128)(2,1)}), bf16[512,1024]{1,0:T(8,128)(2,1)}) %reduce-scatter.53.cloned.1.call-update) | async-done | bytes 1048592 | tf_op jit(solution)/shard_map/reduce_scatter | solution.py:437
  2899.9 152.0 %reduce-scatter.51.cloned.1.call-done = bf16[512,1024]{1,0:T(8,128)(2,1)} async-done(((bf16[4096,1024]{1,0:T(8,128)(2,1)}), bf16[512,1024]{1,0:T(8,128)(2,1)}) %reduce-scatter.51.cloned.1.call-update) | async-done | bytes 1048592 | tf_op jit(solution)/shard_map/reduce_scatter | solution.py:437
  3055.1 148.5 %reduce-scatter.39.cloned.1.call-done = bf16[512,1024]{1,0:T(8,128)(2,1)} async-done(((bf16[4096,1024]{1,0:T(8,128)(2,1)}), bf16[512,1024]{1,0:T(8,128)(2,1)}) %reduce-scatter.39.cloned.1.call-update) | async-done | bytes 1048592 | tf_op jit(solution)/shard_map/reduce_scatter | solution.py:428
  3203.6 152.1 %reduce-scatter.41.cloned.1.call-done = bf16[512,1024]{1,0:T(8,128)(2,1)} async-done(((bf16[4096,1024]{1,0:T(8,128)(2,1)}), bf16[512,1024]{1,0:T(8,128)(2,1)}) %reduce-scatter.41.cloned.1.call-update) | async-done | bytes 1048592 | tf_op jit(solution)/shard_map/reduce_scatter | solution.py:428
  3359.0 403.8 %reduce-scatter.65.cloned.1.call-done = bf16[512,3072]{0,1:T(8,128)(2,1)} async-done(((bf16[4096,3072]{0,1:T(8,128)(2,1)}), bf16[512,3072]{0,1:T(8,128)(2,1)}) %reduce-scatter.65.cloned.1.call-update) | async-done | bytes 3145744 | tf_op jit(solution)/shard_map/reduce_scatter | solution.py:446
  3762.8 407.3 %reduce-scatter.63.cloned.1.call-done = bf16[512,3072]{0,1:T(8,128)(2,1)} async-done(((bf16[4096,3072]{0,1:T(8,128)(2,1)}), bf16[512,3072]{0,1:T(8,128)(2,1)}) %reduce-scatter.63.cloned.1.call-update) | async-done | bytes 3145744 | tf_op jit(solution)/shard_map/reduce_scatter | solution.py:446
  4170.1 6.5 convert_add_fusion
  4176.6 7.1 copy.259
  4183.7 393.2 %reduce-scatter.61.cloned.1.call-done = bf16[512,3072]{1,0:T(8,128)(2,1)} async-done(((bf16[4096,3072]{1,0:T(8,128)(2,1)}), bf16[512,3072]{1,0:T(8,128)(2,1)}) %reduce-scatter.61.cloned.1.call-update) | async-done | bytes 3145744 | tf_op jit(solution)/shard_map/reduce_scatter | solution.py:443
  4576.9 406.7 %reduce-scatter.59.cloned.1.call-done = bf16[512,3072]{1,0:T(8,128)(2,1)} async-done(((bf16[4096,3072]{1,0:T(8,128)(2,1)}), bf16[512,3072]{1,0:T(8,128)(2,1)}) %reduce-scatter.59.cloned.1.call-update) | async-done | bytes 3145744 | tf_op jit(solution)/shard_map/reduce_scatter | solution.py:443
  4983.6 6.7 convert_add_fusion.1
  4990.2 400.0 %reduce-scatter.57.cloned.1.call-done = bf16[512,3072]{1,0:T(8,128)(2,1)} async-done(((bf16[4096,3072]{1,0:T(8,128)(2,1)}), bf16[512,3072]{1,0:T(8,128)(2,1)}) %reduce-scatter.57.cloned.1.call-update) | async-done | bytes 3145744 | tf_op jit(solution)/shard_map/reduce_scatter | solution.py:440
  5390.2 406.8 %reduce-scatter.55.cloned.1.call-done = bf16[512,3072]{1,0:T(8,128)(2,1)} async-done(((bf16[4096,3072]{1,0:T(8,128)(2,1)}), bf16[512,3072]{1,0:T(8,128)(2,1)}) %reduce-scatter.55.cloned.1.call-update) | async-done | bytes 3145744 | tf_op jit(solution)/shard_map/reduce_scatter | solution.py:440
  5797.0 6.7 convert_add_fusion.2
  (557 shorter events, 148.4 us)
Async XLA Ops:
  7.2 45.1 all-gather.36.cloned.1.call-start
  9.1 44.8 all-gather.18.cloned.1.call-start
  9.9 88.7 %all-gather.22.cloned.1.call-start = ((), (), s32[]{:S(2)}) async-start(), calls=%async_computation.24 | async-start | bytes 2359296 | tf_op jit(solution)/shard_map/all_gather | solution.py:65
  10.6 137.8 %all-gather.20.cloned.1.call-start = ((), (), s32[]{:S(2)}) async-start(), calls=%async_computation.23 | async-start | bytes 2359296 | tf_op jit(solution)/shard_map/all_gather | solution.py:66
  11.2 262.6 %all-gather.24.cloned.1.call-start = ((), (), s32[]{:S(2)}) async-start(), calls=%async_computation.25 | async-start | bytes 9437184 | tf_op jit(solution)/shard_map/all_gather | solution.py:64
  11.8 387.2 %all-gather.26.cloned.1.call-start = ((), (), s32[]{:S(2)}) async-start(), calls=%async_computation.26 | async-start | bytes 9437184 | tf_op jit(solution)/shard_map/all_gather | solution.py:67
  12.3 422.9 %reduce-scatter.27.cloned.1.call-start = ((), (), s32[]{:S(2)}) async-start(), calls=%async_computation.34 | async-start | bytes 2621440 | tf_op jit(solution)/shard_map/reduce_scatter | solution.py:143
  49.5 357.4 %copy-start.45 = (f32[32,1,128]{2,1,0:T(1,128)}, f32[32,1,128]{2,1,0:T(1,128)S(1)}, u32[]{:S(2)}) copy-start(f32[32,1,128]{2,1,0:T(1,128)S(1)} %all-gather) | copy-start | bytes 49156
  51.6 100.1 %copy-start.70 = (f32[128,128]{0,1:T(8,128)}, f32[128,128]{0,1:T(8,128)S(1)}, u32[]{:S(2)}) copy-start(f32[128,128]{0,1:T(8,128)S(1)} %get-tuple-element.145) | copy-start | bytes 196612
  51.6 100.1 %copy-start.73 = (f32[128,128]{0,1:T(8,128)}, f32[128,128]{0,1:T(8,128)S(1)}, u32[]{:S(2)}) copy-start(f32[128,128]{0,1:T(8,128)S(1)} %get-tuple-element.144) | copy-start | bytes 196612
  55.5 218.3 %copy-start.123 = (f32[128]{0:T(128)}, f32[128]{0:T(128)S(1)}, u32[]{:S(2)}) copy-start(f32[128]{0:T(128)S(1)} %add_rsqrt_fusion.5) | copy-start | bytes 1540
  100.9 50.2 copy-start.65
  152.4 126.3 %copy-start.120 = (f32[128]{0:T(128)S(1)}, f32[128]{0:T(128)}, u32[]{:S(2)}) copy-start(f32[128]{0:T(128)} %copy-done.119) | copy-start | bytes 1540
  285.9 120.7 %copy-start.49 = (bf16[128,2,4,128]{0,3,2,1:T(8,128)(2,1)}, bf16[128,2,4,128]{0,3,2,1:T(8,128)(2,1)S(1)}, u32[]{:S(2)}) copy-start(bf16[128,2,4,128]{0,3,2,1:T(8,128)(2,1)S(1)} %get-tuple-element.160) | copy-start | bytes 786436
  286.3 120.2 %copy-start.125 = (f32[2,4,128]{2,1,0:T(4,128)}, f32[2,4,128]{2,1,0:T(4,128)S(1)}, u32[]{:S(2)}) copy-start(f32[2,4,128]{2,1,0:T(4,128)S(1)} %fusion.45) | copy-start | bytes 12292
  287.3 119.3 %copy-start.78 = (bf16[2,128,4,128]{3,1,2,0:T(8,128)(2,1)}, bf16[2,128,4,128]{3,1,2,0:T(8,128)(2,1)S(1)}, u32[]{:S(2)}) copy-start(bf16[2,128,4,128]{3,1,2,0:T(8,128)(2,1)S(1)} %convolution_convert_fusion.16) | copy-start | bytes 786436
  406.6 63.3 %reduce-scatter.23.cloned.1.call-start = ((), (), s32[]{:S(2)}) async-start(), calls=%async_computation.27 | async-start | bytes 2621440 | tf_op jit(solution)/shard_map/reduce_scatter | solution.py:143
  419.7 50.2 copy-start.37
  419.7 94.9 %all-gather.28.cloned.1.call-start = ((), (), s32[]{:S(2)}) async-start(), calls=%async_computation.28 | async-start | bytes 2621440 | tf_op jit(solution)/shard_map/all_gather | solution.py:147
  472.3 47.4 all-gather.38.cloned.1.call-start
  472.9 530.0 %all-gather.30.cloned.1.call-start = ((), (), s32[]{:S(2)}) async-start(), calls=%async_computation.29 | async-start | bytes 28311552 | tf_op jit(solution)/shard_map/all_gather | solution.py:82
  473.7 1011.1 %all-gather.32.cloned.1.call-start = ((), (), s32[]{:S(2)}) async-start(), calls=%async_computation.30 | async-start | bytes 28311552 | tf_op jit(solution)/shard_map/all_gather | solution.py:83
  474.2 1028.2 %all-gather.40.cloned.1.call-start = ((), (), s32[]{:S(2)}) async-start(), calls=%async_computation.37 | async-start | bytes 1310720 | tf_op jit(solution)/shard_map/all_gather | solution.py:216
  475.5 1509.9 %all-gather.34.cloned.1.call-start = ((), (), s32[]{:S(2)}) async-start(), calls=%async_computation.31 | async-start | bytes 28311552 | tf_op jit(solution)/shard_map/all_gather | solution.py:84
  476.1 1577.5 %all-gather.44.cloned.1.call-start = ((), (), s32[]{:S(2)}) async-start(), calls=%async_computation.41 | async-start | bytes 1310720 | tf_op jit(solution)/shard_map/all_gather | solution.py:216
  476.7 1644.5 %reduce-scatter.29.cloned.1.call-start = ((), (), s32[]{:S(2)}) async-start(), calls=%async_computation.36 | async-start | bytes 1310720 | tf_op jit(solution)/shard_map/reduce_scatter | solution.py:153
  522.5 962.3 %copy-start.4 = (bf16[128,4096]{1,0:T(8,128)(2,1)}, bf16[128,4096]{1,0:T(8,128)(2,1)S(1)}, u32[]{:S(2)}) copy-start(bf16[128,4096]{1,0:T(8,128)(2,1)S(1)} %multiply_convert_fusion.1) | copy-start | bytes 3145732
  2082.7 60.3 %reduce-scatter.35.cloned.1.call-start = ((), (), s32[]{:S(2)}) async-start(), calls=%async_computation.42 | async-start | bytes 2621440 | tf_op jit(solution)/shard_map/reduce_scatter | solution.py:231
  2112.5 64.9 %copy-start.21 = (f32[128,1024]{1,0:T(8,128)S(1)}, f32[128,1024]{1,0:T(8,128)}, u32[]{:S(2)}) copy-start(f32[128,1024]{1,0:T(8,128)} %get-tuple-element.122) | copy-start | bytes 1572868
  2112.5 64.9 %copy-start.24 = (f32[128,1024]{1,0:T(8,128)S(1)}, f32[128,1024]{1,0:T(8,128)}, u32[]{:S(2)}) copy-start(f32[128,1024]{1,0:T(8,128)} %get-tuple-element.123) | copy-start | bytes 1572868
  2112.5 64.9 %copy-start.40 = (bf16[256,1024]{1,0:T(8,128)(2,1)S(1)}, bf16[256,1024]{1,0:T(8,128)(2,1)}, u32[]{:S(2)}) copy-start(bf16[256,1024]{1,0:T(8,128)(2,1)} %param.27) | copy-start | bytes 1572868
  2112.5 64.9 %copy-start.142 = (f32[128]{0:T(128)S(1)}, f32[128]{0:T(128)}, u32[]{:S(2)}) copy-start(f32[128]{0:T(128)} %add_rsqrt_fusion.4) | copy-start | bytes 1540
  2112.5 64.9 %copy-start.145 = (f32[128]{0:T(128)S(1)}, f32[128]{0:T(128)}, u32[]{:S(2)}) copy-start(f32[128]{0:T(128)} %add_rsqrt_fusion.6) | copy-start | bytes 1540
  2112.5 64.8 %reduce-scatter.31.cloned.1.call-start = ((), (), s32[]{:S(2)}) async-start(), calls=%async_computation.38 | async-start | bytes 2621440 | tf_op jit(solution)/shard_map/reduce_scatter | solution.py:231
  2113.1 66.8 %copy-start.75 = (f32[128,128]{0,1:T(8,128)S(1)}, f32[128,128]{0,1:T(8,128)}, u32[]{:S(2)}) copy-start(f32[128,128]{0,1:T(8,128)} %copy-done.73) | copy-start | bytes 196612
  2113.1 83.7 %all-gather.46.cloned.1.call-start = ((), (), s32[]{:S(2)}) async-start(), calls=%async_computation.43 | async-start | bytes 1310720 | tf_op jit(solution)/shard_map/all_gather | solution.py:282
  2113.2 64.2 %copy-start.113 = (f32[1024]{0:T(1024)}, f32[1024]{0:T(1024)S(1)}, u32[]{:S(2)}) copy-start(f32[1024]{0:T(1024)S(1)} %dynamic_slice.6) | copy-start | bytes 12292
  2120.5 59.7 %copy-start.149 = (f32[128]{0:T(128)}, f32[128]{0:T(128)S(1)}, u32[]{:S(2)}) copy-start(f32[128]{0:T(128)S(1)} %fusion.68) | copy-start | bytes 1540
  2121.1 59.0 %copy-start.151 = (f32[128]{0:T(128)}, f32[128]{0:T(128)S(1)}, u32[]{:S(2)}) copy-start(f32[128]{0:T(128)S(1)} %fusion.71) | copy-start | bytes 1540
  2121.2 59.7 %copy-start.72 = (f32[128,128]{0,1:T(8,128)S(1)}, f32[128,128]{0,1:T(8,128)}, u32[]{:S(2)}) copy-start(f32[128,128]{0,1:T(8,128)} %copy-done.70) | copy-start | bytes 196612
  2121.2 60.5 %copy-start.139 = (f32[128]{0:T(128)S(1)}, f32[128]{0:T(128)}, u32[]{:S(2)}) copy-start(f32[128]{0:T(128)} %param.25) | copy-start | bytes 1540
  2121.2 61.0 %copy-start.107 = (f32[128,8]{0,1:T(8,128)S(1)}, f32[128,8]{0,1:T(8,128)}, u32[]{:S(2)}) copy-start(f32[128,8]{0,1:T(8,128)} %copy-done.106) | copy-start | bytes 12292
  2179.9 35.7 all-gather.42.cloned.1.call-start
  2185.0 213.8 %all-reduce.12.cloned.1.call-start = ((), (), s32[]{:S(2)}) async-start(), calls=%async_computation.59 | async-start | bytes 131072
  2258.3 148.2 %reduce-scatter.25.cloned.1.call-start = ((), (), s32[]{:S(2)}) async-start(), calls=%async_computation.32 | async-start | bytes 1310720 | tf_op jit(solution)/shard_map/reduce_scatter | solution.py:153
  2272.6 162.0 %reduce-scatter.33.cloned.1.call-start = ((), (), s32[]{:S(2)}) async-start(), calls=%async_computation.40 | async-start | bytes 1310720 | tf_op jit(solution)/shard_map/reduce_scatter | solution.py:339
  2273.4 189.2 %reduce-scatter.37.cloned.1.call-start = ((), (), s32[]{:S(2)}) async-start(), calls=%async_computation.44 | async-start | bytes 1310720 | tf_op jit(solution)/shard_map/reduce_scatter | solution.py:339
  2274.0 261.7 %reduce-scatter.47.cloned.1.call-start = ((), (), s32[]{:S(2)}) async-start(), calls=%async_computation.49 | async-start | bytes 2359296 | tf_op jit(solution)/shard_map/reduce_scatter | solution.py:434
  2276.2 330.1 %reduce-scatter.49.cloned.1.call-start = ((), (), s32[]{:S(2)}) async-start(), calls=%async_computation.50 | async-start | bytes 2359296 | tf_op jit(solution)/shard_map/reduce_scatter | solution.py:434
  2278.4 398.8 %reduce-scatter.45.cloned.1.call-start = ((), (), s32[]{:S(2)}) async-start(), calls=%async_computation.48 | async-start | bytes 2359296 | tf_op jit(solution)/shard_map/reduce_scatter | solution.py:431
  2280.6 467.6 %reduce-scatter.43.cloned.1.call-start = ((), (), s32[]{:S(2)}) async-start(), calls=%async_computation.47 | async-start | bytes 2359296 | tf_op jit(solution)/shard_map/reduce_scatter | solution.py:431
  2282.8 617.1 %reduce-scatter.53.cloned.1.call-start = ((), (), s32[]{:S(2)}) async-start(), calls=%async_computation.52 | async-start | bytes 9437184 | tf_op jit(solution)/shard_map/reduce_scatter | solution.py:437
  2289.8 762.1 %reduce-scatter.51.cloned.1.call-start = ((), (), s32[]{:S(2)}) async-start(), calls=%async_computation.51 | async-start | bytes 9437184 | tf_op jit(solution)/shard_map/reduce_scatter | solution.py:437
  2297.7 905.9 %reduce-scatter.39.cloned.1.call-start = ((), (), s32[]{:S(2)}) async-start(), calls=%async_computation.45 | async-start | bytes 9437184 | tf_op jit(solution)/shard_map/reduce_scatter | solution.py:428
  2304.4 1051.3 %reduce-scatter.41.cloned.1.call-start = ((), (), s32[]{:S(2)}) async-start(), calls=%async_computation.46 | async-start | bytes 9437184 | tf_op jit(solution)/shard_map/reduce_scatter | solution.py:428
  2310.3 1452.5 %reduce-scatter.65.cloned.1.call-start = ((), (), s32[]{:S(2)}) async-start(), calls=%async_computation.58 | async-start | bytes 28311552 | tf_op jit(solution)/shard_map/reduce_scatter | solution.py:446
  2323.5 1846.6 %reduce-scatter.63.cloned.1.call-start = ((), (), s32[]{:S(2)}) async-start(), calls=%async_computation.57 | async-start | bytes 28311552 | tf_op jit(solution)/shard_map/reduce_scatter | solution.py:446
  2336.7 2240.1 %reduce-scatter.61.cloned.1.call-start = ((), (), s32[]{:S(2)}) async-start(), calls=%async_computation.56 | async-start | bytes 28311552 | tf_op jit(solution)/shard_map/reduce_scatter | solution.py:443
  2350.0 2633.6 %reduce-scatter.59.cloned.1.call-start = ((), (), s32[]{:S(2)}) async-start(), calls=%async_computation.55 | async-start | bytes 28311552 | tf_op jit(solution)/shard_map/reduce_scatter | solution.py:443
  2363.4 3026.8 %reduce-scatter.57.cloned.1.call-start = ((), (), s32[]{:S(2)}) async-start(), calls=%async_computation.54 | async-start | bytes 28311552 | tf_op jit(solution)/shard_map/reduce_scatter | solution.py:440
  2376.3 3420.6 %reduce-scatter.55.cloned.1.call-start = ((), (), s32[]{:S(2)}) async-start(), calls=%async_computation.53 | async-start | bytes 28311552 | tf_op jit(solution)/shard_map/reduce_scatter | solution.py:440
  2389.5 73.1 %copy-start.25 = (f32[128,1024]{1,0:T(8,128)S(1)}, f32[128,1024]{1,0:T(8,128)}, u32[]{:S(2)}) copy-start(f32[128,1024]{1,0:T(8,128)} %get-tuple-element.123) | copy-start | bytes 1572868
  2389.5 73.1 %copy-start.143 = (f32[128]{0:T(128)S(1)}, f32[128]{0:T(128)}, u32[]{:S(2)}) copy-start(f32[128]{0:T(128)} %add_rsqrt_fusion.4) | copy-start | bytes 1540
  2389.5 73.1 %copy-start.152 = (f32[128]{0:T(128)S(1)}, f32[128]{0:T(128)}, u32[]{:S(2)}) copy-start(f32[128]{0:T(128)} %copy-done.151) | copy-start | bytes 1540
  (133 other events, 1035.2 us)
Sparse Core Ops, SparseCore 0:
  10.2 16.8 all-gather.35
  29.2 16.7 all-gather.17
  48.1 50.4 all-gather.21
  100.6 47.7 all-gather.19
  150.3 123.4 all-gather.23
  275.8 123.1 all-gather.25
  406.7 28.4 reduce-scatter.26
  438.5 31.4 reduce-scatter.22
  472.4 22.6 all-gather.27
  497.1 22.5 all-gather.37
  521.3 481.5 all-gather.29
  1004.3 480.3 all-gather.31
  1486.9 15.5 all-gather.39
  1503.8 481.5 all-gather.33
  1987.5 15.5 all-gather.43
  2082.8 23.7 reduce-scatter.28
  2112.7 30.2 reduce-scatter.34
  2145.9 31.4 reduce-scatter.30
  2180.0 16.7 all-gather.45
  2198.8 16.7 all-gather.41
  2258.5 120.3 all-reduce.11
  2381.5 25.0 reduce-scatter.24
  2409.6 24.9 reduce-scatter.32
  2437.7 24.8 reduce-scatter.36
  2466.7 68.8 reduce-scatter.46
  2539.6 66.6 reduce-scatter.48
  2610.2 66.9 reduce-scatter.44
  2681.3 66.8 reduce-scatter.42
  2751.9 147.9 reduce-scatter.52
  2903.8 148.0 reduce-scatter.50
  3055.5 148.0 reduce-scatter.38
  3207.6 148.0 reduce-scatter.40
  3359.4 403.2 reduce-scatter.64
  3766.7 403.3 reduce-scatter.62
  4174.0 402.8 reduce-scatter.60
  4580.6 402.9 reduce-scatter.58
  4987.3 402.8 reduce-scatter.56
  5394.1 402.8 reduce-scatter.54
where the time goes:
time: 5820 us; the launch traced here: 5810 us
  waiting for transfers between devices  5260 us (90%)
  matrix products  334 us (6%)
  blocking collectives  88.8 us (2%)
  other arithmetic  61.9 us (1%)
    reduce_scatter x2, waiting for transfers between devices, on_device(): lax.psum_scatter(ffn_grads[2].astype(jnp.bfloat16), 'dp', scatter_dimensi...  811 us
    reduce_scatter x2, waiting for transfers between devices, on_device(): lax.psum_scatter(ffn_grads[0].astype(jnp.bfloat16), 'dp', scatter_dimensi...  807 us
    reduce_scatter x2, waiting for transfers between devices, on_device(): lax.psum_scatter(ffn_grads[1].astype(jnp.bfloat16), 'dp', scatter_dimensi...  800 us
    all_gather x1, waiting for transfers between devices, fetch_feedforward(): lax.all_gather(shards[6], 'dp', axis=0, tiled=True)  483 us
    all_gather x1, waiting for transfers between devices, fetch_feedforward(): lax.all_gather(shards[4], 'dp', axis=0, tiled=True)  480 us
    all_gather x1, waiting for transfers between devices, fetch_feedforward(): lax.all_gather(shards[5], 'dp', axis=0, tiled=True)  472 us
    reduce_scatter x2, waiting for transfers between devices, on_device(): lax.psum_scatter(attn_grads[3].astype(jnp.bfloat16), 'dp', scatter_dimens...  302 us
    reduce_scatter x2, waiting for transfers between devices, on_device(): lax.psum_scatter(attn_grads[0].astype(jnp.bfloat16), 'dp', scatter_dimens...  301 us
  transfers between devices with their start and end apart: 38, of which 32 were waited for; matrix products, arithmetic and copies ran while one was open for 6% of the time, Pallas kernels for 0%

commit v1 on v0

v1 whole, which is shorter than its diff:
```python
import jax
import jax.numpy as jnp
from jax import lax
from jax.sharding import Mesh
from jax.sharding import PartitionSpec as P

epsilon = 1e-06
rope_base = 1000000.0
masked_score = -1e30
f32 = jnp.float32
bf16 = jnp.bfloat16


def shift(value, axis, step):
    size = lax.axis_size(axis)
    return lax.ppermute(value, axis, [(i, (i + step) % size) for i in range(size)])


def flip(value, axis, mask=1):
    return lax.ppermute(value, axis, [(i, i ^ mask) for i in range(lax.axis_size(axis))])


def transpose_blocks(value):
    size = lax.axis_size("a")
    inner = lax.axis_size("c")
    outer = lax.axis_size("x")
    pairs = []
    for a in range(size):
        for t in range(outer * inner):
            pairs.append((a * size + t, t * size + a))
    return lax.ppermute(value, ("a", "x", "c"), pairs)


def ring_sum(value):
    if lax.axis_size("a") != 4:
        return lax.psum(value, "a")
    value = value + flip(value, "a", 1)
    return value + flip(value, "a", 3)


def ring_scatter(partial):
    rows = partial.shape[0] // 4
    half = rows // 2
    one = partial[rows : 2 * rows]
    two = partial[2 * rows : 3 * rows]
    three = partial[3 * rows :]
    up_first = shift(two[:half], "a", 1)
    down_first = shift(two[half:], "a", -1)
    one = jnp.concatenate([one[:half] + up_first, one[half:]], axis=0)
    three = jnp.concatenate([three[:half], three[half:] + down_first], axis=0)
    return partial[:rows] + shift(one, "a", 1) + shift(three, "a", -1)


def ring_gather(own):
    half = own.shape[0] // 2
    from_before = shift(own, "a", 1)
    from_after = shift(own, "a", -1)
    top = shift(from_before[:half], "a", 1)
    bottom = shift(from_after[half:], "a", -1)
    return jnp.concatenate([own, from_after, top, bottom, from_before], axis=0)


def tensor_scatter(partial):
    size = lax.axis_size("a")
    a = lax.axis_index("a")
    x = lax.axis_index("x")
    c = lax.axis_index("c")
    rows = partial.shape[0] // size

    def block(t):
        return lax.dynamic_slice_in_dim(partial, ((t - a) % size) * rows, rows)

    send = jnp.stack([block(2 * (1 - x) + 1 - c), block(2 * x + 1 - c)])
    got = flip(send, "c")
    far = block(2 * (1 - x) + c) + got[0]
    near = block(2 * x + c) + got[1]
    return near + flip(far, "x")


def tensor_gather(own):
    size = lax.axis_size("a")
    a = lax.axis_index("a")
    t = lax.axis_index("x") * 2 + lax.axis_index("c")
    pair = jnp.stack([own, flip(own, "x")])
    other = flip(pair, "c")
    pieces = jnp.stack([pair[0], other[0], pair[1], other[1]])
    return jnp.concatenate(
        [lax.dynamic_index_in_dim(pieces, ((a + r) % size) ^ t, 0, False) for r in range(size)], axis=0
    )


def own_half_first(value):
    if lax.axis_size("b") != 2:
        return value
    half = value.shape[-1] // 2
    b = lax.axis_index("b")
    axis = value.ndim - 1
    return jnp.concatenate(
        [
            lax.dynamic_slice_in_dim(value, b * half, half, axis),
            lax.dynamic_slice_in_dim(value, (1 - b) * half, half, axis),
        ],
        axis=axis,
    )


def fetch(shard):
    if lax.axis_size("b") == 2:
        return (shard, flip(shard, "b"))
    return (lax.all_gather(shard, "b", axis=0, tiled=True),)


def dot(left, right, left_dim, right_dim):
    return lax.dot_general(
        left, right, (((left_dim,), (right_dim,)), ((), ())), preferred_element_type=f32
    )


def project_in(rows, pieces):
    total = None
    at = 0
    for piece in pieces:
        part = dot(rows[:, at : at + piece.shape[0]], piece, 1, 0)
        total = part if total is None else total + part
        at += piece.shape[0]
    return total


def project_out(rows, pieces):
    return jnp.concatenate([dot(rows, piece, 1, 1) for piece in pieces], axis=1)


def weight_grad(rows, grads):
    if lax.axis_size("b") == 2:
        half = rows.shape[1] // 2
        sent = dot(rows[:, half:], grads, 0, 0).astype(bf16)
        return dot(rows[:, :half], grads, 0, 0) + flip(sent, "b").astype(f32)
    return lax.psum_scatter(
        dot(rows, grads, 0, 0).astype(bf16), "b", scatter_dimension=0, tiled=True
    ).astype(f32)


def rope_tables(segments, head_size):
    rows = segments.shape[1]
    starts = jnp.sum((segments[:, None, :] < segments[:, :, None]).astype(jnp.int32), axis=2)
    position = (jnp.arange(rows, dtype=jnp.int32)[None] - starts).astype(f32)
    half_size = head_size // 2
    frequency = jnp.power(rope_base, -2.0 * jnp.arange(half_size, dtype=f32) / head_size)
    angles = position[:, :, None] * frequency[None, None, :]
    angles = jnp.concatenate([angles, angles], axis=2)
    return (jnp.cos(angles)[:, :, None, :], jnp.sin(angles)[:, :, None, :])


def visible(segments):
    order = jnp.arange(segments.shape[1], dtype=jnp.int32)
    same = segments[:, :, None] == segments[:, None, :]
    return same & (order[:, None] >= order[None, :])[None]


def apply_rotary(value, cosine, sine):
    half = value.shape[-1] // 2
    turned = jnp.concatenate([-value[..., half:], value[..., :half]], axis=-1)
    return value * cosine + turned * sine


def rotate_back(upstream, cosine, sine):
    scaled = upstream * sine
    half = upstream.shape[-1] // 2
    turned = jnp.concatenate([scaled[..., half:], -scaled[..., :half]], axis=-1)
    return upstream * cosine + turned


def norm_back(upstream, normed, inverse, gain):
    scaled = upstream * gain
    return inverse * (scaled - normed * jnp.mean(scaled * normed, axis=-1, keepdims=True))


def attention_forward(qkv, segments, query_gain, key_gain, kv_heads):
    batch, length = segments.shape
    head = query_gain.shape[0]
    kv_width = kv_heads * head
    heads = (qkv.shape[1] - 2 * kv_width) // head
    query_pre = qkv[:, : heads * head].reshape(batch, length, heads, head)
    key_pre = qkv[:, heads * head : heads * head + kv_width].reshape(batch, length, kv_heads, head)
    value = qkv[:, heads * head + kv_width :].astype(bf16).reshape(batch, length, kv_heads, head)
    cosine, sine = rope_tables(segments, head)
    query_inv = lax.rsqrt(jnp.mean(query_pre * query_pre, axis=3, keepdims=True) + epsilon)
    key_inv = lax.rsqrt(jnp.mean(key_pre * key_pre, axis=3, keepdims=True) + epsilon)
    query_rot = apply_rotary(query_pre * query_inv * query_gain, cosine, sine).astype(bf16)
    query_rot = query_rot.reshape(batch, length, kv_heads, heads // kv_heads, head)
    key_rot = apply_rotary(key_pre * key_inv * key_gain, cosine, sine).astype(bf16)
    allowed = visible(segments)[:, None, None]
    scores = jnp.einsum("bqkgd,bskd->bkgqs", query_rot, key_rot, preferred_element_type=f32)
    scores = jnp.where(allowed, scores * head ** (-0.5), masked_score)
    top = jnp.max(scores, axis=4, keepdims=True)
    exps = jnp.exp(scores - top)
    totals = jnp.sum(exps, axis=4, keepdims=True)
    probs = exps / totals
    probs_low = probs.astype(bf16)
    mixed = jnp.einsum("bkgqs,bskd->bqkgd", probs_low, value, preferred_element_type=f32)
    mixed = mixed.astype(bf16).reshape(batch * length, heads * head)
    return mixed, (query_pre, key_pre, value, query_inv, key_inv, query_rot, key_rot, cosine, sine, probs)


def attention_backward(d_mixed, saved, query_gain, key_gain):
    query_pre, key_pre, value, query_inv, key_inv, query_rot, key_rot, cosine, sine, probs = saved
    batch, length, heads, head = query_pre.shape
    scale = head ** (-0.5)
    d_mixed = d_mixed.astype(bf16).reshape(query_rot.shape)
    d_probs = jnp.einsum("bqkgd,bskd->bkgqs", d_mixed, value, preferred_element_type=f32)
    delta = jnp.sum(probs * d_probs, axis=4, keepdims=True)
    d_scores = (probs * (d_probs - delta)).astype(bf16)
    d_value = jnp.einsum("bkgqs,bqkgd->bskd", probs.astype(bf16), d_mixed, preferred_element_type=f32)
    d_query = jnp.einsum("bkgqs,bskd->bqkgd", d_scores, key_rot, preferred_element_type=f32) * scale
    d_query = d_query.reshape(query_pre.shape)
    d_key = jnp.einsum("bkgqs,bqkgd->bskd", d_scores, query_rot, preferred_element_type=f32) * scale
    query_normed = query_pre * query_inv
    key_normed = key_pre * key_inv
    d_query = rotate_back(d_query, cosine, sine)
    d_key = rotate_back(d_key, cosine, sine)
    query_gain_part = jnp.sum(d_query * query_normed, axis=(0, 1, 2))
    key_gain_part = jnp.sum(d_key * key_normed, axis=(0, 1, 2))
    d_query = norm_back(d_query, query_normed, query_inv, query_gain).astype(bf16)
    d_key = norm_back(d_key, key_normed, key_inv, key_gain).astype(bf16)
    rows = batch * length
    d_qkv = jnp.concatenate(
        [d_query.reshape(rows, -1), d_key.reshape(rows, -1), d_value.astype(bf16).reshape(rows, -1)],
        axis=1,
    )
    return d_qkv, query_gain_part, key_gain_part


def on_device(
    tokens,
    segments,
    w_query,
    key_weight,
    value_weight,
    w_out,
    w_gate,
    w_up,
    w_down,
    attn_gain,
    ffn_gain,
    query_gain,
    key_gain,
    cotangent,
):
    size = lax.axis_size("a")
    width = tokens.shape[1] * size
    head = query_gain.shape[0]
    kv_heads = key_weight.shape[1] // head
    query_width = w_query.shape[1]
    kv_width = key_weight.shape[1]

    x_block = own_half_first(transpose_blocks(tokens)).astype(f32)
    attn_gain = own_half_first(lax.all_gather(attn_gain, ("b", "x", "c"), axis=0, tiled=True))
    ffn_gain = own_half_first(lax.all_gather(ffn_gain, ("b", "x", "c"), axis=0, tiled=True))
    wqkv = fetch(jnp.concatenate([w_query, key_weight, value_weight], axis=1))
    inv_one = lax.rsqrt(ring_sum(jnp.sum(x_block * x_block, axis=1, keepdims=True)) / width + epsilon)
    normed_one = x_block * inv_one
    hidden_one = tensor_gather((normed_one * attn_gain).astype(bf16))
    qkv = ring_scatter(project_in(hidden_one, wqkv))
    mixed, saved = attention_forward(qkv, segments, query_gain, key_gain, kv_heads)
    mixed_rows = ring_gather(mixed)
    wo = fetch(w_out)
    resid = x_block + tensor_scatter(project_out(mixed_rows, wo))
    inv_two = lax.rsqrt(ring_sum(jnp.sum(resid * resid, axis=1, keepdims=True)) / width + epsilon)
    normed_two = resid * inv_two
    hidden_two = tensor_gather((normed_two * ffn_gain).astype(bf16))

    dy_block = own_half_first(transpose_blocks(cotangent))
    dy_rows = tensor_gather(dy_block)
    wd = fetch(w_down)
    d_act = ring_scatter(project_in(dy_rows, wd))
    wg = fetch(w_gate)
    wu = fetch(w_up)
    gate = ring_scatter(project_in(hidden_two, wg))
    up = ring_scatter(project_in(hidden_two, wu))
    sig = jax.nn.sigmoid(gate)
    act = (gate * sig * up).astype(bf16)
    d_gate = (d_act * up * sig * (1.0 + gate * (1.0 - sig))).astype(bf16)
    d_up = (d_act * (gate * sig)).astype(bf16)
    d_gate_rows = ring_gather(d_gate)
    d_up_rows = ring_gather(d_up)
    d_hidden_two = tensor_scatter(project_out(d_gate_rows, wg) + project_out(d_up_rows, wu))
    act_rows = ring_gather(act)
    ffn_out = tensor_scatter(project_out(act_rows, wd))
    block_out = transpose_blocks(own_half_first((resid + ffn_out).astype(bf16)))
    ffn_gain_part = jnp.sum(d_hidden_two * normed_two, axis=0)
    e_two = d_hidden_two * ffn_gain
    stat_two = ring_sum(jnp.sum(e_two * normed_two, axis=1, keepdims=True)) / width
    d_resid = dy_block.astype(f32) + inv_two * (e_two - normed_two * stat_two)
    d_resid_rows = tensor_gather(d_resid.astype(bf16))
    d_mixed = ring_scatter(project_in(d_resid_rows, wo))
    d_qkv, query_part, key_part = attention_backward(d_mixed, saved, query_gain, key_gain)
    d_qkv_rows = ring_gather(d_qkv)
    d_hidden_one = tensor_scatter(project_out(d_qkv_rows, wqkv))
    attn_gain_part = jnp.sum(d_hidden_one * normed_one, axis=0)
    e_one = d_hidden_one * attn_gain
    stat_one = ring_sum(jnp.sum(e_one * normed_one, axis=1, keepdims=True)) / width
    d_tokens = d_resid + inv_one * (e_one - normed_one * stat_one)
    d_tokens = transpose_blocks(own_half_first(d_tokens))

    grad_down = weight_grad(dy_rows, act_rows)
    grad_gate = weight_grad(hidden_two, d_gate_rows)
    grad_up = weight_grad(hidden_two, d_up_rows)
    grad_out = weight_grad(d_resid_rows, mixed_rows)
    grad_qkv = weight_grad(hidden_one, d_qkv_rows)

    head_parts = ring_sum(jnp.stack([query_part, key_part]))
    gains = jnp.concatenate(
        [own_half_first(attn_gain_part), own_half_first(ffn_gain_part), head_parts.reshape(-1)]
    ).reshape(-1, head)
    gains = gains + flip(gains, "c")
    gains = gains + flip(gains, "x")
    gains = gains + flip(gains, "b") if lax.axis_size("b") == 2 else lax.psum(gains, "b")
    chunk = attn_gain_part.shape[0]
    lane = (lax.axis_index("b") * lax.axis_size("x") + lax.axis_index("x")) * lax.axis_size(
        "c"
    ) + lax.axis_index("c")
    part = chunk // (lax.axis_size("b") * size)
    flat = gains.reshape(-1)
    return (
        block_out,
        d_tokens,
        grad_qkv[:, :query_width],
        grad_qkv[:, query_width : query_width + kv_width],
        grad_qkv[:, query_width + kv_width :],
        grad_out,
        grad_gate,
        grad_up,
        grad_down,
        lax.dynamic_slice_in_dim(flat, lane * part, part),
        lax.dynamic_slice_in_dim(flat, chunk + lane * part, part),
        flat[2 * chunk : 2 * chunk + head],
        flat[2 * chunk + head :],
    )


def solution(mesh):
    dp = mesh.shape["dp"]
    tensor = mesh.shape["tensor"]
    split = Mesh(mesh.devices.reshape(tensor, dp // tensor, tensor // 2, 2), ("a", "b", "x", "c"))
    matrix = P(("a", "b"), ("x", "c"))
    vector = P(("a", "b", "x", "c"))
    return jax.shard_map(
        on_device,
        mesh=split,
        in_specs=(matrix, P(("a", "b"), None)) + (matrix,) * 7 + (vector, vector, P(), P(), matrix),
        out_specs=(matrix,) * 9 + (vector, vector, P(), P()),
        check_vma=False,
    )
```

time: 5820 us -> 1780 us (0.31)
  waiting for transfers between devices: 5260 us -> 1090 us
  starting transfers between devices: 2.6 us -> 304 us
  matrix products: 334 us -> 160 us
  blocking collectives: 88.8 us -> 17.1 us
    reduce_scatter x22 -> x0, waiting for transfers between devices: 3470 us -> none  [the longest x2 811 us: on_device(): lax.psum_scatter(ffn_grads[2].astype(jnp.bfloat16), 'dp', scatter_dimensi...]
    all_gather x15 -> x0, waiting for transfers between devices: 1780 us -> none  [the longest x1 483 us: fetch_feedforward(): lax.all_gather(shards[6], 'dp', axis=0, tiled=True)]
    ppermute x0 -> x83, waiting for transfers between devices: none -> 1090 us  [the longest x40 557 us: shift(): lax.ppermute(value, axis, [(i, (i + step) % size) for i in range(size)])]
    ppermute x0 -> x83, starting transfers between devices: none -> 304 us  [the longest x40 258 us: shift(): lax.ppermute(value, axis, [(i, (i + step) % size) for i in range(size)])]
    dot_general x54 -> x35, matrix products: 334 us -> 159 us  [the longest x30 149 us: dot(): lax.dot_general(left, right, (((left_dim,), (right_dim,)), ((), ())), pre...]
  transfers between devices with their start and end apart: 38 -> 83, of which waited for: 32 -> 49; matrix products, arithmetic and copies ran while one was open for 6% -> 17% of each run, Pallas kernels for 0% -> 0%
where the time goes in v1:
time: 1780 us; the launch traced here: 1770 us
  waiting for transfers between devices  1090 us (61%)
  starting transfers between devices  304 us (17%)
  matrix products  160 us (9%)
  other arithmetic  99.9 us (6%)
  local copies, waits for them, and re-layouts  92.5 us (5%)
    ppermute x40, waiting for transfers between devices, shift(): lax.ppermute(value, axis, [(i, (i + step) % size) for i in range(size)])  557 us
    ppermute x39, waiting for transfers between devices, flip(): lax.ppermute(value, axis, [(i, i ^ mask) for i in range(lax.axis_size(axi...  388 us
    ppermute x40, starting transfers between devices, shift(): lax.ppermute(value, axis, [(i, (i + step) % size) for i in range(size)])  258 us
    dot_general x30, matrix products, dot(): lax.dot_general(left, right, (((left_dim,), (right_dim,)), ((), ())), pre...  149 us
    ppermute x4, waiting for transfers between devices, transpose_blocks(): return lax.ppermute(value, ('a', 'x', 'c'), pairs)  145 us
    unnamed x274, local copies, waits for them, and re-layouts  37.1 us
  transfers between devices with their start and end apart: 83, of which 49 were waited for; matrix products, arithmetic and copies ran while one was open for 17% of the time, Pallas kernels for 0%

profile of v1, /device:TPU:2, one launch (start us, length us, event | category | flops | bytes accessed | tf_op | source)
XLA Modules:
  0.0 1767.7 jit_solution(18277134322747367863)
XLA Ops:
  6.5 8.8 all-gather.1
  15.3 8.3 all-gather
  23.6 7.7 collective-permute-done
  35.2 5.3 collective-permute-done.2
  41.1 9.0 collective-permute-done.3
  61.2 29.6 %collective-permute-done.5 = bf16[512,1536]{1,0:T(8,128)(2,1)} collective-permute-done((bf16[512,1536]{1,0:T(8,128)(2,1)}, bf16[512,1536]{1,0:T(8,128)(2,1)}, u32[]{:S(2)}, u32[]{:S(2)}) %collective-permute-start.5) | collective-permute-done | bytes 1572896 | tf_op jit(solution)/shard_map/ppermute | solution.py:20
  94.2 21.0 %collective-permute-done.6 = f32[128,1536]{1,0:T(8,128)S(1)} collective-permute-done((f32[128,1536]{1,0:T(8,128)S(1)}, f32[128,1536]{1,0:T(8,128)S(1)}, u32[]{:S(2)}, u32[]{:S(2)}) %collective-permute-start.6) | collective-permute-done | bytes 786464 | tf_op jit(solution)/shard_map/ppermute | solution.py:16
  117.8 18.0 %collective-permute-done.8 = f32[128,1536]{1,0:T(8,128)S(1)} collective-permute-done((f32[128,1536]{1,0:T(8,128)S(1)}, f32[128,1536]{1,0:T(8,128)S(1)}, u32[]{:S(2)}, u32[]{:S(2)}) %collective-permute-start.8) | collective-permute-done | bytes 786464 | tf_op jit(solution)/shard_map/ppermute | solution.py:16
  144.1 80.4 %collective-permute-done.39 = bf16[256,1024]{0,1:T(8,128)(2,1)S(1)} collective-permute-done((bf16[256,1024]{0,1:T(8,128)(2,1)}, bf16[256,1024]{0,1:T(8,128)(2,1)S(1)}, u32[]{:S(2)}, u32[]{:S(2)}) %collective-permute-start.39) | collective-permute-done | bytes 524320 | tf_op jit(solution)/shard_map/ppermute | solution.py:31
  226.9 7.7 collective-permute-done.40
  269.0 9.5 collective-permute-done.11
  280.7 9.0 collective-permute-done.10
  295.3 5.2 collective-permute-done.13
  314.6 43.8 %collective-permute-done.35 = bf16[512,3072]{1,0:T(8,128)(2,1)} collective-permute-done((bf16[512,3072]{1,0:T(8,128)(2,1)}, bf16[512,3072]{1,0:T(8,128)(2,1)}, u32[]{:S(2)}, u32[]{:S(2)}) %collective-permute-start.35) | collective-permute-done | bytes 3145760 | tf_op jit(solution)/shard_map/ppermute | solution.py:20
  358.4 5.7 convolution_add_fusion
  374.6 23.3 %collective-permute-done.16 = f32[256,1024]{0,1:T(8,128)} collective-permute-done((f32[256,1024]{0,1:T(8,128)}, f32[256,1024]{0,1:T(8,128)}, u32[]{:S(2)}, u32[]{:S(2)}) %collective-permute-start.16) | collective-permute-done | bytes 1048608 | tf_op jit(solution)/shard_map/ppermute | solution.py:20
  400.8 6.7 collective-permute-done.42
  413.4 31.9 %collective-permute-done.18 = f32[256,1]{0,1:T(1,128)S(1)} collective-permute-done((f32[256,1]{0,1:T(1,128)S(1)}, f32[256,1]{0,1:T(1,128)S(1)}, u32[]{:S(2)}, u32[]{:S(2)}) %collective-permute-start.18) | collective-permute-done | bytes 1056 | tf_op jit(solution)/shard_map/ppermute | solution.py:20
  449.9 7.1 collective-permute-done.19
  462.3 6.4 fusion.87
  468.7 50.0 %collective-permute-done.21 = bf16[512,3072]{1,0:T(8,128)(2,1)} collective-permute-done((bf16[512,3072]{1,0:T(8,128)(2,1)S(1)}, bf16[512,3072]{1,0:T(8,128)(2,1)}, u32[]{:S(2)}, u32[]{:S(2)}) %collective-permute-start.21) | collective-permute-done | bytes 3145760 | tf_op jit(solution)/shard_map/ppermute | solution.py:20
  518.8 9.3 convolution_add_fusion.2
  531.2 10.7 fusion.85
  542.0 39.3 %collective-permute-done.26 = bf16[512,3072]{1,0:T(8,128)(2,1)} collective-permute-done((bf16[512,3072]{1,0:T(8,128)(2,1)}, bf16[512,3072]{1,0:T(8,128)(2,1)}, u32[]{:S(2)}, u32[]{:S(2)}) %collective-permute-start.26) | collective-permute-done | bytes 3145760 | tf_op jit(solution)/shard_map/ppermute | solution.py:20
  581.3 9.4 convolution_add_fusion.1
  592.6 6.5 slice_add_fusion.8
  608.2 23.4 %collective-permute-done.27 = f32[128,3072]{1,0:T(8,128)} collective-permute-done((f32[128,3072]{1,0:T(8,128)}, f32[128,3072]{1,0:T(8,128)}, u32[]{:S(2)}, u32[]{:S(2)}) %collective-permute-start.27) | collective-permute-done | bytes 1572896 | tf_op jit(solution)/shard_map/ppermute | solution.py:16
  635.8 103.0 %collective-permute-start.29 = (f32[128,3072]{1,0:T(8,128)}, f32[128,3072]{1,0:T(8,128)}, u32[]{:S(2)}, u32[]{:S(2)}) collective-permute-start(f32[128,3072]{1,0:T(8,128)} %get-tuple-element.135), channel_id=1, source_target_pairs={{0,24},{8,0},{16,8},{24,16},{1,25},{9,1},{17,9},{25,17},{2,26},{10... | collective-permute-start | bytes 4718600 | tf_op jit(solution)/shard_map/ppermute | solution.py:16
  744.8 85.3 %collective-permute-done.29 = f32[128,3072]{1,0:T(8,128)} collective-permute-done((f32[128,3072]{1,0:T(8,128)}, f32[128,3072]{1,0:T(8,128)}, u32[]{:S(2)}, u32[]{:S(2)}) %collective-permute-start.29) | collective-permute-done | bytes 1572896 | tf_op jit(solution)/shard_map/ppermute | solution.py:16
  838.1 63.5 %collective-permute-done.25 = f32[256,3072]{1,0:T(8,128)S(1)} collective-permute-done((f32[256,3072]{1,0:T(8,128)S(1)}, f32[256,3072]{1,0:T(8,128)S(1)}, u32[]{:S(2)}, u32[]{:S(2)}) %collective-permute-start.25) | collective-permute-done | bytes 3145760 | tf_op jit(solution)/shard_map/ppermute | solution.py:16
  901.6 6.5 constant_dynamic-update-slice_fusion.22
  908.3 58.2 %collective-permute-start.51 = (bf16[256,3072]{1,0:T(8,128)(2,1)}, bf16[256,3072]{1,0:T(8,128)(2,1)S(1)}, u32[]{:S(2)}, u32[]{:S(2)}) collective-permute-start(bf16[256,3072]{1,0:T(8,128)(2,1)} %get-tuple-element.116), channel_id=1, source_target_pairs={{0,8},{8,16},{16,24},{24,0},{1,9},{9,17},{17,25},{25,1},{2,10},{10... | collective-permute-start | bytes 4718600 | tf_op jit(solution)/shard_map/ppermute | solution.py:16
  968.7 63.7 %collective-permute-done.30 = f32[256,3072]{1,0:T(8,128)} collective-permute-done((f32[256,3072]{1,0:T(8,128)}, f32[256,3072]{1,0:T(8,128)}, u32[]{:S(2)}, u32[]{:S(2)}) %collective-permute-start.30) | collective-permute-done | bytes 3145760 | tf_op jit(solution)/shard_map/ppermute | solution.py:16
  1032.4 8.6 constant_dynamic-update-slice_fusion.17
  1041.0 33.7 %collective-permute-start.46 = (bf16[256,3072]{1,0:T(8,128)(2,1)}, bf16[256,3072]{1,0:T(8,128)(2,1)S(1)}, u32[]{:S(2)}, u32[]{:S(2)}) collective-permute-start(bf16[256,3072]{1,0:T(8,128)(2,1)} %get-tuple-element.119), channel_id=1, source_target_pairs={{0,24},{8,0},{16,8},{24,16},{1,25},{9,1},{17,9},{25,17},{2,26},{10... | collective-permute-start | bytes 4718600 | tf_op jit(solution)/shard_map/ppermute | solution.py:16
  1074.7 28.9 %collective-permute-done.51 = bf16[256,3072]{1,0:T(8,128)(2,1)S(1)} collective-permute-done((bf16[256,3072]{1,0:T(8,128)(2,1)}, bf16[256,3072]{1,0:T(8,128)(2,1)S(1)}, u32[]{:S(2)}, u32[]{:S(2)}) %collective-permute-start.51) | collective-permute-done | bytes 1572896 | tf_op jit(solution)/shard_map/ppermute | solution.py:16
  1108.8 28.4 %collective-permute-done.47 = bf16[256,3072]{1,0:T(8,128)(2,1)S(1)} collective-permute-done((bf16[256,3072]{1,0:T(8,128)(2,1)}, bf16[256,3072]{1,0:T(8,128)(2,1)S(1)}, u32[]{:S(2)}, u32[]{:S(2)}) %collective-permute-start.47) | collective-permute-done | bytes 1572896 | tf_op jit(solution)/shard_map/ppermute | solution.py:16
  1137.3 41.3 %collective-permute-done.46 = bf16[256,3072]{1,0:T(8,128)(2,1)S(1)} collective-permute-done((bf16[256,3072]{1,0:T(8,128)(2,1)}, bf16[256,3072]{1,0:T(8,128)(2,1)S(1)}, u32[]{:S(2)}, u32[]{:S(2)}) %collective-permute-start.46) | collective-permute-done | bytes 1572896 | tf_op jit(solution)/shard_map/ppermute | solution.py:16
  1181.5 6.3 collective-permute-done.52
  1188.7 16.2 collective-permute-done.53
  1207.1 14.4 collective-permute-done.48
  1221.6 6.7 fusion.125
  1238.5 5.4 fusion.126
  1243.9 5.4 fusion.124
  1251.2 10.0 collective-permute-start.31
  1266.4 22.2 %collective-permute-done.55 = f32[256,1024]{0,1:T(8,128)S(1)} collective-permute-done((f32[256,1024]{0,1:T(8,128)}, f32[256,1024]{0,1:T(8,128)S(1)}, u32[]{:S(2)}, u32[]{:S(2)}) %collective-permute-start.55) | collective-permute-done | bytes 1048608 | tf_op jit(solution)/shard_map/ppermute | solution.py:20
  1291.7 38.4 %collective-permute-done.32 = bf16[256,3072]{1,0:T(8,128)(2,1)} collective-permute-done((bf16[256,3072]{1,0:T(8,128)(2,1)}, bf16[256,3072]{1,0:T(8,128)(2,1)}, u32[]{:S(2)}, u32[]{:S(2)}) %collective-permute-start.32) | collective-permute-done | bytes 1572896 | tf_op jit(solution)/shard_map/ppermute | solution.py:16
  1339.5 29.9 %collective-permute-done.57 = f32[256,1]{0,1:T(1,128)S(1)} collective-permute-done((f32[256,1]{0,1:T(1,128)S(1)}, f32[256,1]{0,1:T(1,128)S(1)}, u32[]{:S(2)}, u32[]{:S(2)}) %collective-permute-start.57) | collective-permute-done | bytes 1056 | tf_op jit(solution)/shard_map/ppermute | solution.py:20
  1373.5 8.9 collective-permute-done.58
  1385.2 5.9 fusion.121
  1404.3 9.4 collective-permute-done.60
  1423.2 27.1 %collective-permute-done.62 = f32[128,1024]{1,0:T(8,128)S(1)} collective-permute-done((f32[128,1024]{1,0:T(8,128)S(1)}, f32[128,1024]{1,0:T(8,128)S(1)}, u32[]{:S(2)}, u32[]{:S(2)}) %collective-permute-start.62) | collective-permute-done | bytes 524320 | tf_op jit(solution)/shard_map/ppermute | solution.py:16
  1450.7 5.5 fusion.122
  1459.1 13.5 collective-permute-done.63
  1519.4 8.2 convolution_convert_fusion.2
  1537.7 11.8 collective-permute-start.66
  1549.5 6.8 convert_add_fusion
  1556.3 7.3 collective-permute-done.64
  1579.5 7.2 convert_add_fusion.1
  1594.0 31.2 %collective-permute-done.75 = bf16[512,3072]{1,0:T(8,128)(2,1)} collective-permute-done((bf16[512,3072]{1,0:T(8,128)(2,1)}, bf16[512,3072]{1,0:T(8,128)(2,1)}, u32[]{:S(2)}, u32[]{:S(2)}) %collective-permute-start.75) | collective-permute-done | bytes 3145760 | tf_op jit(solution)/shard_map/ppermute | solution.py:20
  1625.2 6.8 convert_add_fusion.2
  1636.1 11.5 collective-permute-done.74
  1651.5 28.5 %collective-permute-done.73 = bf16[512,1536]{1,0:T(8,128)(2,1)S(1)} collective-permute-done((bf16[512,1536]{1,0:T(8,128)(2,1)}, bf16[512,1536]{1,0:T(8,128)(2,1)S(1)}, u32[]{:S(2)}, u32[]{:S(2)}) %collective-permute-start.73) | collective-permute-done | bytes 1572896 | tf_op jit(solution)/shard_map/ppermute | solution.py:20
  1707.6 57.3 %collective-permute-done.38 = bf16[256,1024]{0,1:T(8,128)(2,1)S(1)} collective-permute-done((bf16[256,1024]{0,1:T(8,128)(2,1)S(1)}, bf16[256,1024]{0,1:T(8,128)(2,1)S(1)}, u32[]{:S(2)}, u32[]{:S(2)}) %collective-permute-start.38) | collective-permute-done | bytes 524320 | tf_op jit(solution)/shard_map/ppermute | solution.py:31
  (596 shorter events, 348.2 us)
Async XLA Ops:
  1.9 29.4 %collective-permute-start = (bf16[256,1024]{0,1:T(8,128)(2,1)S(1)}, bf16[256,1024]{0,1:T(8,128)(2,1)S(1)}, u32[]{:S(2)}, u32[]{:S(2)}) collective-permute-start(bf16[256,1024]{0,1:T(8,128)(2,1)S(1)} %copy.201), channel_id=1, source_target_pairs={{0,0},{1,8},{2,16},{3,24},{8,1},{9,9},{10,17},{11,25},{16,2},{17,1... | collective-permute-start | bytes 1572872 | tf_op jit(solution)/shard_map/ppermute | solution.py:31
  53.7 37.1 %collective-permute-start.5 = (bf16[512,1536]{1,0:T(8,128)(2,1)}, bf16[512,1536]{1,0:T(8,128)(2,1)}, u32[]{:S(2)}, u32[]{:S(2)}) collective-permute-start(bf16[512,1536]{1,0:T(8,128)(2,1)} %constant_dynamic-update-slice_fusion), channel_id=1, source_target_pairs={{0,4},{4,0},{1,5},{5,1},{2,6},{6,2},{3,7},{7,3},{8,12},{12,8},{9,1... | collective-permute-start | bytes 4718600 | tf_op jit(solution)/shard_map/ppermute | solution.py:20
  94.2 21.0 %collective-permute-start.6 = (f32[128,1536]{1,0:T(8,128)S(1)}, f32[128,1536]{1,0:T(8,128)S(1)}, u32[]{:S(2)}, u32[]{:S(2)}) collective-permute-start(f32[128,1536]{1,0:T(8,128)S(1)} %slice.412), channel_id=1, source_target_pairs={{0,8},{8,16},{16,24},{24,0},{1,9},{9,17},{17,25},{25,1},{2,10},{10... | collective-permute-start | bytes 2359304 | tf_op jit(solution)/shard_map/ppermute | solution.py:16
  115.5 20.3 %collective-permute-start.8 = (f32[128,1536]{1,0:T(8,128)S(1)}, f32[128,1536]{1,0:T(8,128)S(1)}, u32[]{:S(2)}, u32[]{:S(2)}) collective-permute-start(f32[128,1536]{1,0:T(8,128)S(1)} %get-tuple-element.139), channel_id=1, source_target_pairs={{0,24},{8,0},{16,8},{24,16},{1,25},{9,1},{17,9},{25,17},{2,26},{10... | collective-permute-start | bytes 2359304 | tf_op jit(solution)/shard_map/ppermute | solution.py:16
  117.3 118.4 %collective-permute-start.7 = (f32[256,1536]{1,0:T(8,128)S(1)}, f32[256,1536]{1,0:T(8,128)}, u32[]{:S(2)}, u32[]{:S(2)}) collective-permute-start(f32[256,1536]{1,0:T(8,128)S(1)} %pad_maximum_fusion.18), channel_id=1, source_target_pairs={{0,8},{8,16},{16,24},{24,0},{1,9},{9,17},{17,25},{25,1},{2,10},{10... | collective-permute-start | bytes 4718600 | tf_op jit(solution)/shard_map/ppermute | solution.py:16
  137.1 98.7 %collective-permute-start.9 = (f32[256,1536]{1,0:T(8,128)}, f32[256,1536]{1,0:T(8,128)}, u32[]{:S(2)}, u32[]{:S(2)}) collective-permute-start(f32[256,1536]{1,0:T(8,128)} %pad_maximum_fusion.19), channel_id=1, source_target_pairs={{0,24},{8,0},{16,8},{24,16},{1,25},{9,1},{17,9},{25,17},{2,26},{10... | collective-permute-start | bytes 4718600 | tf_op jit(solution)/shard_map/ppermute | solution.py:16
  141.8 82.7 %collective-permute-start.39 = (bf16[256,1024]{0,1:T(8,128)(2,1)}, bf16[256,1024]{0,1:T(8,128)(2,1)S(1)}, u32[]{:S(2)}, u32[]{:S(2)}) collective-permute-start(bf16[256,1024]{0,1:T(8,128)(2,1)} %copy.212), channel_id=1, source_target_pairs={{0,0},{1,8},{2,16},{3,24},{8,1},{9,9},{10,17},{11,25},{16,2},{17,1... | collective-permute-start | bytes 1572872 | tf_op jit(solution)/shard_map/ppermute | solution.py:31
  235.8 32.0 %collective-permute-start.41 = (bf16[2,256,1024]{1,2,0:T(8,128)(2,1)}, bf16[2,256,1024]{1,2,0:T(8,128)(2,1)}, u32[]{:S(2)}, u32[]{:S(2)}) collective-permute-start(bf16[2,256,1024]{1,2,0:T(8,128)(2,1)} %pad_maximum_fusion.22), channel_id=1, source_target_pairs={{0,1},{1,0},{2,3},{3,2},{4,5},{5,4},{6,7},{7,6},{8,9},{9,8},{10,11... | collective-permute-start | bytes 3145736 | tf_op jit(solution)/shard_map/ppermute | solution.py:20
  261.8 16.7 collective-permute-start.11
  264.6 25.1 %collective-permute-start.10 = (bf16[256,1024]{1,0:T(8,128)(2,1)S(1)}, bf16[256,1024]{1,0:T(8,128)(2,1)}, u32[]{:S(2)}, u32[]{:S(2)}) collective-permute-start(bf16[256,1024]{1,0:T(8,128)(2,1)S(1)} %reshape.277), channel_id=1, source_target_pairs={{0,24},{8,0},{16,8},{24,16},{1,25},{9,1},{17,9},{25,17},{2,26},{10... | collective-permute-start | bytes 1572872 | tf_op jit(solution)/shard_map/ppermute | solution.py:16
  265.7 37.2 %collective-permute-start.14 = (bf16[512,1024]{1,0:T(8,128)(2,1)}, bf16[512,1024]{1,0:T(8,128)(2,1)}, u32[]{:S(2)}, u32[]{:S(2)}) collective-permute-start(bf16[512,1024]{1,0:T(8,128)(2,1)} %param.19), channel_id=1, source_target_pairs={{0,4},{4,0},{1,5},{5,1},{2,6},{6,2},{3,7},{7,3},{8,12},{12,8},{9,1... | collective-permute-start | bytes 3145736 | tf_op jit(solution)/shard_map/ppermute | solution.py:20
  267.2 91.2 %collective-permute-start.35 = (bf16[512,3072]{1,0:T(8,128)(2,1)}, bf16[512,3072]{1,0:T(8,128)(2,1)}, u32[]{:S(2)}, u32[]{:S(2)}) collective-permute-start(bf16[512,3072]{1,0:T(8,128)(2,1)} %param.22), channel_id=1, source_target_pairs={{0,4},{4,0},{1,5},{5,1},{2,6},{6,2},{3,7},{7,3},{8,12},{12,8},{9,1... | collective-permute-start | bytes 9437192 | tf_op jit(solution)/shard_map/ppermute | solution.py:20
  309.0 61.9 %collective-permute-start.15 = (f32[2,256,1024]{1,2,0:T(8,128)}, f32[2,256,1024]{1,2,0:T(8,128)}, u32[]{:S(2)}, u32[]{:S(2)}) collective-permute-start(f32[2,256,1024]{1,2,0:T(8,128)} %pad_maximum_fusion.8), channel_id=1, source_target_pairs={{0,1},{1,0},{2,3},{3,2},{4,5},{5,4},{6,7},{7,6},{8,9},{9,8},{10,11... | collective-permute-start | bytes 6291464 | tf_op jit(solution)/shard_map/ppermute | solution.py:20
  370.0 37.5 %collective-permute-start.42 = (f32[128,3072]{1,0:T(8,128)}, f32[128,3072]{1,0:T(8,128)}, u32[]{:S(2)}, u32[]{:S(2)}) collective-permute-start(f32[128,3072]{1,0:T(8,128)} %slice.456), channel_id=1, source_target_pairs={{0,8},{8,16},{16,24},{24,0},{1,9},{9,17},{17,25},{25,1},{2,10},{10... | collective-permute-start | bytes 4718600 | tf_op jit(solution)/shard_map/ppermute | solution.py:16
  373.4 24.4 %collective-permute-start.16 = (f32[256,1024]{0,1:T(8,128)}, f32[256,1024]{0,1:T(8,128)}, u32[]{:S(2)}, u32[]{:S(2)}) collective-permute-start(f32[256,1024]{0,1:T(8,128)} %fusion.45), channel_id=1, source_target_pairs={{0,2},{2,0},{1,3},{3,1},{4,6},{6,4},{5,7},{7,5},{8,10},{10,8},{9,1... | collective-permute-start | bytes 3145736 | tf_op jit(solution)/shard_map/ppermute | solution.py:20
  412.6 47.5 %collective-permute-start.44 = (f32[128,3072]{1,0:T(8,128)S(1)}, f32[128,3072]{1,0:T(8,128)S(1)}, u32[]{:S(2)}, u32[]{:S(2)}) collective-permute-start(f32[128,3072]{1,0:T(8,128)S(1)} %get-tuple-element.131), channel_id=1, source_target_pairs={{0,24},{8,0},{16,8},{24,16},{1,25},{9,1},{17,9},{25,17},{2,26},{10... | collective-permute-start | bytes 4718600 | tf_op jit(solution)/shard_map/ppermute | solution.py:16
  413.1 32.2 %collective-permute-start.18 = (f32[256,1]{0,1:T(1,128)S(1)}, f32[256,1]{0,1:T(1,128)S(1)}, u32[]{:S(2)}, u32[]{:S(2)}) collective-permute-start(f32[256,1]{0,1:T(1,128)S(1)} %add.458), channel_id=1, source_target_pairs={{0,24},{8,16},{16,8},{24,0},{1,25},{9,17},{17,9},{25,1},{2,26},{10... | collective-permute-start | bytes 3080 | tf_op jit(solution)/shard_map/ppermute | solution.py:20
  447.6 71.1 %collective-permute-start.21 = (bf16[512,3072]{1,0:T(8,128)(2,1)S(1)}, bf16[512,3072]{1,0:T(8,128)(2,1)}, u32[]{:S(2)}, u32[]{:S(2)}) collective-permute-start(bf16[512,3072]{1,0:T(8,128)(2,1)S(1)} %copy-done.103), channel_id=1, source_target_pairs={{0,4},{4,0},{1,5},{5,1},{2,6},{6,2},{3,7},{7,3},{8,12},{12,8},{9,1... | collective-permute-start | bytes 9437192 | tf_op jit(solution)/shard_map/ppermute | solution.py:20
  449.2 132.1 %collective-permute-start.26 = (bf16[512,3072]{1,0:T(8,128)(2,1)}, bf16[512,3072]{1,0:T(8,128)(2,1)}, u32[]{:S(2)}, u32[]{:S(2)}) collective-permute-start(bf16[512,3072]{1,0:T(8,128)(2,1)} %param.21), channel_id=1, source_target_pairs={{0,4},{4,0},{1,5},{5,1},{2,6},{6,2},{3,7},{7,3},{8,12},{12,8},{9,1... | collective-permute-start | bytes 9437192 | tf_op jit(solution)/shard_map/ppermute | solution.py:20
  459.0 374.6 %collective-permute-start.43 = (f32[256,3072]{1,0:T(8,128)}, f32[256,3072]{1,0:T(8,128)}, u32[]{:S(2)}, u32[]{:S(2)}) collective-permute-start(f32[256,3072]{1,0:T(8,128)} %pad_maximum_fusion.4), channel_id=1, source_target_pairs={{0,8},{8,16},{16,24},{24,0},{1,9},{9,17},{17,25},{25,1},{2,10},{10... | collective-permute-start | bytes 9437192 | tf_op jit(solution)/shard_map/ppermute | solution.py:16
  529.4 63.2 %collective-permute-start.22 = (f32[128,3072]{1,0:T(8,128)}, f32[128,3072]{1,0:T(8,128)}, u32[]{:S(2)}, u32[]{:S(2)}) collective-permute-start(f32[128,3072]{1,0:T(8,128)} %slice.434), channel_id=1, source_target_pairs={{0,8},{8,16},{16,24},{24,0},{1,9},{9,17},{17,25},{25,1},{2,10},{10... | collective-permute-start | bytes 4718600 | tf_op jit(solution)/shard_map/ppermute | solution.py:16
  592.0 39.5 %collective-permute-start.27 = (f32[128,3072]{1,0:T(8,128)}, f32[128,3072]{1,0:T(8,128)}, u32[]{:S(2)}, u32[]{:S(2)}) collective-permute-start(f32[128,3072]{1,0:T(8,128)} %slice.441), channel_id=1, source_target_pairs={{0,8},{8,16},{16,24},{24,0},{1,9},{9,17},{17,25},{25,1},{2,10},{10... | collective-permute-start | bytes 4718600 | tf_op jit(solution)/shard_map/ppermute | solution.py:16
  599.2 139.6 %collective-permute-start.24 = (f32[128,3072]{1,0:T(8,128)}, f32[128,3072]{1,0:T(8,128)}, u32[]{:S(2)}, u32[]{:S(2)}) collective-permute-start(f32[128,3072]{1,0:T(8,128)} %get-tuple-element.127), channel_id=1, source_target_pairs={{0,24},{8,0},{16,8},{24,16},{1,25},{9,1},{17,9},{25,17},{2,26},{10... | collective-permute-start | bytes 4718600 | tf_op jit(solution)/shard_map/ppermute | solution.py:16
  604.1 234.0 %collective-permute-start.45 = (f32[256,3072]{1,0:T(8,128)}, f32[256,3072]{1,0:T(8,128)S(1)}, u32[]{:S(2)}, u32[]{:S(2)}) collective-permute-start(f32[256,3072]{1,0:T(8,128)} %pad_maximum_fusion.5), channel_id=1, source_target_pairs={{0,24},{8,0},{16,8},{24,16},{1,25},{9,1},{17,9},{25,17},{2,26},{10... | collective-permute-start | bytes 9437192 | tf_op jit(solution)/shard_map/ppermute | solution.py:16
  607.9 230.2 %collective-permute-start.23 = (f32[256,3072]{1,0:T(8,128)}, f32[256,3072]{1,0:T(8,128)}, u32[]{:S(2)}, u32[]{:S(2)}) collective-permute-start(f32[256,3072]{1,0:T(8,128)} %pad_maximum_fusion), channel_id=1, source_target_pairs={{0,8},{8,16},{16,24},{24,0},{1,9},{9,17},{17,25},{25,1},{2,10},{10... | collective-permute-start | bytes 9437192 | tf_op jit(solution)/shard_map/ppermute | solution.py:16
  635.8 194.3 %collective-permute-start.29 = (f32[128,3072]{1,0:T(8,128)}, f32[128,3072]{1,0:T(8,128)}, u32[]{:S(2)}, u32[]{:S(2)}) collective-permute-start(f32[128,3072]{1,0:T(8,128)} %get-tuple-element.135), channel_id=1, source_target_pairs={{0,24},{8,0},{16,8},{24,16},{1,25},{9,1},{17,9},{25,17},{2,26},{10... | collective-permute-start | bytes 4718600 | tf_op jit(solution)/shard_map/ppermute | solution.py:16
  741.2 160.4 %collective-permute-start.25 = (f32[256,3072]{1,0:T(8,128)S(1)}, f32[256,3072]{1,0:T(8,128)S(1)}, u32[]{:S(2)}, u32[]{:S(2)}) collective-permute-start(f32[256,3072]{1,0:T(8,128)S(1)} %pad_maximum_fusion.1), channel_id=1, source_target_pairs={{0,24},{8,0},{16,8},{24,16},{1,25},{9,1},{17,9},{25,17},{2,26},{10... | collective-permute-start | bytes 9437192 | tf_op jit(solution)/shard_map/ppermute | solution.py:16
  830.1 138.6 %collective-permute-start.28 = (f32[256,3072]{1,0:T(8,128)}, f32[256,3072]{1,0:T(8,128)}, u32[]{:S(2)}, u32[]{:S(2)}) collective-permute-start(f32[256,3072]{1,0:T(8,128)} %pad_maximum_fusion.2), channel_id=1, source_target_pairs={{0,8},{8,16},{16,24},{24,0},{1,9},{9,17},{17,25},{25,1},{2,10},{10... | collective-permute-start | bytes 9437192 | tf_op jit(solution)/shard_map/ppermute | solution.py:16
  833.7 198.8 %collective-permute-start.30 = (f32[256,3072]{1,0:T(8,128)}, f32[256,3072]{1,0:T(8,128)}, u32[]{:S(2)}, u32[]{:S(2)}) collective-permute-start(f32[256,3072]{1,0:T(8,128)} %pad_maximum_fusion.3), channel_id=1, source_target_pairs={{0,24},{8,0},{16,8},{24,16},{1,25},{9,1},{17,9},{25,17},{2,26},{10... | collective-permute-start | bytes 9437192 | tf_op jit(solution)/shard_map/ppermute | solution.py:16
  908.1 195.6 %collective-permute-start.50 = (bf16[256,3072]{1,0:T(8,128)(2,1)}, bf16[256,3072]{1,0:T(8,128)(2,1)}, u32[]{:S(2)}, u32[]{:S(2)}) collective-permute-start(bf16[256,3072]{1,0:T(8,128)(2,1)} %get-tuple-element.116), channel_id=1, source_target_pairs={{0,24},{8,0},{16,8},{24,16},{1,25},{9,1},{17,9},{25,17},{2,26},{10... | collective-permute-start | bytes 4718600 | tf_op jit(solution)/shard_map/ppermute | solution.py:16
  908.3 195.3 %collective-permute-start.51 = (bf16[256,3072]{1,0:T(8,128)(2,1)}, bf16[256,3072]{1,0:T(8,128)(2,1)S(1)}, u32[]{:S(2)}, u32[]{:S(2)}) collective-permute-start(bf16[256,3072]{1,0:T(8,128)(2,1)} %get-tuple-element.116), channel_id=1, source_target_pairs={{0,8},{8,16},{16,24},{24,0},{1,9},{9,17},{17,25},{25,1},{2,10},{10... | collective-permute-start | bytes 4718600 | tf_op jit(solution)/shard_map/ppermute | solution.py:16
  1041.0 96.2 %collective-permute-start.47 = (bf16[256,3072]{1,0:T(8,128)(2,1)}, bf16[256,3072]{1,0:T(8,128)(2,1)S(1)}, u32[]{:S(2)}, u32[]{:S(2)}) collective-permute-start(bf16[256,3072]{1,0:T(8,128)(2,1)} %get-tuple-element.119), channel_id=1, source_target_pairs={{0,8},{8,16},{16,24},{24,0},{1,9},{9,17},{17,25},{25,1},{2,10},{10... | collective-permute-start | bytes 4718600 | tf_op jit(solution)/shard_map/ppermute | solution.py:16
  1041.0 137.6 %collective-permute-start.46 = (bf16[256,3072]{1,0:T(8,128)(2,1)}, bf16[256,3072]{1,0:T(8,128)(2,1)S(1)}, u32[]{:S(2)}, u32[]{:S(2)}) collective-permute-start(bf16[256,3072]{1,0:T(8,128)(2,1)} %get-tuple-element.119), channel_id=1, source_target_pairs={{0,24},{8,0},{16,8},{24,16},{1,25},{9,1},{17,9},{25,17},{2,26},{10... | collective-permute-start | bytes 4718600 | tf_op jit(solution)/shard_map/ppermute | solution.py:16
  1103.6 84.1 %collective-permute-start.52 = (bf16[128,3072]{1,0:T(8,128)(2,1)S(1)}, bf16[128,3072]{1,0:T(8,128)(2,1)S(1)}, u32[]{:S(2)}, u32[]{:S(2)}) collective-permute-start(bf16[128,3072]{1,0:T(8,128)(2,1)S(1)} %slice.463), channel_id=1, source_target_pairs={{0,8},{8,16},{16,24},{24,0},{1,9},{9,17},{17,25},{25,1},{2,10},{10... | collective-permute-start | bytes 2359304 | tf_op jit(solution)/shard_map/ppermute | solution.py:16
  1104.9 100.0 %collective-permute-start.53 = (bf16[128,3072]{1,0:T(8,128)(2,1)S(1)}, bf16[128,3072]{1,0:T(8,128)(2,1)S(1)}, u32[]{:S(2)}, u32[]{:S(2)}) collective-permute-start(bf16[128,3072]{1,0:T(8,128)(2,1)S(1)} %slice.464), channel_id=1, source_target_pairs={{0,24},{8,0},{16,8},{24,16},{1,25},{9,1},{17,9},{25,17},{2,26},{10... | collective-permute-start | bytes 2359304 | tf_op jit(solution)/shard_map/ppermute | solution.py:16
  1137.2 84.3 %collective-permute-start.48 = (bf16[128,3072]{1,0:T(8,128)(2,1)S(1)}, bf16[128,3072]{1,0:T(8,128)(2,1)S(1)}, u32[]{:S(2)}, u32[]{:S(2)}) collective-permute-start(bf16[128,3072]{1,0:T(8,128)(2,1)S(1)} %slice.461), channel_id=1, source_target_pairs={{0,8},{8,16},{16,24},{24,0},{1,9},{9,17},{17,25},{25,1},{2,10},{10... | collective-permute-start | bytes 2359304 | tf_op jit(solution)/shard_map/ppermute | solution.py:16
  1178.7 54.7 %collective-permute-start.49 = (bf16[128,3072]{1,0:T(8,128)(2,1)S(1)}, bf16[128,3072]{1,0:T(8,128)(2,1)S(1)}, u32[]{:S(2)}, u32[]{:S(2)}) collective-permute-start(bf16[128,3072]{1,0:T(8,128)(2,1)S(1)} %slice.462), channel_id=1, source_target_pairs={{0,24},{8,0},{16,8},{24,16},{1,25},{9,1},{17,9},{25,17},{2,26},{10... | collective-permute-start | bytes 2359304 | tf_op jit(solution)/shard_map/ppermute | solution.py:16
  1251.2 82.0 %collective-permute-start.31 = (bf16[256,3072]{1,0:T(8,128)(2,1)}, bf16[256,3072]{1,0:T(8,128)(2,1)}, u32[]{:S(2)}, u32[]{:S(2)}) collective-permute-start(bf16[256,3072]{1,0:T(8,128)(2,1)} %get-tuple-element.125), channel_id=1, source_target_pairs={{0,24},{8,0},{16,8},{24,16},{1,25},{9,1},{17,9},{25,17},{2,26},{10... | collective-permute-start | bytes 4718600 | tf_op jit(solution)/shard_map/ppermute | solution.py:16
  1261.1 69.0 %collective-permute-start.32 = (bf16[256,3072]{1,0:T(8,128)(2,1)}, bf16[256,3072]{1,0:T(8,128)(2,1)}, u32[]{:S(2)}, u32[]{:S(2)}) collective-permute-start(bf16[256,3072]{1,0:T(8,128)(2,1)} %get-tuple-element.125), channel_id=1, source_target_pairs={{0,8},{8,16},{16,24},{24,0},{1,9},{9,17},{17,25},{25,1},{2,10},{10... | collective-permute-start | bytes 4718600 | tf_op jit(solution)/shard_map/ppermute | solution.py:16
  1263.2 25.5 %collective-permute-start.55 = (f32[256,1024]{0,1:T(8,128)}, f32[256,1024]{0,1:T(8,128)S(1)}, u32[]{:S(2)}, u32[]{:S(2)}) collective-permute-start(f32[256,1024]{0,1:T(8,128)} %fusion.59), channel_id=1, source_target_pairs={{0,2},{2,0},{1,3},{3,1},{4,6},{6,4},{5,7},{7,5},{8,10},{10,8},{9,1... | collective-permute-start | bytes 3145736 | tf_op jit(solution)/shard_map/ppermute | solution.py:20
  1290.7 45.8 %collective-permute-start.56 = (f32[256,1]{0,1:T(1,128)S(1)}, f32[256,1]{0,1:T(1,128)S(1)}, u32[]{:S(2)}, u32[]{:S(2)}) collective-permute-start(f32[256,1]{0,1:T(1,128)S(1)} %bitcast.343), channel_id=1, source_target_pairs={{0,8},{8,0},{16,24},{24,16},{1,9},{9,1},{17,25},{25,17},{2,10},{10... | collective-permute-start | bytes 3080 | tf_op jit(solution)/shard_map/ppermute | solution.py:20
  1331.4 40.2 %collective-permute-start.33 = (bf16[128,3072]{1,0:T(8,128)(2,1)S(1)}, bf16[128,3072]{1,0:T(8,128)(2,1)S(1)}, u32[]{:S(2)}, u32[]{:S(2)}) collective-permute-start(bf16[128,3072]{1,0:T(8,128)(2,1)S(1)} %slice.446), channel_id=1, source_target_pairs={{0,8},{8,16},{16,24},{24,0},{1,9},{9,17},{17,25},{25,1},{2,10},{10... | collective-permute-start | bytes 2359304 | tf_op jit(solution)/shard_map/ppermute | solution.py:16
  1334.4 38.1 %collective-permute-start.34 = (bf16[128,3072]{1,0:T(8,128)(2,1)S(1)}, bf16[128,3072]{1,0:T(8,128)(2,1)S(1)}, u32[]{:S(2)}, u32[]{:S(2)}) collective-permute-start(bf16[128,3072]{1,0:T(8,128)(2,1)S(1)} %slice.447), channel_id=1, source_target_pairs={{0,24},{8,0},{16,8},{24,16},{1,25},{9,1},{17,9},{25,17},{2,26},{10... | collective-permute-start | bytes 2359304 | tf_op jit(solution)/shard_map/ppermute | solution.py:16
  1336.5 32.9 %collective-permute-start.57 = (f32[256,1]{0,1:T(1,128)S(1)}, f32[256,1]{0,1:T(1,128)S(1)}, u32[]{:S(2)}, u32[]{:S(2)}) collective-permute-start(f32[256,1]{0,1:T(1,128)S(1)} %add.486), channel_id=1, source_target_pairs={{0,24},{8,16},{16,8},{24,0},{1,25},{9,17},{17,9},{25,1},{2,26},{10... | collective-permute-start | bytes 3080 | tf_op jit(solution)/shard_map/ppermute | solution.py:20
  1397.6 16.2 collective-permute-start.60
  1414.1 36.3 %collective-permute-start.62 = (f32[128,1024]{1,0:T(8,128)S(1)}, f32[128,1024]{1,0:T(8,128)S(1)}, u32[]{:S(2)}, u32[]{:S(2)}) collective-permute-start(f32[128,1024]{1,0:T(8,128)S(1)} %get-tuple-element.145), channel_id=1, source_target_pairs={{0,24},{8,0},{16,8},{24,16},{1,25},{9,1},{17,9},{25,17},{2,26},{10... | collective-permute-start | bytes 1572872 | tf_op jit(solution)/shard_map/ppermute | solution.py:16
  1419.0 118.7 %collective-permute-start.77 = (bf16[512,3072]{1,0:T(8,128)(2,1)}, bf16[512,3072]{1,0:T(8,128)(2,1)}, u32[]{:S(2)}, u32[]{:S(2)}) collective-permute-start(bf16[512,3072]{1,0:T(8,128)(2,1)} %convolution_convert_fusion), channel_id=1, source_target_pairs={{0,4},{4,0},{1,5},{5,1},{2,6},{6,2},{3,7},{7,3},{8,12},{12,8},{9,1... | collective-permute-start | bytes 9437192 | tf_op jit(solution)/shard_map/ppermute | solution.py:20
  1420.6 158.9 %collective-permute-start.76 = (bf16[512,3072]{1,0:T(8,128)(2,1)}, bf16[512,3072]{1,0:T(8,128)(2,1)}, u32[]{:S(2)}, u32[]{:S(2)}) collective-permute-start(bf16[512,3072]{1,0:T(8,128)(2,1)} %convolution_convert_fusion.1), channel_id=1, source_target_pairs={{0,4},{4,0},{1,5},{5,1},{2,6},{6,2},{3,7},{7,3},{8,12},{12,8},{9,1... | collective-permute-start | bytes 9437192 | tf_op jit(solution)/shard_map/ppermute | solution.py:20
  1421.2 37.9 %collective-permute-start.61 = (f32[256,1024]{1,0:T(8,128)S(1)}, f32[256,1024]{1,0:T(8,128)S(1)}, u32[]{:S(2)}, u32[]{:S(2)}) collective-permute-start(f32[256,1024]{1,0:T(8,128)S(1)} %pad_maximum_fusion.24), channel_id=1, source_target_pairs={{0,8},{8,16},{16,24},{24,0},{1,9},{9,17},{17,25},{25,1},{2,10},{10... | collective-permute-start | bytes 3145736 | tf_op jit(solution)/shard_map/ppermute | solution.py:16
  1450.5 22.1 %collective-permute-start.63 = (f32[256,1024]{1,0:T(8,128)S(1)}, f32[256,1024]{1,0:T(8,128)S(1)}, u32[]{:S(2)}, u32[]{:S(2)}) collective-permute-start(f32[256,1024]{1,0:T(8,128)S(1)} %pad_maximum_fusion.25), channel_id=1, source_target_pairs={{0,24},{8,0},{16,8},{24,16},{1,25},{9,1},{17,9},{25,17},{2,26},{10... | collective-permute-start | bytes 3145736 | tf_op jit(solution)/shard_map/ppermute | solution.py:16
  1459.1 70.1 %collective-permute-start.36 = (f32[2,256,1024]{1,2,0:T(8,128)}, f32[2,256,1024]{1,2,0:T(8,128)}, u32[]{:S(2)}, u32[]{:S(2)}) collective-permute-start(f32[2,256,1024]{1,2,0:T(8,128)} %pad_maximum_fusion.11), channel_id=1, source_target_pairs={{0,1},{1,0},{2,3},{3,2},{4,5},{5,4},{6,7},{7,6},{8,9},{9,8},{10,11... | collective-permute-start | bytes 6291464 | tf_op jit(solution)/shard_map/ppermute | solution.py:20
  1519.0 17.6 collective-permute-start.65
  1527.6 97.6 %collective-permute-start.75 = (bf16[512,3072]{1,0:T(8,128)(2,1)}, bf16[512,3072]{1,0:T(8,128)(2,1)}, u32[]{:S(2)}, u32[]{:S(2)}) collective-permute-start(bf16[512,3072]{1,0:T(8,128)(2,1)} %convolution_convert_fusion.2), channel_id=1, source_target_pairs={{0,4},{4,0},{1,5},{5,1},{2,6},{6,2},{3,7},{7,3},{8,12},{12,8},{9,1... | collective-permute-start | bytes 9437192 | tf_op jit(solution)/shard_map/ppermute | solution.py:20
  1530.6 160.9 %collective-permute-start.37 = (f32[256,1024]{0,1:T(8,128)S(1)}, f32[256,1024]{0,1:T(8,128)S(1)}, u32[]{:S(2)}, u32[]{:S(2)}) collective-permute-start(f32[256,1024]{0,1:T(8,128)S(1)} %fusion.34), channel_id=1, source_target_pairs={{0,2},{2,0},{1,3},{3,1},{4,6},{6,4},{5,7},{7,5},{8,10},{10,8},{9,1... | collective-permute-start | bytes 3145736 | tf_op jit(solution)/shard_map/ppermute | solution.py:20
  1536.7 26.9 %collective-permute-start.64 = (bf16[256,1536]{1,0:T(8,128)(2,1)S(1)}, bf16[256,1536]{1,0:T(8,128)(2,1)S(1)}, u32[]{:S(2)}, u32[]{:S(2)}) collective-permute-start(bf16[256,1536]{1,0:T(8,128)(2,1)S(1)} %get-tuple-element.190), channel_id=1, source_target_pairs={{0,24},{8,0},{16,8},{24,16},{1,25},{9,1},{17,9},{25,17},{2,26},{10... | collective-permute-start | bytes 2359304 | tf_op jit(solution)/shard_map/ppermute | solution.py:16
  1537.7 30.3 %collective-permute-start.66 = (bf16[128,1536]{1,0:T(8,128)(2,1)S(1)}, bf16[128,1536]{1,0:T(8,128)(2,1)S(1)}, u32[]{:S(2)}, u32[]{:S(2)}) collective-permute-start(bf16[128,1536]{1,0:T(8,128)(2,1)S(1)} %slice.482), channel_id=1, source_target_pairs={{0,8},{8,16},{16,24},{24,0},{1,9},{9,17},{17,25},{25,1},{2,10},{10... | collective-permute-start | bytes 1179656 | tf_op jit(solution)/shard_map/ppermute | solution.py:16
  1579.4 54.6 %collective-permute-start.68 = (f32[2,256,1024]{1,2,0:T(8,128)S(1)}, f32[2,256,1024]{1,2,0:T(8,128)S(1)}, u32[]{:S(2)}, u32[]{:S(2)}) collective-permute-start(f32[2,256,1024]{1,2,0:T(8,128)S(1)} %pad_maximum_fusion.17), channel_id=1, source_target_pairs={{0,1},{1,0},{2,3},{3,2},{4,5},{5,4},{6,7},{7,6},{8,9},{9,8},{10,11... | collective-permute-start | bytes 6291464 | tf_op jit(solution)/shard_map/ppermute | solution.py:20
  1589.0 58.6 %collective-permute-start.74 = (bf16[512,1024]{1,0:T(8,128)(2,1)}, bf16[512,1024]{1,0:T(8,128)(2,1)S(1)}, u32[]{:S(2)}, u32[]{:S(2)}) collective-permute-start(bf16[512,1024]{1,0:T(8,128)(2,1)} %convolution_convert_fusion.4), channel_id=1, source_target_pairs={{0,4},{4,0},{1,5},{5,1},{2,6},{6,2},{3,7},{7,3},{8,12},{12,8},{9,1... | collective-permute-start | bytes 3145736 | tf_op jit(solution)/shard_map/ppermute | solution.py:20
  1593.5 86.4 %collective-permute-start.73 = (bf16[512,1536]{1,0:T(8,128)(2,1)}, bf16[512,1536]{1,0:T(8,128)(2,1)S(1)}, u32[]{:S(2)}, u32[]{:S(2)}) collective-permute-start(bf16[512,1536]{1,0:T(8,128)(2,1)} %convolution_convert_fusion.3), channel_id=1, source_target_pairs={{0,4},{4,0},{1,5},{5,1},{2,6},{6,2},{3,7},{7,3},{8,12},{12,8},{9,1... | collective-permute-start | bytes 4718600 | tf_op jit(solution)/shard_map/ppermute | solution.py:20
  1632.0 18.2 %collective-permute-start.78 = (f32[2,128]{1,0:T(2,128)S(1)}, f32[2,128]{1,0:T(2,128)S(1)}, u32[]{:S(2)}, u32[]{:S(2)}) collective-permute-start(f32[2,128]{1,0:T(2,128)S(1)} %pad_maximum_fusion.35), channel_id=1, source_target_pairs={{0,8},{8,0},{16,24},{24,16},{1,9},{9,1},{17,25},{25,17},{2,10},{10... | collective-permute-start | bytes 3080 | tf_op jit(solution)/shard_map/ppermute | solution.py:20
  1634.2 47.6 %collective-permute-start.69 = (f32[256,1024]{0,1:T(8,128)S(1)}, f32[256,1024]{0,1:T(8,128)S(1)}, u32[]{:S(2)}, u32[]{:S(2)}) collective-permute-start(f32[256,1024]{0,1:T(8,128)S(1)} %fusion.25), channel_id=1, source_target_pairs={{0,2},{2,0},{1,3},{3,1},{4,6},{6,4},{5,7},{7,5},{8,10},{10,8},{9,1... | collective-permute-start | bytes 3145736 | tf_op jit(solution)/shard_map/ppermute | solution.py:20
  1650.2 37.1 %collective-permute-start.79 = (f32[2,128]{1,0:T(2,128)S(1)}, f32[2,128]{1,0:T(2,128)S(1)}, u32[]{:S(2)}, u32[]{:S(2)}) collective-permute-start(f32[2,128]{1,0:T(2,128)S(1)} %fusion.101), channel_id=1, source_target_pairs={{0,24},{8,16},{16,8},{24,0},{1,25},{9,17},{17,9},{25,1},{2,26},{10... | collective-permute-start | bytes 3080 | tf_op jit(solution)/shard_map/ppermute | solution.py:20
  1694.5 71.4 %collective-permute-start.72 = (f32[256,1024]{0,1:T(8,128)S(1)}, f32[256,1024]{0,1:T(8,128)S(1)}, u32[]{:S(2)}, u32[]{:S(2)}) collective-permute-start(f32[256,1024]{0,1:T(8,128)S(1)} %pad_maximum_fusion.27), channel_id=1, source_target_pairs={{0,0},{1,8},{2,16},{3,24},{8,1},{9,9},{10,17},{11,25},{16,2},{17,1... | collective-permute-start | bytes 3145736 | tf_op jit(solution)/shard_map/ppermute | solution.py:31
  1697.2 67.8 %collective-permute-start.38 = (bf16[256,1024]{0,1:T(8,128)(2,1)S(1)}, bf16[256,1024]{0,1:T(8,128)(2,1)S(1)}, u32[]{:S(2)}, u32[]{:S(2)}) collective-permute-start(bf16[256,1024]{0,1:T(8,128)(2,1)S(1)} %pad_maximum_fusion.30), channel_id=1, source_target_pairs={{0,0},{1,8},{2,16},{3,24},{8,1},{9,9},{10,17},{11,25},{16,2},{17,1... | collective-permute-start | bytes 1572872 | tf_op jit(solution)/shard_map/ppermute | solution.py:31
  (141 other events, 2962.4 us)

commit v2 on v1

--- a/solution.py
+++ b/solution.py
@@ -38,26 +38,75 @@
     return value + flip(value, "a", 3)
 
 
-def ring_scatter(partial):
-    rows = partial.shape[0] // 4
-    half = rows // 2
-    one = partial[rows : 2 * rows]
-    two = partial[2 * rows : 3 * rows]
-    three = partial[3 * rows :]
-    up_first = shift(two[:half], "a", 1)
-    down_first = shift(two[half:], "a", -1)
-    one = jnp.concatenate([one[:half] + up_first, one[half:]], axis=0)
-    three = jnp.concatenate([three[:half], three[half:] + down_first], axis=0)
-    return partial[:rows] + shift(one, "a", 1) + shift(three, "a", -1)
-
-
-def ring_gather(own):
-    half = own.shape[0] // 2
-    from_before = shift(own, "a", 1)
-    from_after = shift(own, "a", -1)
-    top = shift(from_before[:half], "a", 1)
-    bottom = shift(from_after[half:], "a", -1)
-    return jnp.concatenate([own, from_after, top, bottom, from_before], axis=0)
+def line(value, pairs):
+    return lax.ppermute(value, "a", pairs)
+
+
+def ring_scatter(partial, held=()):
+    zero, one, two, three = jnp.split(partial, 4, axis=0)
+    i = lax.axis_index("a")
+    two = two + line(jnp.where(i == 0, three, one), [(0, 1), (3, 2)])
+    two, *held = lax.optimization_barrier((two, *held))
+    one = one + line(two, [(0, 1), (1, 2)])
+    three = three + line(two, [(3, 2), (2, 1)])
+    total = zero + line(one, [(0, 1), (1, 2), (2, 3)]) + line(three, [(3, 2), (2, 1), (1, 0)])
+    return (total, *held) if held else total
+
+
+def ring_blocks(own):
+    i = lax.axis_index("a")
+    before = line(own, [(0, 1), (1, 2), (2, 3)])
+    after = line(own, [(3, 2), (2, 1), (1, 0)])
+    before_two = line(before, [(1, 2), (2, 3)])
+    after_two = line(after, [(2, 1), (1, 0)])
+    far = line(jnp.where(i == 2, before_two, after_two), [(2, 3), (1, 0)])
+    return [
+        own,
+        jnp.where(i == 3, far, after),
+        jnp.where(i < 2, after_two, before_two),
+        jnp.where(i == 0, far, before),
+    ]
+
+
+def ring_gather(own, axis=0):
+    return jnp.concatenate(ring_blocks(own), axis=axis)
+
+
+def column_block(value, r):
+    size = lax.axis_size("a")
+    width = value.shape[1] // size
+    return lax.dynamic_slice_in_dim(value, ((lax.axis_index("a") + r) % size) * width, width, 1)
+
+
+def ring_columns(value):
+    return jnp.concatenate([column_block(value, r) for r in range(4)], axis=1)
+
+
+def plain_columns(value):
+    twice = 2 * lax.axis_index("a")
+    return jnp.concatenate([column_block(value, r - twice) for r in range(4)], axis=1)
+
+
+def swap_columns(shards):
+    def blocks(r):
+        return jnp.concatenate([column_block(shard, r) for shard in shards], axis=1)
+
+    return [blocks(0)] + [shift(blocks(4 - r), "a", 4 - r) for r in (1, 2, 3)]
+
+
+def together(*values):
+    return lax.optimization_barrier(values)
+
+
+def gather_all(own):
+    pieces = ring_blocks(jnp.concatenate([own, flip(own, "x")], axis=0))
+    return [jnp.concatenate([piece, flip(piece, "c")], axis=0) for piece in pieces]
+
+
+def flip_scatter(partial):
+    blocks = partial.reshape(2, 2, partial.shape[0] // 4, partial.shape[1])
+    pair = blocks[0] + flip(blocks[1], "c")
+    return pair[0] + flip(pair[1], "x")
 
 
 def tensor_scatter(partial):
@@ -89,25 +138,18 @@
     )
 
 
-def own_half_first(value):
+def chunk_gains(value):
     if lax.axis_size("b") != 2:
-        return value
-    half = value.shape[-1] // 2
-    b = lax.axis_index("b")
-    axis = value.ndim - 1
-    return jnp.concatenate(
-        [
-            lax.dynamic_slice_in_dim(value, b * half, half, axis),
-            lax.dynamic_slice_in_dim(value, (1 - b) * half, half, axis),
-        ],
-        axis=axis,
-    )
+        return lax.all_gather(value, ("b", "x", "c"), axis=0, tiled=False)
+    lane = (lax.axis_index("b") * 2 + lax.axis_index("x")) * 2 + lax.axis_index("c")
+    total = lax.dynamic_update_slice_in_dim(jnp.zeros((8,) + value.shape, f32), value[None], lane, 0)
+    for axis in ("c", "x", "b"):
+        total = total + flip(total, axis)
+    return total
 
 
 def fetch(shard):
-    if lax.axis_size("b") == 2:
-        return (shard, flip(shard, "b"))
-    return (lax.all_gather(shard, "b", axis=0, tiled=True),)
+    return lax.all_gather(shard, "b", axis=0, tiled=True)
 
 
 def dot(left, right, left_dim, right_dim):
@@ -116,28 +158,40 @@
     )
 
 
-def project_in(rows, pieces):
+def project_in(rows, weight):
+    return dot(rows, weight, 1, 0)
+
+
+def project_out(rows, weight):
+    return dot(rows, weight, 1, 1)
+
+
+def project_all(pieces, weights):
     total = None
-    at = 0
-    for piece in pieces:
-        part = dot(rows[:, at : at + piece.shape[0]], piece, 1, 0)
+    for piece, weight in zip(pieces, weights):
+        part = project_in(piece, weight)
         total = part if total is None else total + part
-        at += piece.shape[0]
     return total
 
 
-def project_out(rows, pieces):
-    return jnp.concatenate([dot(rows, piece, 1, 1) for piece in pieces], axis=1)
+def project_blocks(blocks, weight, total=None):
+    width = blocks[0].shape[1]
+    for r, block in enumerate(blocks):
+        part = project_out(block, weight[:, r * width : (r + 1) * width])
+        total = part if total is None else total + part
+    return total
+
+
+def weight_partial(rows, grads):
+    return dot(rows, grads, 0, 0).astype(bf16)
+
+
+def pair_scatter(partial):
+    return lax.psum_scatter(partial, "b", scatter_dimension=0, tiled=True).astype(f32)
 
 
 def weight_grad(rows, grads):
-    if lax.axis_size("b") == 2:
-        half = rows.shape[1] // 2
-        sent = dot(rows[:, half:], grads, 0, 0).astype(bf16)
-        return dot(rows[:, :half], grads, 0, 0) + flip(sent, "b").astype(f32)
-    return lax.psum_scatter(
-        dot(rows, grads, 0, 0).astype(bf16), "b", scatter_dimension=0, tiled=True
-    ).astype(f32)
+    return pair_scatter(weight_partial(rows, grads))
 
 
 def rope_tables(segments, head_size):
@@ -253,64 +307,78 @@
     query_width = w_query.shape[1]
     kv_width = key_weight.shape[1]
 
-    x_block = own_half_first(transpose_blocks(tokens)).astype(f32)
-    attn_gain = own_half_first(lax.all_gather(attn_gain, ("b", "x", "c"), axis=0, tiled=True))
-    ffn_gain = own_half_first(lax.all_gather(ffn_gain, ("b", "x", "c"), axis=0, tiled=True))
+    x_block = transpose_blocks(tokens).astype(f32)
+    dy_block = transpose_blocks(cotangent)
+    gains = chunk_gains(jnp.stack([attn_gain, ffn_gain]))
+    attn_gain = gains[:, 0].reshape(-1)
+    ffn_gain = gains[:, 1].reshape(-1)
     wqkv = fetch(jnp.concatenate([w_query, key_weight, value_weight], axis=1))
     inv_one = lax.rsqrt(ring_sum(jnp.sum(x_block * x_block, axis=1, keepdims=True)) / width + epsilon)
     normed_one = x_block * inv_one
-    hidden_one = tensor_gather((normed_one * attn_gain).astype(bf16))
-    qkv = ring_scatter(project_in(hidden_one, wqkv))
+    hidden_block, dy_block = together((normed_one * attn_gain).astype(bf16), dy_block)
+    columns = swap_columns([w_gate, w_up])
+    hidden_one = tensor_gather(hidden_block)
+    qkv, *columns = ring_scatter(project_in(hidden_one, wqkv), tuple(columns))
+    wo = fetch(w_out)
+    columns = [fetch(piece) for piece in columns]
+    qkv, down = together(qkv, w_down)
+    down = swap_columns([down])
     mixed, saved = attention_forward(qkv, segments, query_gain, key_gain, kv_heads)
-    mixed_rows = ring_gather(mixed)
-    wo = fetch(w_out)
+    mixed, *down = together(mixed, *down)
+    down = [fetch(piece) for piece in down]
+    mixed_rows, dy_block = together(ring_gather(mixed), dy_block)
+    dy_pieces = gather_all(dy_block)
     resid = x_block + tensor_scatter(project_out(mixed_rows, wo))
     inv_two = lax.rsqrt(ring_sum(jnp.sum(resid * resid, axis=1, keepdims=True)) / width + epsilon)
     normed_two = resid * inv_two
-    hidden_two = tensor_gather((normed_two * ffn_gain).astype(bf16))
-
-    dy_block = own_half_first(transpose_blocks(cotangent))
-    dy_rows = tensor_gather(dy_block)
-    wd = fetch(w_down)
-    d_act = ring_scatter(project_in(dy_rows, wd))
-    wg = fetch(w_gate)
-    wu = fetch(w_up)
-    gate = ring_scatter(project_in(hidden_two, wg))
-    up = ring_scatter(project_in(hidden_two, wu))
+    hidden_block, *dy_pieces = together((normed_two * ffn_gain).astype(bf16), *dy_pieces)
+    dy_rows = dy_pieces[0]
+    hidden_pieces = gather_all(hidden_block)
+    hidden_two = hidden_pieces[0]
+
+    d_act = project_all(dy_pieces, down)
+    gate, up = jnp.split(project_all(hidden_pieces, columns), 2, axis=1)
+    wg = fetch(ring_columns(w_gate))
+    wu = fetch(ring_columns(w_up))
+    wd = fetch(ring_columns(w_down))
     sig = jax.nn.sigmoid(gate)
     act = (gate * sig * up).astype(bf16)
     d_gate = (d_act * up * sig * (1.0 + gate * (1.0 - sig))).astype(bf16)
     d_up = (d_act * (gate * sig)).astype(bf16)
-    d_gate_rows = ring_gather(d_gate)
-    d_up_rows = ring_gather(d_up)
-    d_hidden_two = tensor_scatter(project_out(d_gate_rows, wg) + project_out(d_up_rows, wu))
-    act_rows = ring_gather(act)
-    ffn_out = tensor_scatter(project_out(act_rows, wd))
-    block_out = transpose_blocks(own_half_first((resid + ffn_out).astype(bf16)))
+    d_gate = ring_blocks(d_gate)
+    d_up = ring_blocks(d_up)
+    d_hidden_two = flip_scatter(project_blocks(d_up, wu, project_blocks(d_gate, wg)))
+    *d_up, act = together(*d_up, act)
+    act_rows = ring_gather(act, 1)
     ffn_gain_part = jnp.sum(d_hidden_two * normed_two, axis=0)
     e_two = d_hidden_two * ffn_gain
     stat_two = ring_sum(jnp.sum(e_two * normed_two, axis=1, keepdims=True)) / width
     d_resid = dy_block.astype(f32) + inv_two * (e_two - normed_two * stat_two)
-    d_resid_rows = tensor_gather(d_resid.astype(bf16))
+    d_resid_rows, act_rows = together(tensor_gather(d_resid.astype(bf16)), act_rows)
     d_mixed = ring_scatter(project_in(d_resid_rows, wo))
+    grad_down = weight_partial(dy_rows, act_rows)
+    ffn_out = project_out(act_rows, wd)
+    d_mixed, grad_down, ffn_out = together(d_mixed, grad_down, ffn_out)
+    grad_down = pair_scatter(grad_down)
+    ffn_out = flip_scatter(ffn_out)
+    block_out = transpose_blocks((resid + ffn_out).astype(bf16))
     d_qkv, query_part, key_part = attention_backward(d_mixed, saved, query_gain, key_gain)
     d_qkv_rows = ring_gather(d_qkv)
     d_hidden_one = tensor_scatter(project_out(d_qkv_rows, wqkv))
+    grad_gate = plain_columns(weight_grad(hidden_two, jnp.concatenate(d_gate, axis=1)))
+    grad_up = plain_columns(weight_grad(hidden_two, jnp.concatenate(d_up, axis=1)))
+    d_hidden_one, grad_gate, grad_up = together(d_hidden_one, grad_gate, grad_up)
     attn_gain_part = jnp.sum(d_hidden_one * normed_one, axis=0)
     e_one = d_hidden_one * attn_gain
     stat_one = ring_sum(jnp.sum(e_one * normed_one, axis=1, keepdims=True)) / width
     d_tokens = d_resid + inv_one * (e_one - normed_one * stat_one)
-    d_tokens = transpose_blocks(own_half_first(d_tokens))
-
-    grad_down = weight_grad(dy_rows, act_rows)
-    grad_gate = weight_grad(hidden_two, d_gate_rows)
-    grad_up = weight_grad(hidden_two, d_up_rows)
+    d_tokens = transpose_blocks(d_tokens)
     grad_out = weight_grad(d_resid_rows, mixed_rows)
     grad_qkv = weight_grad(hidden_one, d_qkv_rows)
 
     head_parts = ring_sum(jnp.stack([query_part, key_part]))
     gains = jnp.concatenate(
-        [own_half_first(attn_gain_part), own_half_first(ffn_gain_part), head_parts.reshape(-1)]
+        [attn_gain_part, ffn_gain_part, head_parts.reshape(-1)]
     ).reshape(-1, head)
     gains = gains + flip(gains, "c")
     gains = gains + flip(gains, "x")
@@ -330,7 +398,7 @@
         grad_out,
         grad_gate,
         grad_up,
-        grad_down,
+        plain_columns(grad_down),
         lax.dynamic_slice_in_dim(flat, lane * part, part),
         lax.dynamic_slice_in_dim(flat, chunk + lane * part, part),
         flat[2 * chunk : 2 * chunk + head],

time: 1780 us -> 1460 us (0.82)
  waiting for transfers between devices: 1090 us -> 819 us
  starting transfers between devices: 304 us -> 206 us
  matrix products: 160 us -> 194 us
  other arithmetic: 99.9 us -> 132 us
    ppermute x0 -> x45, waiting for transfers between devices: none -> 454 us  [line(): return lax.ppermute(value, 'a', pairs)]
    ppermute x40 -> x6, waiting for transfers between devices: 557 us -> 155 us  [shift(): lax.ppermute(value, axis, [(i, (i + step) % size) for i in range(size)])]
    ppermute x39 -> x38, waiting for transfers between devices: 388 us -> 113 us  [flip(): lax.ppermute(value, axis, [(i, i ^ mask) for i in range(lax.axis_size(axi...]
    ppermute x40 -> x6, starting transfers between devices: 258 us -> 9.67 us  [shift(): lax.ppermute(value, axis, [(i, (i + step) % size) for i in range(size)])]
    ppermute x0 -> x45, starting transfers between devices: none -> 128 us  [line(): return lax.ppermute(value, 'a', pairs)]
    ppermute x4, waiting for transfers between devices: 145 us -> 78.1 us  [transpose_blocks(): return lax.ppermute(value, ('a', 'x', 'c'), pairs)]
    dot_general x30 -> x26, matrix products: 149 us -> 187 us  [dot(): lax.dot_general(left, right, (((left_dim,), (right_dim,)), ((), ())), pre...]
    select_n x0 -> x16, other arithmetic: none -> 24.4 us  [the longest x6 7.98 us: ring_blocks(): jnp.where(i < 2, after_two, before_two)]
  transfers between devices with their start and end apart: 83 -> 111, of which waited for: 49 -> 53; matrix products, arithmetic and copies ran while one was open for 17% -> 25% of each run, Pallas kernels for 0% -> 0%
where the time goes in v2:
time: 1460 us; the launch traced here: 1450 us
  waiting for transfers between devices  819 us (56%)
  starting transfers between devices  206 us (14%)
  matrix products  194 us (13%)
  other arithmetic  132 us (9%)
  local copies, waits for them, and re-layouts  78 us (5%)
  between operations  16.8 us (1%)
    ppermute x45, waiting for transfers between devices, line(): return lax.ppermute(value, 'a', pairs)  454 us
    dot_general x26, matrix products, dot(): lax.dot_general(left, right, (((left_dim,), (right_dim,)), ((), ())), pre...  187 us
    ppermute x6, waiting for transfers between devices, shift(): lax.ppermute(value, axis, [(i, (i + step) % size) for i in range(size)])  155 us
    ppermute x45, starting transfers between devices, line(): return lax.ppermute(value, 'a', pairs)  128 us
    ppermute x38, waiting for transfers between devices, flip(): lax.ppermute(value, axis, [(i, i ^ mask) for i in range(lax.axis_size(axi...  113 us
    ppermute x4, waiting for transfers between devices, transpose_blocks(): return lax.ppermute(value, ('a', 'x', 'c'), pairs)  78.1 us
    ppermute x38, starting transfers between devices, flip(): lax.ppermute(value, axis, [(i, i ^ mask) for i in range(lax.axis_size(axi...  53.4 us
  transfers between devices with their start and end apart: 111, of which 53 were waited for; matrix products, arithmetic and copies ran while one was open for 25% of the time, Pallas kernels for 0%

profile of v2, /device:TPU:2, one launch (start us, length us, event | category | flops | bytes accessed | tf_op | source)
XLA Modules:
  0.0 1445.6 jit_solution(5991027626727206576)
XLA Ops:
  20.4 16.3 %collective-permute-done = bf16[256,1024]{1,0:T(8,128)(2,1)S(1)} collective-permute-done((bf16[256,1024]{1,0:T(8,128)(2,1)}, bf16[256,1024]{1,0:T(8,128)(2,1)S(1)}, u32[]{:S(2)}, u32[]{:S(2)}) %collective-permute-start) | collective-permute-done | bytes 524320 | tf_op jit(solution)/shard_map/ppermute | solution.py:31
  40.6 10.5 collective-permute-done.2
  51.3 13.2 collective-permute-done.6
  64.6 9.2 collective-permute-done.7
  83.9 6.4 fusion.89
  91.7 7.8 collective-permute-start.9
  108.2 25.1 %collective-permute-done.9 = f32[256,1536]{1,0:T(8,128)} collective-permute-done((f32[256,1536]{1,0:T(8,128)}, f32[256,1536]{1,0:T(8,128)}, u32[]{:S(2)}, u32[]{:S(2)}) %collective-permute-start.9) | collective-permute-done | bytes 1572896 | tf_op jit(solution)/shard_map/ppermute | solution.py:42
  135.4 35.9 %collective-permute-done.10 = bf16[512,1536]{1,0:T(8,128)(2,1)} collective-permute-done((bf16[512,1536]{1,0:T(8,128)(2,1)}, bf16[512,1536]{1,0:T(8,128)(2,1)}, u32[]{:S(2)}, u32[]{:S(2)}) %collective-permute-start.10) | collective-permute-done | bytes 1572896 | tf_op jit(solution)/shard_map/ppermute | solution.py:16
  171.3 29.5 %collective-permute-done.11 = bf16[512,1536]{1,0:T(8,128)(2,1)} collective-permute-done((bf16[512,1536]{1,0:T(8,128)(2,1)}, bf16[512,1536]{1,0:T(8,128)(2,1)}, u32[]{:S(2)}, u32[]{:S(2)}) %collective-permute-start.11) | collective-permute-done | bytes 1572896 | tf_op jit(solution)/shard_map/ppermute | solution.py:16
  200.8 36.8 %collective-permute-done.12 = bf16[512,1536]{1,0:T(8,128)(2,1)} collective-permute-done((bf16[512,1536]{1,0:T(8,128)(2,1)}, bf16[512,1536]{1,0:T(8,128)(2,1)}, u32[]{:S(2)}, u32[]{:S(2)}) %collective-permute-start.12) | collective-permute-done | bytes 1572896 | tf_op jit(solution)/shard_map/ppermute | solution.py:16
  237.6 5.7 collective-permute-start.13
  244.1 32.3 %collective-permute-done.13 = f32[256,1536]{1,0:T(8,128)S(1)} collective-permute-done((f32[256,1536]{1,0:T(8,128)S(1)}, f32[256,1536]{1,0:T(8,128)S(1)}, u32[]{:S(2)}, u32[]{:S(2)}) %collective-permute-start.13) | collective-permute-done | bytes 1572896 | tf_op jit(solution)/shard_map/ppermute | solution.py:42
  281.3 10.3 collective-permute-start.14
  293.9 27.8 %collective-permute-done.16 = f32[256,1536]{1,0:T(8,128)} collective-permute-done((f32[256,1536]{1,0:T(8,128)}, f32[256,1536]{1,0:T(8,128)}, u32[]{:S(2)}, u32[]{:S(2)}) %collective-permute-start.16) | collective-permute-done | bytes 1572896 | tf_op jit(solution)/shard_map/ppermute | solution.py:42
  329.7 5.6 constant_dynamic-slice_fusion.15
  354.3 6.1 collective-permute-done.17
  360.4 47.0 %collective-permute-done.18 = bf16[512,768]{1,0:T(8,128)(2,1)} collective-permute-done((bf16[512,768]{1,0:T(8,128)(2,1)}, bf16[512,768]{1,0:T(8,128)(2,1)}, u32[]{:S(2)}, u32[]{:S(2)}) %collective-permute-start.18) | collective-permute-done | bytes 786464 | tf_op jit(solution)/shard_map/ppermute | solution.py:16
  417.3 8.3 collective-permute-done.22
  427.6 13.4 collective-permute-done.23
  443.2 13.1 collective-permute-done.24
  460.7 9.0 collective-permute-done.29
  485.6 8.4 collective-permute-done.33
  499.1 17.4 %collective-permute-done.34 = bf16[512,1024]{1,0:T(8,128)(2,1)S(1)} collective-permute-done((bf16[512,1024]{1,0:T(8,128)(2,1)}, bf16[512,1024]{1,0:T(8,128)(2,1)S(1)}, u32[]{:S(2)}, u32[]{:S(2)}) %collective-permute-start.34) | collective-permute-done | bytes 1048608 | tf_op jit(solution)/shard_map/ppermute | solution.py:42
  524.7 16.0 %collective-permute-done.35 = bf16[512,1024]{1,0:T(8,128)(2,1)} collective-permute-done((bf16[512,1024]{1,0:T(8,128)(2,1)S(1)}, bf16[512,1024]{1,0:T(8,128)(2,1)}, u32[]{:S(2)}, u32[]{:S(2)}) %collective-permute-start.35) | collective-permute-done | bytes 1048608 | tf_op jit(solution)/shard_map/ppermute | solution.py:42
  564.1 9.1 collective-permute-done.39
  577.6 17.3 %collective-permute-done.41 = bf16[512,1024]{1,0:T(8,128)(2,1)} collective-permute-done((bf16[512,1024]{1,0:T(8,128)(2,1)}, bf16[512,1024]{1,0:T(8,128)(2,1)}, u32[]{:S(2)}, u32[]{:S(2)}) %collective-permute-start.41) | collective-permute-done | bytes 1048608 | tf_op jit(solution)/shard_map/ppermute | solution.py:42
  608.8 13.9 collective-permute-done.44
  625.3 10.0 collective-permute-start.45
  640.9 6.2 fusion.127
  652.4 8.7 fusion.129
  661.6 8.7 fusion.28
  670.3 9.1 fusion.24
  679.5 14.4 add_add_fusion
  693.9 13.5 all-gather.24.cloned.1.call-done
  707.5 12.4 multiply_convert_fusion.2
  721.2 5.7 collective-permute-start.49
  728.8 29.5 %collective-permute-done.51 = bf16[1024,768]{0,1:T(8,128)(2,1)} collective-permute-done((bf16[1024,768]{0,1:T(8,128)(2,1)}, bf16[1024,768]{0,1:T(8,128)(2,1)}, u32[]{:S(2)}, u32[]{:S(2)}) %collective-permute-start.51) | collective-permute-done | bytes 1572896 | tf_op jit(solution)/shard_map/ppermute | solution.py:42
  761.7 9.2 collective-permute-start.54
  770.8 26.9 %collective-permute-done.52 = bf16[1024,768]{0,1:T(8,128)(2,1)S(1)} collective-permute-done((bf16[1024,768]{0,1:T(8,128)(2,1)}, bf16[1024,768]{0,1:T(8,128)(2,1)S(1)}, u32[]{:S(2)}, u32[]{:S(2)}) %collective-permute-start.52) | collective-permute-done | bytes 1572896 | tf_op jit(solution)/shard_map/ppermute | solution.py:42
  799.5 31.9 %collective-permute-done.56 = bf16[1024,768]{0,1:T(8,128)(2,1)S(1)} collective-permute-done((bf16[1024,768]{0,1:T(8,128)(2,1)}, bf16[1024,768]{0,1:T(8,128)(2,1)S(1)}, u32[]{:S(2)}, u32[]{:S(2)}) %collective-permute-start.56) | collective-permute-done | bytes 1572896 | tf_op jit(solution)/shard_map/ppermute | solution.py:42
  834.6 30.5 %collective-permute-done.53 = bf16[1024,768]{0,1:T(8,128)(2,1)S(1)} collective-permute-done((bf16[1024,768]{0,1:T(8,128)(2,1)S(1)}, bf16[1024,768]{0,1:T(8,128)(2,1)S(1)}, u32[]{:S(2)}, u32[]{:S(2)}) %collective-permute-start.53) | collective-permute-done | bytes 1572896 | tf_op jit(solution)/shard_map/ppermute | solution.py:42
  868.5 13.5 fusion.20
  882.1 14.8 %collective-permute-done.57 = bf16[1024,768]{0,1:T(8,128)(2,1)} collective-permute-done((bf16[1024,768]{0,1:T(8,128)(2,1)S(1)}, bf16[1024,768]{0,1:T(8,128)(2,1)}, u32[]{:S(2)}, u32[]{:S(2)}) %collective-permute-start.57) | collective-permute-done | bytes 1572896 | tf_op jit(solution)/shard_map/ppermute | solution.py:42
  901.7 5.8 fusion.43
  915.5 21.3 %collective-permute-done.58 = bf16[1024,768]{0,1:T(8,128)(2,1)} collective-permute-done((bf16[1024,768]{0,1:T(8,128)(2,1)}, bf16[1024,768]{0,1:T(8,128)(2,1)}, u32[]{:S(2)}, u32[]{:S(2)}) %collective-permute-start.58) | collective-permute-done | bytes 1572896 | tf_op jit(solution)/shard_map/ppermute | solution.py:42
  954.5 10.7 add_add_fusion.1
  973.9 30.6 %collective-permute-done.67 = bf16[1024,768]{0,1:T(8,128)(2,1)S(1)} collective-permute-done((bf16[1024,768]{0,1:T(8,128)(2,1)S(1)}, bf16[1024,768]{0,1:T(8,128)(2,1)S(1)}, u32[]{:S(2)}, u32[]{:S(2)}) %collective-permute-start.67) | collective-permute-done | bytes 1572896 | tf_op jit(solution)/shard_map/ppermute | solution.py:42
  1007.1 8.5 collective-permute-start.61
  1015.6 29.2 %collective-permute-done.61 = f32[256,1]{0,1:T(1,128)S(1)} collective-permute-done((f32[256,1]{0,1:T(1,128)S(1)}, f32[256,1]{0,1:T(1,128)S(1)}, u32[]{:S(2)}, u32[]{:S(2)}) %collective-permute-start.61) | collective-permute-done | bytes 1056 | tf_op jit(solution)/shard_map/ppermute | solution.py:20
  1044.8 5.7 collective-permute-start.62
  1057.5 6.8 collective-permute-done.63
  1065.5 13.1 fusion.17
  1078.7 12.7 collective-permute-done.69
  1111.1 16.0 %collective-permute-done.70 = f32[256,1024]{1,0:T(8,128)} collective-permute-done((f32[256,1024]{1,0:T(8,128)}, f32[256,1024]{1,0:T(8,128)}, u32[]{:S(2)}, u32[]{:S(2)}) %collective-permute-start.70) | collective-permute-done | bytes 1048608 | tf_op jit(solution)/shard_map/ppermute | solution.py:42
  1136.8 11.5 convolution_convert_fusion
  1157.9 8.9 collective-permute-start.72
  1166.8 12.1 fusion.131
  1211.3 6.1 collective-permute-start.78
  1221.3 6.9 collective-permute-done.80
  1230.2 15.3 %collective-permute-done.81 = bf16[256,1536]{1,0:T(8,128)(2,1)S(1)} collective-permute-done((bf16[256,1536]{1,0:T(8,128)(2,1)S(1)}, bf16[256,1536]{1,0:T(8,128)(2,1)S(1)}, u32[]{:S(2)}, u32[]{:S(2)}) %collective-permute-start.81) | collective-permute-done | bytes 786464 | tf_op jit(solution)/shard_map/ppermute | solution.py:42
  1247.3 12.6 collective-permute-done.82
  1306.7 26.2 %collective-permute-done.84 = f32[256,1024]{1,0:T(8,128)} collective-permute-done((f32[256,1024]{1,0:T(8,128)}, f32[256,1024]{1,0:T(8,128)}, u32[]{:S(2)}, u32[]{:S(2)}) %collective-permute-start.84) | collective-permute-done | bytes 1048608 | tf_op jit(solution)/shard_map/ppermute | solution.py:20
  1337.0 9.9 collective-permute-start.89
  1375.1 48.6 %collective-permute-done.77 = bf16[256,1024]{1,0:T(8,128)(2,1)S(1)} collective-permute-done((bf16[256,1024]{1,0:T(8,128)(2,1)}, bf16[256,1024]{1,0:T(8,128)(2,1)S(1)}, u32[]{:S(2)}, u32[]{:S(2)}) %collective-permute-start.77) | collective-permute-done | bytes 524320 | tf_op jit(solution)/shard_map/ppermute | solution.py:31
  (651 shorter events, 413.9 us)
Async XLA Ops:
  7.2 76.7 %all-gather.14.cloned.1.call-start = ((), (), s32[]{:S(2)}) async-start(), calls=%async_computation.5 | async-start | bytes 4718592 | tf_op jit(solution)/shard_map/all_gather | solution.py:152
  7.2 29.5 %collective-permute-start = (bf16[256,1024]{1,0:T(8,128)(2,1)}, bf16[256,1024]{1,0:T(8,128)(2,1)S(1)}, u32[]{:S(2)}, u32[]{:S(2)}) collective-permute-start(bf16[256,1024]{1,0:T(8,128)(2,1)} %param.14), channel_id=1, source_target_pairs={{0,0},{1,8},{2,16},{3,24},{8,1},{9,9},{10,17},{11,25},{16,2},{17,1... | collective-permute-start | bytes 1572872 | tf_op jit(solution)/shard_map/ppermute | solution.py:31
  17.9 459.6 %all-gather.16.cloned.1.call-start = ((), (), s32[]{:S(2)}) async-start(), calls=%async_computation.6 | async-start | bytes 3145728 | tf_op jit(solution)/shard_map/all_gather | solution.py:152
  37.1 27.4 %collective-permute-start.6 = (bf16[256,1024]{1,0:T(8,128)(2,1)S(1)}, bf16[256,1024]{1,0:T(8,128)(2,1)S(1)}, u32[]{:S(2)}, u32[]{:S(2)}) collective-permute-start(bf16[256,1024]{1,0:T(8,128)(2,1)S(1)} %copy-done.131), channel_id=1, source_target_pairs={{0,0},{1,8},{2,16},{3,24},{8,1},{9,9},{10,17},{11,25},{16,2},{17,1... | collective-permute-start | bytes 1572872 | tf_op jit(solution)/shard_map/ppermute | solution.py:31
  91.7 41.7 %collective-permute-start.9 = (f32[256,1536]{1,0:T(8,128)}, f32[256,1536]{1,0:T(8,128)}, u32[]{:S(2)}, u32[]{:S(2)}) collective-permute-start(f32[256,1536]{1,0:T(8,128)} %slice_select_fusion), channel_id=1, source_target_pairs={{0,8},{24,16},{1,9},{25,17},{2,10},{26,18},{3,11},{27,19},{4,12},{... | collective-permute-start | bytes 4718600 | tf_op jit(solution)/shard_map/ppermute | solution.py:42
  100.8 70.5 %collective-permute-start.10 = (bf16[512,1536]{1,0:T(8,128)(2,1)}, bf16[512,1536]{1,0:T(8,128)(2,1)}, u32[]{:S(2)}, u32[]{:S(2)}) collective-permute-start(bf16[512,1536]{1,0:T(8,128)(2,1)} %pad_maximum_fusion.21), channel_id=1, source_target_pairs={{0,24},{8,0},{16,8},{24,16},{1,25},{9,1},{17,9},{25,17},{2,26},{10... | collective-permute-start | bytes 4718600 | tf_op jit(solution)/shard_map/ppermute | solution.py:16
  105.1 95.7 %collective-permute-start.11 = (bf16[512,1536]{1,0:T(8,128)(2,1)}, bf16[512,1536]{1,0:T(8,128)(2,1)}, u32[]{:S(2)}, u32[]{:S(2)}) collective-permute-start(bf16[512,1536]{1,0:T(8,128)(2,1)} %pad_maximum_fusion.22), channel_id=1, source_target_pairs={{0,16},{8,24},{16,0},{24,8},{1,17},{9,25},{17,1},{25,9},{2,18},{10... | collective-permute-start | bytes 4718600 | tf_op jit(solution)/shard_map/ppermute | solution.py:16
  106.4 131.2 %collective-permute-start.12 = (bf16[512,1536]{1,0:T(8,128)(2,1)}, bf16[512,1536]{1,0:T(8,128)(2,1)}, u32[]{:S(2)}, u32[]{:S(2)}) collective-permute-start(bf16[512,1536]{1,0:T(8,128)(2,1)} %pad_maximum_fusion.23), channel_id=1, source_target_pairs={{0,8},{8,16},{16,24},{24,0},{1,9},{9,17},{17,25},{25,1},{2,10},{10... | collective-permute-start | bytes 4718600 | tf_op jit(solution)/shard_map/ppermute | solution.py:16
  237.6 38.8 %collective-permute-start.13 = (f32[256,1536]{1,0:T(8,128)S(1)}, f32[256,1536]{1,0:T(8,128)S(1)}, u32[]{:S(2)}, u32[]{:S(2)}) collective-permute-start(f32[256,1536]{1,0:T(8,128)S(1)} %slice_add_fusion), channel_id=1, source_target_pairs={{0,8},{8,16},{1,9},{9,17},{2,10},{10,18},{3,11},{11,19},{4,12},{12... | collective-permute-start | bytes 4718600 | tf_op jit(solution)/shard_map/ppermute | solution.py:42
  243.3 33.1 %collective-permute-start.15 = (f32[256,1536]{1,0:T(8,128)S(1)}, f32[256,1536]{1,0:T(8,128)S(1)}, u32[]{:S(2)}, u32[]{:S(2)}) collective-permute-start(f32[256,1536]{1,0:T(8,128)S(1)} %slice_add_fusion), channel_id=1, source_target_pairs={{24,16},{16,8},{25,17},{17,9},{26,18},{18,10},{27,19},{19,11},{28,... | collective-permute-start | bytes 4718600 | tf_op jit(solution)/shard_map/ppermute | solution.py:42
  280.1 41.6 %collective-permute-start.16 = (f32[256,1536]{1,0:T(8,128)}, f32[256,1536]{1,0:T(8,128)}, u32[]{:S(2)}, u32[]{:S(2)}) collective-permute-start(f32[256,1536]{1,0:T(8,128)} %get-tuple-element.110), channel_id=1, source_target_pairs={{24,16},{16,8},{8,0},{25,17},{17,9},{9,1},{26,18},{18,10},{10,2},{... | collective-permute-start | bytes 4718600 | tf_op jit(solution)/shard_map/ppermute | solution.py:42
  281.3 41.1 %collective-permute-start.14 = (f32[256,1536]{1,0:T(8,128)S(1)}, f32[256,1536]{1,0:T(8,128)}, u32[]{:S(2)}, u32[]{:S(2)}) collective-permute-start(f32[256,1536]{1,0:T(8,128)S(1)} %get-tuple-element.109), channel_id=1, source_target_pairs={{0,8},{8,16},{16,24},{1,9},{9,17},{17,25},{2,10},{10,18},{18,26},{... | collective-permute-start | bytes 4718600 | tf_op jit(solution)/shard_map/ppermute | solution.py:42
  291.6 311.6 %all-gather.22.cloned.1.call-start = ((), (), s32[]{:S(2)}) async-start(), calls=%async_computation.9 | async-start | bytes 2359296 | tf_op jit(solution)/shard_map/all_gather | solution.py:152
  342.0 65.4 %collective-permute-start.18 = (bf16[512,768]{1,0:T(8,128)(2,1)}, bf16[512,768]{1,0:T(8,128)(2,1)}, u32[]{:S(2)}, u32[]{:S(2)}) collective-permute-start(bf16[512,768]{1,0:T(8,128)(2,1)} %get-tuple-element.213), channel_id=1, source_target_pairs={{0,16},{8,24},{16,0},{24,8},{1,17},{9,25},{17,1},{25,9},{2,18},{10... | collective-permute-start | bytes 2359304 | tf_op jit(solution)/shard_map/ppermute | solution.py:16
  342.0 65.4 %collective-permute-start.19 = (bf16[512,768]{1,0:T(8,128)(2,1)}, bf16[512,768]{1,0:T(8,128)(2,1)}, u32[]{:S(2)}, u32[]{:S(2)}) collective-permute-start(bf16[512,768]{1,0:T(8,128)(2,1)} %get-tuple-element.214), channel_id=1, source_target_pairs={{0,8},{8,16},{16,24},{24,0},{1,9},{9,17},{17,25},{25,1},{2,10},{10... | collective-permute-start | bytes 2359304 | tf_op jit(solution)/shard_map/ppermute | solution.py:16
  407.4 227.9 %all-gather.18.cloned.1.call-start = ((), (), s32[]{:S(2)}) async-start(), calls=%async_computation.7 | async-start | bytes 2359296 | tf_op jit(solution)/shard_map/all_gather | solution.py:152
  408.0 232.9 %all-gather.20.cloned.1.call-start = ((), (), s32[]{:S(2)}) async-start(), calls=%async_computation.8 | async-start | bytes 2359296 | tf_op jit(solution)/shard_map/all_gather | solution.py:152
  408.6 243.8 %all-gather.26.cloned.1.call-start = ((), (), s32[]{:S(2)}) async-start(), calls=%async_computation.11 | async-start | bytes 4718592 | tf_op jit(solution)/shard_map/all_gather | solution.py:152
  409.2 252.5 %all-gather.30.cloned.1.call-start = ((), (), s32[]{:S(2)}) async-start(), calls=%async_computation.13 | async-start | bytes 4718592 | tf_op jit(solution)/shard_map/all_gather | solution.py:152
  409.9 260.4 %all-gather.28.cloned.1.call-start = ((), (), s32[]{:S(2)}) async-start(), calls=%async_computation.12 | async-start | bytes 4718592 | tf_op jit(solution)/shard_map/all_gather | solution.py:152
  410.7 268.8 %all-gather.32.cloned.1.call-start = ((), (), s32[]{:S(2)}) async-start(), calls=%async_computation.14 | async-start | bytes 4718592 | tf_op jit(solution)/shard_map/all_gather | solution.py:152
  411.4 296.1 %all-gather.24.cloned.1.call-start = ((), (), s32[]{:S(2)}) async-start(), calls=%async_computation.10 | async-start | bytes 2359296 | tf_op jit(solution)/shard_map/all_gather | solution.py:152
  459.9 441.8 %all-gather.36.cloned.1.call-start = ((), (), s32[]{:S(2)}) async-start(), calls=%async_computation.16 | async-start | bytes 9437184 | tf_op jit(solution)/shard_map/all_gather | solution.py:152
  470.7 23.4 %collective-permute-start.33 = (bf16[512,1024]{1,0:T(8,128)(2,1)}, bf16[512,1024]{1,0:T(8,128)(2,1)}, u32[]{:S(2)}, u32[]{:S(2)}) collective-permute-start(bf16[512,1024]{1,0:T(8,128)(2,1)} %constant_dynamic-update-slice_fusion), channel_id=1, source_target_pairs={{24,16},{16,8},{8,0},{25,17},{17,9},{9,1},{26,18},{18,10},{10,2},{... | collective-permute-start | bytes 3145736 | tf_op jit(solution)/shard_map/ppermute | solution.py:42
  471.9 23.4 %collective-permute-start.31 = (bf16[512,1024]{1,0:T(8,128)(2,1)}, bf16[512,1024]{1,0:T(8,128)(2,1)}, u32[]{:S(2)}, u32[]{:S(2)}) collective-permute-start(bf16[512,1024]{1,0:T(8,128)(2,1)} %constant_dynamic-update-slice_fusion), channel_id=1, source_target_pairs={{0,8},{8,16},{16,24},{1,9},{9,17},{17,25},{2,10},{10,18},{18,26},{... | collective-permute-start | bytes 3145736 | tf_op jit(solution)/shard_map/ppermute | solution.py:42
  485.6 34.8 %collective-permute-start.25 = (f32[2,256,1024]{2,1,0:T(8,128)}, f32[2,256,1024]{2,1,0:T(8,128)}, u32[]{:S(2)}, u32[]{:S(2)}) collective-permute-start(f32[2,256,1024]{2,1,0:T(8,128)} %pad_maximum_fusion.11), channel_id=1, source_target_pairs={{0,1},{1,0},{2,3},{3,2},{4,5},{5,4},{6,7},{7,6},{8,9},{9,8},{10,11... | collective-permute-start | bytes 6291464 | tf_op jit(solution)/shard_map/ppermute | solution.py:20
  499.0 408.4 %all-gather.34.cloned.1.call-start = ((), (), s32[]{:S(2)}) async-start(), calls=%async_computation.15 | async-start | bytes 9437184 | tf_op jit(solution)/shard_map/all_gather | solution.py:152
  524.1 30.4 %collective-permute-start.30 = (bf16[512,1024]{1,0:T(8,128)(2,1)}, bf16[512,1024]{1,0:T(8,128)(2,1)}, u32[]{:S(2)}, u32[]{:S(2)}) collective-permute-start(bf16[512,1024]{1,0:T(8,128)(2,1)} %constant_dynamic-update-slice_fusion), channel_id=1, source_target_pairs={{0,1},{1,0},{2,3},{3,2},{4,5},{5,4},{6,7},{7,6},{8,9},{9,8},{10,11... | collective-permute-start | bytes 3145736 | tf_op jit(solution)/shard_map/ppermute | solution.py:20
  524.2 33.3 %collective-permute-start.37 = (bf16[512,1024]{1,0:T(8,128)(2,1)S(1)}, bf16[512,1024]{1,0:T(8,128)(2,1)S(1)}, u32[]{:S(2)}, u32[]{:S(2)}) collective-permute-start(bf16[512,1024]{1,0:T(8,128)(2,1)S(1)} %get-tuple-element.149), channel_id=1, source_target_pairs={{0,1},{1,0},{2,3},{3,2},{4,5},{5,4},{6,7},{7,6},{8,9},{9,8},{10,11... | collective-permute-start | bytes 3145736 | tf_op jit(solution)/shard_map/ppermute | solution.py:20
  576.3 23.6 %collective-permute-start.43 = (bf16[512,1024]{1,0:T(8,128)(2,1)}, bf16[512,1024]{1,0:T(8,128)(2,1)}, u32[]{:S(2)}, u32[]{:S(2)}) collective-permute-start(bf16[512,1024]{1,0:T(8,128)(2,1)} %get-tuple-element.184), channel_id=1, source_target_pairs={{24,16},{16,8},{8,0},{25,17},{17,9},{9,1},{26,18},{18,10},{10,2},{... | collective-permute-start | bytes 3145736 | tf_op jit(solution)/shard_map/ppermute | solution.py:42
  603.1 563.7 %all-gather.38.cloned.1.call-start = ((), (), s32[]{:S(2)}) async-start(), calls=%async_computation.17 | async-start | bytes 9437184 | tf_op jit(solution)/shard_map/all_gather | solution.py:152
  608.7 38.3 %collective-permute-start.40 = (bf16[512,1024]{1,0:T(8,128)(2,1)}, bf16[512,1024]{1,0:T(8,128)(2,1)}, u32[]{:S(2)}, u32[]{:S(2)}) collective-permute-start(bf16[512,1024]{1,0:T(8,128)(2,1)} %get-tuple-element.184), channel_id=1, source_target_pairs={{0,1},{1,0},{2,3},{3,2},{4,5},{5,4},{6,7},{7,6},{8,9},{9,8},{10,11... | collective-permute-start | bytes 3145736 | tf_op jit(solution)/shard_map/ppermute | solution.py:20
  625.3 24.4 %collective-permute-start.45 = (bf16[512,1024]{1,0:T(8,128)(2,1)}, bf16[512,1024]{1,0:T(8,128)(2,1)}, u32[]{:S(2)}, u32[]{:S(2)}) collective-permute-start(bf16[512,1024]{1,0:T(8,128)(2,1)} %get-tuple-element.147), channel_id=1, source_target_pairs={{16,24},{8,0},{17,25},{9,1},{18,26},{10,2},{19,27},{11,3},{20,28},... | collective-permute-start | bytes 3145736 | tf_op jit(solution)/shard_map/ppermute | solution.py:42
  719.9 38.4 %collective-permute-start.51 = (bf16[1024,768]{0,1:T(8,128)(2,1)}, bf16[1024,768]{0,1:T(8,128)(2,1)}, u32[]{:S(2)}, u32[]{:S(2)}) collective-permute-start(bf16[1024,768]{0,1:T(8,128)(2,1)} %get-tuple-element.94), channel_id=1, source_target_pairs={{24,16},{16,8},{8,0},{25,17},{17,9},{9,1},{26,18},{18,10},{10,2},{... | collective-permute-start | bytes 4718600 | tf_op jit(solution)/shard_map/ppermute | solution.py:42
  721.2 38.4 %collective-permute-start.49 = (bf16[1024,768]{0,1:T(8,128)(2,1)}, bf16[1024,768]{0,1:T(8,128)(2,1)}, u32[]{:S(2)}, u32[]{:S(2)}) collective-permute-start(bf16[1024,768]{0,1:T(8,128)(2,1)} %get-tuple-element.94), channel_id=1, source_target_pairs={{0,8},{8,16},{16,24},{1,9},{9,17},{17,25},{2,10},{10,18},{18,26},{... | collective-permute-start | bytes 4718600 | tf_op jit(solution)/shard_map/ppermute | solution.py:42
  728.8 561.2 %reduce-scatter.6.cloned.1.call-start = ((), (), s32[]{:S(2)}) async-start(), calls=%async_computation.18 | async-start | bytes 9437184 | tf_op jit(solution)/shard_map/reduce_scatter | solution.py:190
  758.3 39.4 %collective-permute-start.52 = (bf16[1024,768]{0,1:T(8,128)(2,1)}, bf16[1024,768]{0,1:T(8,128)(2,1)S(1)}, u32[]{:S(2)}, u32[]{:S(2)}) collective-permute-start(bf16[1024,768]{0,1:T(8,128)(2,1)} %collective-permute-done.51), channel_id=1, source_target_pairs={{16,8},{8,0},{17,9},{9,1},{18,10},{10,2},{19,11},{11,3},{20,12},{1... | collective-permute-start | bytes 4718600 | tf_op jit(solution)/shard_map/ppermute | solution.py:42
  759.6 38.1 %collective-permute-start.50 = (bf16[1024,768]{0,1:T(8,128)(2,1)}, bf16[1024,768]{0,1:T(8,128)(2,1)S(1)}, u32[]{:S(2)}, u32[]{:S(2)}) collective-permute-start(bf16[1024,768]{0,1:T(8,128)(2,1)} %collective-permute-done.49), channel_id=1, source_target_pairs={{8,16},{16,24},{9,17},{17,25},{10,18},{18,26},{11,19},{19,27},{12,... | collective-permute-start | bytes 4718600 | tf_op jit(solution)/shard_map/ppermute | solution.py:42
  760.4 71.1 %collective-permute-start.56 = (bf16[1024,768]{0,1:T(8,128)(2,1)}, bf16[1024,768]{0,1:T(8,128)(2,1)S(1)}, u32[]{:S(2)}, u32[]{:S(2)}) collective-permute-start(bf16[1024,768]{0,1:T(8,128)(2,1)} %get-tuple-element.73), channel_id=1, source_target_pairs={{24,16},{16,8},{8,0},{25,17},{17,9},{9,1},{26,18},{18,10},{10,2},{... | collective-permute-start | bytes 4718600 | tf_op jit(solution)/shard_map/ppermute | solution.py:42
  761.7 71.1 %collective-permute-start.54 = (bf16[1024,768]{0,1:T(8,128)(2,1)}, bf16[1024,768]{0,1:T(8,128)(2,1)}, u32[]{:S(2)}, u32[]{:S(2)}) collective-permute-start(bf16[1024,768]{0,1:T(8,128)(2,1)} %get-tuple-element.73), channel_id=1, source_target_pairs={{0,8},{8,16},{16,24},{1,9},{9,17},{17,25},{2,10},{10,18},{18,26},{... | collective-permute-start | bytes 4718600 | tf_op jit(solution)/shard_map/ppermute | solution.py:42
  798.0 67.2 %collective-permute-start.53 = (bf16[1024,768]{0,1:T(8,128)(2,1)S(1)}, bf16[1024,768]{0,1:T(8,128)(2,1)S(1)}, u32[]{:S(2)}, u32[]{:S(2)}) collective-permute-start(bf16[1024,768]{0,1:T(8,128)(2,1)S(1)} %get-tuple-element.130), channel_id=1, source_target_pairs={{16,24},{8,0},{17,25},{9,1},{18,26},{10,2},{19,27},{11,3},{20,28},... | collective-permute-start | bytes 4718600 | tf_op jit(solution)/shard_map/ppermute | solution.py:42
  831.4 65.5 %collective-permute-start.57 = (bf16[1024,768]{0,1:T(8,128)(2,1)S(1)}, bf16[1024,768]{0,1:T(8,128)(2,1)}, u32[]{:S(2)}, u32[]{:S(2)}) collective-permute-start(bf16[1024,768]{0,1:T(8,128)(2,1)S(1)} %collective-permute-done.56), channel_id=1, source_target_pairs={{16,8},{8,0},{17,9},{9,1},{18,10},{10,2},{19,11},{11,3},{20,12},{1... | collective-permute-start | bytes 4718600 | tf_op jit(solution)/shard_map/ppermute | solution.py:42
  832.7 64.2 %collective-permute-start.55 = (bf16[1024,768]{0,1:T(8,128)(2,1)}, bf16[1024,768]{0,1:T(8,128)(2,1)}, u32[]{:S(2)}, u32[]{:S(2)}) collective-permute-start(bf16[1024,768]{0,1:T(8,128)(2,1)} %collective-permute-done.54), channel_id=1, source_target_pairs={{8,16},{16,24},{9,17},{17,25},{10,18},{18,26},{11,19},{19,27},{12,... | collective-permute-start | bytes 4718600 | tf_op jit(solution)/shard_map/ppermute | solution.py:42
  882.1 413.3 %reduce-scatter.8.cloned.1.call-start = ((), (), s32[]{:S(2)}) async-start(), calls=%async_computation.19 | async-start | bytes 9437184 | tf_op jit(solution)/shard_map/reduce_scatter | solution.py:190
  900.2 36.6 %collective-permute-start.58 = (bf16[1024,768]{0,1:T(8,128)(2,1)}, bf16[1024,768]{0,1:T(8,128)(2,1)}, u32[]{:S(2)}, u32[]{:S(2)}) collective-permute-start(bf16[1024,768]{0,1:T(8,128)(2,1)} %get-tuple-element.128), channel_id=1, source_target_pairs={{16,24},{8,0},{17,25},{9,1},{18,26},{10,2},{19,27},{11,3},{20,28},... | collective-permute-start | bytes 4718600 | tf_op jit(solution)/shard_map/ppermute | solution.py:42
  966.6 37.9 %collective-permute-start.67 = (bf16[1024,768]{0,1:T(8,128)(2,1)S(1)}, bf16[1024,768]{0,1:T(8,128)(2,1)S(1)}, u32[]{:S(2)}, u32[]{:S(2)}) collective-permute-start(bf16[1024,768]{0,1:T(8,128)(2,1)S(1)} %copy-done.67), channel_id=1, source_target_pairs={{24,16},{16,8},{8,0},{25,17},{17,9},{9,1},{26,18},{18,10},{10,2},{... | collective-permute-start | bytes 4718600 | tf_op jit(solution)/shard_map/ppermute | solution.py:42
  967.9 38.0 %collective-permute-start.65 = (bf16[1024,768]{0,1:T(8,128)(2,1)S(1)}, bf16[1024,768]{0,1:T(8,128)(2,1)S(1)}, u32[]{:S(2)}, u32[]{:S(2)}) collective-permute-start(bf16[1024,768]{0,1:T(8,128)(2,1)S(1)} %copy-done.67), channel_id=1, source_target_pairs={{0,8},{8,16},{16,24},{1,9},{9,17},{17,25},{2,10},{10,18},{18,26},{... | collective-permute-start | bytes 4718600 | tf_op jit(solution)/shard_map/ppermute | solution.py:42
  973.1 33.5 %collective-permute-start.60 = (f32[256,1024]{1,0:T(8,128)S(1)}, f32[256,1024]{1,0:T(8,128)S(1)}, u32[]{:S(2)}, u32[]{:S(2)}) collective-permute-start(f32[256,1024]{1,0:T(8,128)S(1)} %slice_bitcast_fusion.4), channel_id=1, source_target_pairs={{0,2},{2,0},{1,3},{3,1},{4,6},{6,4},{5,7},{7,5},{8,10},{10,8},{9,1... | collective-permute-start | bytes 3145736 | tf_op jit(solution)/shard_map/ppermute | solution.py:20
  1004.5 49.5 %collective-permute-start.68 = (bf16[1024,768]{0,1:T(8,128)(2,1)S(1)}, bf16[1024,768]{0,1:T(8,128)(2,1)S(1)}, u32[]{:S(2)}, u32[]{:S(2)}) collective-permute-start(bf16[1024,768]{0,1:T(8,128)(2,1)S(1)} %collective-permute-done.67), channel_id=1, source_target_pairs={{16,8},{8,0},{17,9},{9,1},{18,10},{10,2},{19,11},{11,3},{20,12},{1... | collective-permute-start | bytes 4718600 | tf_op jit(solution)/shard_map/ppermute | solution.py:42
  1005.9 48.2 %collective-permute-start.66 = (bf16[1024,768]{0,1:T(8,128)(2,1)S(1)}, bf16[1024,768]{0,1:T(8,128)(2,1)S(1)}, u32[]{:S(2)}, u32[]{:S(2)}) collective-permute-start(bf16[1024,768]{0,1:T(8,128)(2,1)S(1)} %collective-permute-done.65), channel_id=1, source_target_pairs={{8,16},{16,24},{9,17},{17,25},{10,18},{18,26},{11,19},{19,27},{12,... | collective-permute-start | bytes 4718600 | tf_op jit(solution)/shard_map/ppermute | solution.py:42
  1007.1 37.7 %collective-permute-start.61 = (f32[256,1]{0,1:T(1,128)S(1)}, f32[256,1]{0,1:T(1,128)S(1)}, u32[]{:S(2)}, u32[]{:S(2)}) collective-permute-start(f32[256,1]{0,1:T(1,128)S(1)} %bitcast.321), channel_id=1, source_target_pairs={{0,8},{8,0},{16,24},{24,16},{1,9},{9,1},{17,25},{25,17},{2,10},{10... | collective-permute-start | bytes 3080 | tf_op jit(solution)/shard_map/ppermute | solution.py:20
  1055.9 35.4 %collective-permute-start.69 = (bf16[1024,768]{0,1:T(8,128)(2,1)}, bf16[1024,768]{0,1:T(8,128)(2,1)}, u32[]{:S(2)}, u32[]{:S(2)}) collective-permute-start(bf16[1024,768]{0,1:T(8,128)(2,1)} %get-tuple-element.126), channel_id=1, source_target_pairs={{16,24},{8,0},{17,25},{9,1},{18,26},{10,2},{19,27},{11,3},{20,28},... | collective-permute-start | bytes 4718600 | tf_op jit(solution)/shard_map/ppermute | solution.py:42
  1065.4 31.4 %collective-permute-start.64 = (bf16[2,256,1024]{2,1,0:T(8,128)(2,1)}, bf16[2,256,1024]{2,1,0:T(8,128)(2,1)}, u32[]{:S(2)}, u32[]{:S(2)}) collective-permute-start(bf16[2,256,1024]{2,1,0:T(8,128)(2,1)} %pad_maximum_fusion.25), channel_id=1, source_target_pairs={{0,1},{1,0},{2,3},{3,2},{4,5},{5,4},{6,7},{7,6},{8,9},{9,8},{10,11... | collective-permute-start | bytes 3145736 | tf_op jit(solution)/shard_map/ppermute | solution.py:20
  1078.6 293.7 %reduce-scatter.12.cloned.1.call-start = ((), (), s32[]{:S(2)}) async-start(), calls=%async_computation.21 | async-start | bytes 3145728 | tf_op jit(solution)/shard_map/reduce_scatter | solution.py:190
  1156.6 24.1 %collective-permute-start.74 = (f32[256,1024]{1,0:T(8,128)}, f32[256,1024]{1,0:T(8,128)S(1)}, u32[]{:S(2)}, u32[]{:S(2)}) collective-permute-start(f32[256,1024]{1,0:T(8,128)} %get-tuple-element.116), channel_id=1, source_target_pairs={{24,16},{16,8},{8,0},{25,17},{17,9},{9,1},{26,18},{18,10},{10,2},{... | collective-permute-start | bytes 3145736 | tf_op jit(solution)/shard_map/ppermute | solution.py:42
  1157.9 24.1 %collective-permute-start.72 = (f32[256,1024]{1,0:T(8,128)}, f32[256,1024]{1,0:T(8,128)}, u32[]{:S(2)}, u32[]{:S(2)}) collective-permute-start(f32[256,1024]{1,0:T(8,128)} %get-tuple-element.115), channel_id=1, source_target_pairs={{0,8},{8,16},{16,24},{1,9},{9,17},{17,25},{2,10},{10,18},{18,26},{... | collective-permute-start | bytes 3145736 | tf_op jit(solution)/shard_map/ppermute | solution.py:42
  1221.3 203.6 %reduce-scatter.10.cloned.1.call-start = ((), (), s32[]{:S(2)}) async-start(), calls=%async_computation.20 | async-start | bytes 4718592 | tf_op jit(solution)/shard_map/reduce_scatter | solution.py:190
  1266.4 162.4 %reduce-scatter.14.cloned.1.call-start = ((), (), s32[]{:S(2)}) async-start(), calls=%async_computation.22 | async-start | bytes 9437184 | tf_op jit(solution)/shard_map/reduce_scatter | solution.py:190
  1279.6 57.5 %collective-permute-start.88 = (f32[2,128]{1,0:T(2,128)S(1)}, f32[2,128]{1,0:T(2,128)S(1)}, u32[]{:S(2)}, u32[]{:S(2)}) collective-permute-start(f32[2,128]{1,0:T(2,128)S(1)} %pad_maximum_fusion.31), channel_id=1, source_target_pairs={{0,8},{8,0},{16,24},{24,16},{1,9},{9,1},{17,25},{25,17},{2,10},{10... | collective-permute-start | bytes 3080 | tf_op jit(solution)/shard_map/ppermute | solution.py:20
  1285.3 71.2 %collective-permute-start.76 = (f32[256,1024]{1,0:T(8,128)}, f32[256,1024]{1,0:T(8,128)}, u32[]{:S(2)}, u32[]{:S(2)}) collective-permute-start(f32[256,1024]{1,0:T(8,128)} %slice_bitcast_fusion.2), channel_id=1, source_target_pairs={{0,2},{2,0},{1,3},{3,1},{4,6},{6,4},{5,7},{7,5},{8,10},{10,8},{9,1... | collective-permute-start | bytes 3145736 | tf_op jit(solution)/shard_map/ppermute | solution.py:20
  1289.2 43.7 %collective-permute-start.84 = (f32[256,1024]{1,0:T(8,128)}, f32[256,1024]{1,0:T(8,128)}, u32[]{:S(2)}, u32[]{:S(2)}) collective-permute-start(f32[256,1024]{1,0:T(8,128)} %fusion.76), channel_id=1, source_target_pairs={{0,2},{2,0},{1,3},{3,1},{4,6},{6,4},{5,7},{7,5},{8,10},{10,8},{9,1... | collective-permute-start | bytes 3145736 | tf_op jit(solution)/shard_map/ppermute | solution.py:20
  1353.6 71.3 %collective-permute-start.87 = (f32[256,1024]{1,0:T(8,128)}, f32[256,1024]{1,0:T(8,128)}, u32[]{:S(2)}, u32[]{:S(2)}) collective-permute-start(f32[256,1024]{1,0:T(8,128)} %fusion.69), channel_id=1, source_target_pairs={{0,0},{1,8},{2,16},{3,24},{8,1},{9,9},{10,17},{11,25},{16,2},{17,1... | collective-permute-start | bytes 3145736 | tf_op jit(solution)/shard_map/ppermute | solution.py:31
  1358.7 65.0 %collective-permute-start.77 = (bf16[256,1024]{1,0:T(8,128)(2,1)}, bf16[256,1024]{1,0:T(8,128)(2,1)S(1)}, u32[]{:S(2)}, u32[]{:S(2)}) collective-permute-start(bf16[256,1024]{1,0:T(8,128)(2,1)} %fusion.81), channel_id=1, source_target_pairs={{0,0},{1,8},{2,16},{3,24},{8,1},{9,9},{10,17},{11,25},{16,2},{17,1... | collective-permute-start | bytes 1572872 | tf_op jit(solution)/shard_map/ppermute | solution.py:31
  1371.3 52.5 %collective-permute-start.92 = (f32[18,128]{1,0:T(8,128)S(1)}, f32[18,128]{1,0:T(8,128)S(1)}, u32[]{:S(2)}, u32[]{:S(2)}) collective-permute-start(f32[18,128]{1,0:T(8,128)S(1)} %fusion.179), channel_id=1, source_target_pairs={{0,4},{4,0},{1,5},{5,1},{2,6},{6,2},{3,7},{7,3},{8,12},{12,8},{9,1... | collective-permute-start | bytes 27656 | tf_op jit(solution)/shard_map/ppermute | solution.py:20
  (181 other events, 2819.3 us)
Sparse Core Ops, SparseCore 0:
  18.0 43.8 all-gather.13
  291.8 31.8 all-gather.15
  407.5 27.4 all-gather.21
  436.4 27.2 all-gather.17
  465.1 27.2 all-gather.19
  494.3 44.9 all-gather.25
  540.8 44.9 all-gather.29
  587.3 44.9 all-gather.27
  633.8 44.9 all-gather.31
  680.2 27.1 all-gather.23
  709.0 80.3 all-gather.35
  790.8 80.3 all-gather.33
  872.8 80.3 all-gather.37
  955.9 77.0 reduce-scatter.5
  1078.7 77.4 reduce-scatter.7
  1221.4 32.3 reduce-scatter.11
  1266.6 50.6 reduce-scatter.9
  1319.4 77.2 reduce-scatter.13

commit v3 on v2

--- a/solution.py
+++ b/solution.py
@@ -42,32 +42,51 @@
     return lax.ppermute(value, "a", pairs)
 
 
-def ring_scatter(partial, held=()):
-    zero, one, two, three = jnp.split(partial, 4, axis=0)
+def ring_scatter(partial, held=(), held_two=()):
+    return ring_add(jnp.split(partial, 4, axis=0), held, held_two)
+
+
+def ring_add(blocks, held=(), held_two=()):
+    zero, one, two, three = blocks
     i = lax.axis_index("a")
     two = two + line(jnp.where(i == 0, three, one), [(0, 1), (3, 2)])
     two, *held = lax.optimization_barrier((two, *held))
     one = one + line(two, [(0, 1), (1, 2)])
     three = three + line(two, [(3, 2), (2, 1)])
+    one, three, *held_two = lax.optimization_barrier((one, three, *held_two))
     total = zero + line(one, [(0, 1), (1, 2), (2, 3)]) + line(three, [(3, 2), (2, 1), (1, 0)])
-    return (total, *held) if held else total
-
-
-def ring_blocks(own):
+    return (total, *held, *held_two) if held or held_two else total
+
+
+def ring_first(own):
+    return line(own, [(0, 1), (1, 2), (2, 3)]), line(own, [(3, 2), (2, 1), (1, 0)])
+
+
+def ring_second(before, behind):
+    return line(before, [(1, 2), (2, 3)]), line(behind, [(2, 1), (1, 0)])
+
+
+def ring_third(before_two, behind_two):
     i = lax.axis_index("a")
-    before = line(own, [(0, 1), (1, 2), (2, 3)])
-    after = line(own, [(3, 2), (2, 1), (1, 0)])
-    before_two = line(before, [(1, 2), (2, 3)])
-    after_two = line(after, [(2, 1), (1, 0)])
-    far = line(jnp.where(i == 2, before_two, after_two), [(2, 3), (1, 0)])
+    return line(jnp.where(i == 2, before_two, behind_two), [(2, 3), (1, 0)])
+
+
+def ring_order(own, before, behind, before_two, behind_two, far):
+    i = lax.axis_index("a")
     return [
         own,
-        jnp.where(i == 3, far, after),
-        jnp.where(i < 2, after_two, before_two),
+        jnp.where(i == 3, far, behind),
+        jnp.where(i < 2, behind_two, before_two),
         jnp.where(i == 0, far, before),
     ]
 
 
+def ring_blocks(own):
+    first = ring_first(own)
+    second = ring_second(*first)
+    return ring_order(own, *first, *second, ring_third(*second))
+
+
 def ring_gather(own, axis=0):
     return jnp.concatenate(ring_blocks(own), axis=axis)
 
@@ -78,20 +97,25 @@
     return lax.dynamic_slice_in_dim(value, ((lax.axis_index("a") + r) % size) * width, width, 1)
 
 
-def ring_columns(value):
-    return jnp.concatenate([column_block(value, r) for r in range(4)], axis=1)
-
-
-def plain_columns(value):
-    twice = 2 * lax.axis_index("a")
-    return jnp.concatenate([column_block(value, r - twice) for r in range(4)], axis=1)
-
-
-def swap_columns(shards):
-    def blocks(r):
-        return jnp.concatenate([column_block(shard, r) for shard in shards], axis=1)
-
-    return [blocks(0)] + [shift(blocks(4 - r), "a", 4 - r) for r in (1, 2, 3)]
+def ring_columns(*values):
+    return jnp.concatenate([column_block(value, r) for r in range(4) for value in values], axis=1)
+
+
+def plain_columns(value, which=0, count=1):
+    size = lax.axis_size("a")
+    width = value.shape[1] // (size * count)
+    a = lax.axis_index("a")
+    blocks = []
+    for j in range(size):
+        at = ((j - a) % size) * count + which
+        blocks.append(lax.dynamic_slice_in_dim(value, at * width, width, 1))
+    return jnp.concatenate(blocks, axis=1).astype(f32)
+
+
+def swapped(shards, r):
+    blocks = [column_block(shard, (4 - r) % 4) for shard in shards]
+    blocks = jnp.concatenate(blocks, axis=1) if len(blocks) > 1 else blocks[0]
+    return shift(blocks, "a", 4 - r) if r else blocks
 
 
 def together(*values):
@@ -99,13 +123,31 @@
 
 
 def gather_all(own):
-    pieces = ring_blocks(jnp.concatenate([own, flip(own, "x")], axis=0))
-    return [jnp.concatenate([piece, flip(piece, "c")], axis=0) for piece in pieces]
-
-
-def flip_scatter(partial):
+    i = lax.axis_index("a")
+
+    def spread(block):
+        pair = jnp.concatenate([block, flip(block, "x")], axis=0)
+        return jnp.concatenate([pair, flip(pair, "c")], axis=0)
+
+    first = ring_first(own)
+    second = ring_second(*first)
+    far = ring_third(*second)
+    two = jnp.where(i < 2, second[1], second[0])
+    return [spread(block) for block in (own, first[1], two, first[0], far)]
+
+
+def ring_pieces(pieces):
+    i = lax.axis_index("a")
+    own, one, two, three, far = pieces
+    return [own, jnp.where(i == 3, far, one), two, jnp.where(i == 0, far, three)]
+
+
+def flip_half(partial):
     blocks = partial.reshape(2, 2, partial.shape[0] // 4, partial.shape[1])
-    pair = blocks[0] + flip(blocks[1], "c")
+    return blocks[0] + flip(blocks[1], "c")
+
+
+def flip_rest(pair):
     return pair[0] + flip(pair[1], "x")
 
 
@@ -167,19 +209,12 @@
 
 
 def project_all(pieces, weights):
-    total = None
-    for piece, weight in zip(pieces, weights):
-        part = project_in(piece, weight)
-        total = part if total is None else total + part
-    return total
-
-
-def project_blocks(blocks, weight, total=None):
-    width = blocks[0].shape[1]
-    for r, block in enumerate(blocks):
-        part = project_out(block, weight[:, r * width : (r + 1) * width])
-        total = part if total is None else total + part
-    return total
+    total = project_in(pieces[0], weights[0])
+    for r in (1, 3, 2):
+        total = total + project_in(pieces[r], weights[r])
+    weight = jnp.where(lax.axis_index("a") == 3, weights[1], weights[3])
+    total, weight, far = together(total, weight, pieces[4])
+    return total + project_in(far, weight)
 
 
 def weight_partial(rows, grads):
@@ -187,11 +222,11 @@
 
 
 def pair_scatter(partial):
-    return lax.psum_scatter(partial, "b", scatter_dimension=0, tiled=True).astype(f32)
+    return lax.psum_scatter(partial, "b", scatter_dimension=0, tiled=True)
 
 
 def weight_grad(rows, grads):
-    return pair_scatter(weight_partial(rows, grads))
+    return pair_scatter(weight_partial(rows, grads)).astype(f32)
 
 
 def rope_tables(segments, head_size):
@@ -308,75 +343,106 @@
     kv_width = key_weight.shape[1]
 
     x_block = transpose_blocks(tokens).astype(f32)
-    dy_block = transpose_blocks(cotangent)
-    gains = chunk_gains(jnp.stack([attn_gain, ffn_gain]))
+    wqkv = jnp.concatenate([w_query, key_weight, value_weight], axis=1)
+    gains, wqkv = together(jnp.stack([attn_gain, ffn_gain]), wqkv)
+    wqkv = fetch(wqkv)
+    gains = chunk_gains(gains)
     attn_gain = gains[:, 0].reshape(-1)
     ffn_gain = gains[:, 1].reshape(-1)
-    wqkv = fetch(jnp.concatenate([w_query, key_weight, value_weight], axis=1))
     inv_one = lax.rsqrt(ring_sum(jnp.sum(x_block * x_block, axis=1, keepdims=True)) / width + epsilon)
     normed_one = x_block * inv_one
-    hidden_block, dy_block = together((normed_one * attn_gain).astype(bf16), dy_block)
-    columns = swap_columns([w_gate, w_up])
+    hidden_block, gate_shard, up_shard = together(
+        (normed_one * attn_gain).astype(bf16), w_gate, w_up
+    )
+    near = [swapped([gate_shard, up_shard], r) for r in (1, 3)]
     hidden_one = tensor_gather(hidden_block)
-    qkv, *columns = ring_scatter(project_in(hidden_one, wqkv), tuple(columns))
+    qkv, *near = ring_scatter(project_in(hidden_one, wqkv), near)
     wo = fetch(w_out)
-    columns = [fetch(piece) for piece in columns]
-    qkv, down = together(qkv, w_down)
-    down = swap_columns([down])
+    zero, one, three = [fetch(piece) for piece in (swapped([w_gate, w_up], 0), *near)]
+    qkv, down_shard = together(qkv, w_down)
+    down = [swapped([down_shard], r) for r in range(4)]
     mixed, saved = attention_forward(qkv, segments, query_gain, key_gain, kv_heads)
-    mixed, *down = together(mixed, *down)
+    mixed, zero, one, three, dy_block, *down = together(mixed, zero, one, three, cotangent, *down)
+    dy_block = transpose_blocks(dy_block)
+    dy_pieces = gather_all(dy_block)
     down = [fetch(piece) for piece in down]
-    mixed_rows, dy_block = together(ring_gather(mixed), dy_block)
-    dy_pieces = gather_all(dy_block)
+    mixed_rows, gate_shard, up_shard = together(ring_gather(mixed), w_gate, w_up)
+    opposite = swapped([gate_shard, up_shard], 2)
     resid = x_block + tensor_scatter(project_out(mixed_rows, wo))
     inv_two = lax.rsqrt(ring_sum(jnp.sum(resid * resid, axis=1, keepdims=True)) / width + epsilon)
     normed_two = resid * inv_two
-    hidden_block, *dy_pieces = together((normed_two * ffn_gain).astype(bf16), *dy_pieces)
+    values = together((normed_two * ffn_gain).astype(bf16), opposite, *down, *dy_pieces)
+    hidden_block, opposite, down, dy_pieces = values[0], values[1], values[2:6], values[6:]
     dy_rows = dy_pieces[0]
+    two = fetch(opposite)
+    columns = [zero, one, two, three]
     hidden_pieces = gather_all(hidden_block)
-    hidden_two = hidden_pieces[0]
-
     d_act = project_all(dy_pieces, down)
     gate, up = jnp.split(project_all(hidden_pieces, columns), 2, axis=1)
-    wg = fetch(ring_columns(w_gate))
-    wu = fetch(ring_columns(w_up))
+    hidden_pieces = ring_pieces(hidden_pieces)
     wd = fetch(ring_columns(w_down))
     sig = jax.nn.sigmoid(gate)
     act = (gate * sig * up).astype(bf16)
     d_gate = (d_act * up * sig * (1.0 + gate * (1.0 - sig))).astype(bf16)
     d_up = (d_act * (gate * sig)).astype(bf16)
-    d_gate = ring_blocks(d_gate)
-    d_up = ring_blocks(d_up)
-    d_hidden_two = flip_scatter(project_blocks(d_up, wu, project_blocks(d_gate, wg)))
-    *d_up, act = together(*d_up, act)
-    act_rows = ring_gather(act, 1)
+    d_gate_up = jnp.concatenate([d_gate, d_up], axis=1)
+    parts = {r: project_out(d_gate_up, columns[r]) for r in (3, 1)}
+    parts[3], parts[1], d_gate_up = together(parts[3], parts[1], d_gate_up)
+    next_grad = weight_partial(hidden_pieces[1], d_gate_up)
+    d_gate_up, next_grad = together(d_gate_up, next_grad)
+    next_grad = shift(pair_scatter(next_grad), "a", 1)
+    parts.update({r: project_out(d_gate_up, columns[r]) for r in (2, 0)})
+    parts = {r: flip_half(parts[r]) for r in (3, 1, 2, 0)}
+    parts[3], *act_first = together(parts[3], *ring_first(act))
+    act_second = ring_second(*act_first)
+    parts = {r: flip_rest(parts[r]) for r in (3, 1, 2, 0)}
+    parts[3], parts[1], next_grad, *act_second = together(
+        parts[3], parts[1], next_grad, *act_second
+    )
+    d_hidden_two, *grads = together(
+        ring_add([parts[r] for r in range(4)]),
+        *[weight_partial(hidden_pieces[r], d_gate_up) for r in (3, 2, 0)],
+    )
+    last_grad, far_grad, own_grad = [pair_scatter(grad) for grad in grads]
+    last_grad = shift(last_grad, "a", 3)
     ffn_gain_part = jnp.sum(d_hidden_two * normed_two, axis=0)
     e_two = d_hidden_two * ffn_gain
     stat_two = ring_sum(jnp.sum(e_two * normed_two, axis=1, keepdims=True)) / width
     d_resid = dy_block.astype(f32) + inv_two * (e_two - normed_two * stat_two)
-    d_resid_rows, act_rows = together(tensor_gather(d_resid.astype(bf16)), act_rows)
-    d_mixed = ring_scatter(project_in(d_resid_rows, wo))
-    grad_down = weight_partial(dy_rows, act_rows)
-    ffn_out = project_out(act_rows, wd)
-    d_mixed, grad_down, ffn_out = together(d_mixed, grad_down, ffn_out)
+    d_resid_rows = tensor_gather(d_resid.astype(bf16))
+    d_mixed, last_grad = together(project_in(d_resid_rows, wo), last_grad)
+    d_mixed, far_grad, own_grad, *act_second = together(
+        ring_scatter(d_mixed), far_grad, own_grad, *act_second
+    )
+    act_third = ring_third(*act_second)
+    d_qkv, query_part, key_part = attention_backward(d_mixed, saved, query_gain, key_gain)
+    d_qkv, act_third = together(d_qkv, act_third)
+    act_rows = jnp.concatenate(ring_order(act, *act_first, *act_second, act_third), axis=1)
+    d_qkv_rows, head_parts, grad_down, ffn_out, grad_out = together(
+        ring_gather(d_qkv),
+        ring_sum(jnp.stack([query_part, key_part])),
+        weight_partial(dy_rows, act_rows),
+        project_out(act_rows, wd),
+        weight_partial(d_resid_rows, mixed_rows),
+    )
     grad_down = pair_scatter(grad_down)
-    ffn_out = flip_scatter(ffn_out)
-    block_out = transpose_blocks((resid + ffn_out).astype(bf16))
-    d_qkv, query_part, key_part = attention_backward(d_mixed, saved, query_gain, key_gain)
-    d_qkv_rows = ring_gather(d_qkv)
-    d_hidden_one = tensor_scatter(project_out(d_qkv_rows, wqkv))
-    grad_gate = plain_columns(weight_grad(hidden_two, jnp.concatenate(d_gate, axis=1)))
-    grad_up = plain_columns(weight_grad(hidden_two, jnp.concatenate(d_up, axis=1)))
-    d_hidden_one, grad_gate, grad_up = together(d_hidden_one, grad_gate, grad_up)
+    grad_out = pair_scatter(grad_out).astype(f32)
+    block_out = transpose_blocks((resid + flip_rest(flip_half(ffn_out))).astype(bf16))
+    d_qkv_rows, far_grad = together(d_qkv_rows, far_grad)
+    d_hidden_one, far_grad = together(
+        tensor_scatter(project_out(d_qkv_rows, wqkv)), shift(far_grad, "a", 2)
+    )
     attn_gain_part = jnp.sum(d_hidden_one * normed_one, axis=0)
     e_one = d_hidden_one * attn_gain
     stat_one = ring_sum(jnp.sum(e_one * normed_one, axis=1, keepdims=True)) / width
     d_tokens = d_resid + inv_one * (e_one - normed_one * stat_one)
     d_tokens = transpose_blocks(d_tokens)
-    grad_out = weight_grad(d_resid_rows, mixed_rows)
+    grad_gate_up = jnp.concatenate([own_grad, last_grad, far_grad, next_grad], axis=1)
+    grad_gate = plain_columns(grad_gate_up, 0, 2)
+    grad_up = plain_columns(grad_gate_up, 1, 2)
+    grad_down = plain_columns(grad_down)
     grad_qkv = weight_grad(hidden_one, d_qkv_rows)
 
-    head_parts = ring_sum(jnp.stack([query_part, key_part]))
     gains = jnp.concatenate(
         [attn_gain_part, ffn_gain_part, head_parts.reshape(-1)]
     ).reshape(-1, head)
@@ -398,7 +464,7 @@
         grad_out,
         grad_gate,
         grad_up,
-        plain_columns(grad_down),
+        grad_down,
         lax.dynamic_slice_in_dim(flat, lane * part, part),
         lax.dynamic_slice_in_dim(flat, chunk + lane * part, part),
         flat[2 * chunk : 2 * chunk + head],

time: 1460 us -> 1380 us (0.945)
  matrix products: 194 us -> 154 us
  starting transfers between devices: 206 us -> 172 us
    ppermute x45 -> x40, waiting for transfers between devices: 454 us -> 317 us  [line(): return lax.ppermute(value, 'a', pairs)]
    ppermute x6 -> x9, waiting for transfers between devices: 155 us -> 219 us  [shift(): lax.ppermute(value, axis, [(i, (i + step) % size) for i in range(size)])]
    ppermute x38 -> x54, waiting for transfers between devices: 113 us -> 159 us  [flip(): lax.ppermute(value, axis, [(i, i ^ mask) for i in range(lax.axis_size(axi...]
    dot_general x26, matrix products: 187 us -> 145 us  [dot(): lax.dot_general(left, right, (((left_dim,), (right_dim,)), ((), ())), pre...]
    ppermute x45 -> x40, starting transfers between devices: 128 us -> 100 us  [line(): return lax.ppermute(value, 'a', pairs)]
    reduce_scatter x5 -> x7, waiting for transfers between devices: 0.01 us -> 21.4 us  [pair_scatter(): return lax.psum_scatter(partial, 'b', scatter_dimension=0, tiled=True)]
    ppermute x4, waiting for transfers between devices: 78.1 us -> 98.3 us  [transpose_blocks(): return lax.ppermute(value, ('a', 'x', 'c'), pairs)]
    ppermute x38 -> x54, starting transfers between devices: 53.4 us -> 38.4 us  [flip(): lax.ppermute(value, axis, [(i, i ^ mask) for i in range(lax.axis_size(axi...]
  transfers between devices with their start and end apart: 111 -> 125, of which waited for: 53 -> 60; matrix products, arithmetic and copies ran while one was open for 25% -> 21% of each run, Pallas kernels for 0% -> 0%
where the time goes in v3:
time: 1380 us; the launch traced here: 1370 us
  waiting for transfers between devices  817 us (59%)
  starting transfers between devices  172 us (12%)
  matrix products  154 us (11%)
  other arithmetic  123 us (9%)
  local copies, waits for them, and re-layouts  91.4 us (7%)
  between operations  17.6 us (1%)
    ppermute x40, waiting for transfers between devices, line(): return lax.ppermute(value, 'a', pairs)  317 us
    ppermute x9, waiting for transfers between devices, shift(): lax.ppermute(value, axis, [(i, (i + step) % size) for i in range(size)])  219 us
    ppermute x54, waiting for transfers between devices, flip(): lax.ppermute(value, axis, [(i, i ^ mask) for i in range(lax.axis_size(axi...  159 us
    dot_general x26, matrix products, dot(): lax.dot_general(left, right, (((left_dim,), (right_dim,)), ((), ())), pre...  145 us
    ppermute x40, starting transfers between devices, line(): return lax.ppermute(value, 'a', pairs)  100 us
    ppermute x4, waiting for transfers between devices, transpose_blocks(): return lax.ppermute(value, ('a', 'x', 'c'), pairs)  98.3 us
    ppermute x54, starting transfers between devices, flip(): lax.ppermute(value, axis, [(i, i ^ mask) for i in range(lax.axis_size(axi...  38.4 us
    unnamed x311, local copies, waits for them, and re-layouts  34.5 us
  transfers between devices with their start and end apart: 125, of which 60 were waited for; matrix products, arithmetic and copies ran while one was open for 21% of the time, Pallas kernels for 0%

profile of v3, /device:TPU:2, one launch (start us, length us, event | category | flops | bytes accessed | tf_op | source)
XLA Modules:
  0.0 1374.7 jit_solution(10475834576345952066)
XLA Ops:
  22.5 17.5 %collective-permute-done = bf16[256,1024]{1,0:T(8,128)(2,1)S(1)} collective-permute-done((bf16[256,1024]{1,0:T(8,128)(2,1)S(1)}, bf16[256,1024]{1,0:T(8,128)(2,1)S(1)}, u32[]{:S(2)}, u32[]{:S(2)}) %collective-permute-start) | collective-permute-done | bytes 524320 | tf_op jit(solution)/shard_map/ppermute | solution.py:31
  43.8 5.3 collective-permute-done.2
  50.0 9.5 collective-permute-done.6
  64.1 6.0 fusion.49
  80.1 27.2 %collective-permute-done.8 = f32[256,1536]{1,0:T(8,128)S(1)} collective-permute-done((f32[256,1536]{1,0:T(8,128)S(1)}, f32[256,1536]{1,0:T(8,128)S(1)}, u32[]{:S(2)}, u32[]{:S(2)}) %collective-permute-start.8) | collective-permute-done | bytes 1572896 | tf_op jit(solution)/shard_map/ppermute | solution.py:42
  108.6 35.8 %collective-permute-done.10 = bf16[512,1536]{1,0:T(8,128)(2,1)S(1)} collective-permute-done((bf16[512,1536]{1,0:T(8,128)(2,1)S(1)}, bf16[512,1536]{1,0:T(8,128)(2,1)S(1)}, u32[]{:S(2)}, u32[]{:S(2)}) %collective-permute-start.10) | collective-permute-done | bytes 1572896 | tf_op jit(solution)/shard_map/ppermute | solution.py:16
  144.5 30.0 %collective-permute-done.9 = bf16[512,1536]{1,0:T(8,128)(2,1)} collective-permute-done((bf16[512,1536]{1,0:T(8,128)(2,1)}, bf16[512,1536]{1,0:T(8,128)(2,1)}, u32[]{:S(2)}, u32[]{:S(2)}) %collective-permute-start.9) | collective-permute-done | bytes 1572896 | tf_op jit(solution)/shard_map/ppermute | solution.py:16
  177.2 33.2 %collective-permute-done.11 = f32[256,1536]{1,0:T(8,128)S(1)} collective-permute-done((f32[256,1536]{1,0:T(8,128)}, f32[256,1536]{1,0:T(8,128)S(1)}, u32[]{:S(2)}, u32[]{:S(2)}) %collective-permute-start.11) | collective-permute-done | bytes 1572896 | tf_op jit(solution)/shard_map/ppermute | solution.py:42
  214.1 12.4 collective-permute-start.13
  230.0 28.3 %collective-permute-done.13 = f32[256,1536]{1,0:T(8,128)} collective-permute-done((f32[256,1536]{1,0:T(8,128)}, f32[256,1536]{1,0:T(8,128)}, u32[]{:S(2)}, u32[]{:S(2)}) %collective-permute-start.13) | collective-permute-done | bytes 1572896 | tf_op jit(solution)/shard_map/ppermute | solution.py:42
  258.3 5.0 collective-permute-done.14
  291.5 6.8 collective-permute-done.15
  298.3 47.8 %collective-permute-done.16 = bf16[512,768]{1,0:T(8,128)(2,1)} collective-permute-done((bf16[512,768]{1,0:T(8,128)(2,1)}, bf16[512,768]{1,0:T(8,128)(2,1)}, u32[]{:S(2)}, u32[]{:S(2)}) %collective-permute-start.16) | collective-permute-done | bytes 786464 | tf_op jit(solution)/shard_map/ppermute | solution.py:16
  349.9 9.9 collective-permute-done.18
  366.0 7.8 collective-permute-start.25
  373.8 6.1 collective-permute-done.21
  383.4 21.1 %collective-permute-done.25 = bf16[256,1024]{1,0:T(8,128)(2,1)S(1)} collective-permute-done((bf16[256,1024]{1,0:T(8,128)(2,1)}, bf16[256,1024]{1,0:T(8,128)(2,1)S(1)}, u32[]{:S(2)}, u32[]{:S(2)}) %collective-permute-start.25) | collective-permute-done | bytes 524320 | tf_op jit(solution)/shard_map/ppermute | solution.py:31
  421.4 5.2 collective-permute-start.29
  432.6 10.8 collective-permute-done.34
  450.8 10.9 collective-permute-done.32
  467.9 8.6 collective-permute-done.37
  478.4 9.4 collective-permute-done.42
  494.4 14.8 %collective-permute-done.24 = f32[256,1024]{1,0:T(8,128)S(1)} collective-permute-done((f32[256,1024]{1,0:T(8,128)S(1)}, f32[256,1024]{1,0:T(8,128)S(1)}, u32[]{:S(2)}, u32[]{:S(2)}) %collective-permute-start.24) | collective-permute-done | bytes 1048608 | tf_op jit(solution)/shard_map/ppermute | solution.py:20
  511.1 13.1 collective-permute-done.26
  530.5 29.6 %collective-permute-done.28 = bf16[512,1536]{1,0:T(8,128)(2,1)} collective-permute-done((bf16[512,1536]{1,0:T(8,128)(2,1)}, bf16[512,1536]{1,0:T(8,128)(2,1)}, u32[]{:S(2)}, u32[]{:S(2)}) %collective-permute-start.28) | collective-permute-done | bytes 1572896 | tf_op jit(solution)/shard_map/ppermute | solution.py:16
  561.6 5.8 collective-permute-start.49
  591.5 5.5 collective-permute-done.52
  602.3 10.0 collective-permute-done.50
  613.7 9.5 collective-permute-done.54
  626.0 5.4 fusion.94
  631.4 6.2 collective-permute-done.57
  637.9 5.3 fusion.95
  643.4 5.3 fusion.96
  648.8 11.2 add_add_fusion
  662.7 5.3 fusion.97
  672.3 5.3 multiply_convert_fusion.2
  684.5 5.4 fusion.75
  705.9 7.6 collective-permute-start.62
  717.0 29.9 %collective-permute-done.62 = bf16[1024,768]{1,0:T(8,128)(2,1)} collective-permute-done((bf16[1024,768]{1,0:T(8,128)(2,1)S(1)}, bf16[1024,768]{1,0:T(8,128)(2,1)}, u32[]{:S(2)}, u32[]{:S(2)}) %collective-permute-start.62) | collective-permute-done | bytes 1572896 | tf_op jit(solution)/shard_map/ppermute | solution.py:42
  746.9 5.4 collective-permute-done.63
  759.2 6.3 fusion.98
  771.0 8.7 collective-permute-done.64
  781.1 46.0 %collective-permute-done.69 = bf16[1024,768]{1,0:T(8,128)(2,1)} collective-permute-done((bf16[1024,768]{1,0:T(8,128)(2,1)}, bf16[1024,768]{1,0:T(8,128)(2,1)}, u32[]{:S(2)}, u32[]{:S(2)}) %collective-permute-start.69) | collective-permute-done | bytes 1572896 | tf_op jit(solution)/shard_map/ppermute | solution.py:42
  831.6 18.8 %collective-permute-done.72 = f32[256,1024]{1,0:T(8,128)S(1)} collective-permute-done((f32[256,1024]{1,0:T(8,128)S(1)}, f32[256,1024]{1,0:T(8,128)S(1)}, u32[]{:S(2)}, u32[]{:S(2)}) %collective-permute-start.72) | collective-permute-done | bytes 1048608 | tf_op jit(solution)/shard_map/ppermute | solution.py:42
  858.4 5.1 convolution_convert_fusion.2
  871.3 6.7 collective-permute-done.73
  880.4 5.7 collective-permute-start.75
  887.4 6.2 convolution_convert_fusion.3
  893.7 7.7 convolution_convert_fusion.4
  917.0 5.4 collective-permute-done.78
  924.1 7.9 collective-permute-done.79
  933.1 21.3 %reduce-scatter.10.cloned.1.call-done = bf16[512,1536]{1,0:T(8,128)(2,1)} async-done(((bf16[1024,1536]{1,0:T(8,128)(2,1)}), bf16[512,1536]{1,0:T(8,128)(2,1)}) %reduce-scatter.10.cloned.1.call-update) | async-done | bytes 1572880 | tf_op jit(solution)/shard_map/reduce_scatter | solution.py:225
  964.0 27.7 %collective-permute-done.81 = bf16[512,1536]{1,0:T(8,128)(2,1)S(1)} collective-permute-done((bf16[512,1536]{1,0:T(8,128)(2,1)}, bf16[512,1536]{1,0:T(8,128)(2,1)S(1)}, u32[]{:S(2)}, u32[]{:S(2)}) %collective-permute-start.81) | collective-permute-done | bytes 1572896 | tf_op jit(solution)/shard_map/ppermute | solution.py:16
  994.4 21.6 %collective-permute-done.82 = f32[256,1024]{1,0:T(8,128)S(1)} collective-permute-done((f32[256,1024]{1,0:T(8,128)S(1)}, f32[256,1024]{1,0:T(8,128)S(1)}, u32[]{:S(2)}, u32[]{:S(2)}) %collective-permute-start.82) | collective-permute-done | bytes 1048608 | tf_op jit(solution)/shard_map/ppermute | solution.py:42
  1021.6 20.0 %collective-permute-done.83 = f32[256,1024]{1,0:T(8,128)S(1)} collective-permute-done((f32[256,1024]{1,0:T(8,128)S(1)}, f32[256,1024]{1,0:T(8,128)S(1)}, u32[]{:S(2)}, u32[]{:S(2)}) %collective-permute-start.83) | collective-permute-done | bytes 1048608 | tf_op jit(solution)/shard_map/ppermute | solution.py:42
  1043.3 8.6 collective-permute-start.85
  1059.2 12.8 collective-permute-done.85
  1141.6 12.1 fusion.18
  1160.4 9.4 convolution_convert_fusion
  1178.7 7.4 convolution_convert_fusion.1
  1186.7 6.3 fusion.100
  1208.7 18.5 %collective-permute-done.99 = f32[256,1024]{1,0:T(8,128)S(1)} collective-permute-done((f32[256,1024]{1,0:T(8,128)}, f32[256,1024]{1,0:T(8,128)S(1)}, u32[]{:S(2)}, u32[]{:S(2)}) %collective-permute-start.99) | collective-permute-done | bytes 1048608 | tf_op jit(solution)/shard_map/ppermute | solution.py:20
  1228.7 41.5 %collective-permute-done.100 = bf16[512,1536]{1,0:T(8,128)(2,1)} collective-permute-done((bf16[512,1536]{1,0:T(8,128)(2,1)}, bf16[512,1536]{1,0:T(8,128)(2,1)}, u32[]{:S(2)}, u32[]{:S(2)}) %collective-permute-start.100) | collective-permute-done | bytes 1572896 | tf_op jit(solution)/shard_map/ppermute | solution.py:16
  1294.0 59.8 %collective-permute-done.97 = bf16[256,1024]{1,0:T(8,128)(2,1)S(1)} collective-permute-done((bf16[256,1024]{1,0:T(8,128)(2,1)S(1)}, bf16[256,1024]{1,0:T(8,128)(2,1)S(1)}, u32[]{:S(2)}, u32[]{:S(2)}) %collective-permute-start.97) | collective-permute-done | bytes 524320 | tf_op jit(solution)/shard_map/ppermute | solution.py:31
  (736 shorter events, 430.5 us)
Async XLA Ops:
  7.2 56.9 %all-gather.12.cloned.1.call-start = ((), (), s32[]{:S(2)}) async-start(), calls=%async_computation.7 | async-start | bytes 4718592 | tf_op jit(solution)/shard_map/all_gather | solution.py:194
  10.6 280.8 %all-gather.14.cloned.1.call-start = ((), (), s32[]{:S(2)}) async-start(), calls=%async_computation.8 | async-start | bytes 4718592 | tf_op jit(solution)/shard_map/all_gather | solution.py:194
  10.7 29.3 %collective-permute-start = (bf16[256,1024]{1,0:T(8,128)(2,1)S(1)}, bf16[256,1024]{1,0:T(8,128)(2,1)S(1)}, u32[]{:S(2)}, u32[]{:S(2)}) collective-permute-start(bf16[256,1024]{1,0:T(8,128)(2,1)S(1)} %copy-done.146), channel_id=1, source_target_pairs={{0,0},{1,8},{2,16},{3,24},{8,1},{9,9},{10,17},{11,25},{16,2},{17,1... | collective-permute-start | bytes 1572872 | tf_op jit(solution)/shard_map/ppermute | solution.py:31
  63.3 228.1 %all-gather.16.cloned.1.call-start = ((), (), s32[]{:S(2)}) async-start(), calls=%async_computation.9 | async-start | bytes 4718592 | tf_op jit(solution)/shard_map/all_gather | solution.py:194
  70.4 36.9 %collective-permute-start.8 = (f32[256,1536]{1,0:T(8,128)S(1)}, f32[256,1536]{1,0:T(8,128)S(1)}, u32[]{:S(2)}, u32[]{:S(2)}) collective-permute-start(f32[256,1536]{1,0:T(8,128)S(1)} %slice_select_fusion), channel_id=1, source_target_pairs={{0,8},{24,16},{1,9},{25,17},{2,10},{26,18},{3,11},{27,19},{4,12},{... | collective-permute-start | bytes 4718600 | tf_op jit(solution)/shard_map/ppermute | solution.py:42
  75.0 69.5 %collective-permute-start.10 = (bf16[512,1536]{1,0:T(8,128)(2,1)S(1)}, bf16[512,1536]{1,0:T(8,128)(2,1)S(1)}, u32[]{:S(2)}, u32[]{:S(2)}) collective-permute-start(bf16[512,1536]{1,0:T(8,128)(2,1)S(1)} %pad_maximum_fusion.19), channel_id=1, source_target_pairs={{0,8},{8,16},{16,24},{24,0},{1,9},{9,17},{17,25},{25,1},{2,10},{10... | collective-permute-start | bytes 4718600 | tf_op jit(solution)/shard_map/ppermute | solution.py:16
  76.3 98.1 %collective-permute-start.9 = (bf16[512,1536]{1,0:T(8,128)(2,1)}, bf16[512,1536]{1,0:T(8,128)(2,1)}, u32[]{:S(2)}, u32[]{:S(2)}) collective-permute-start(bf16[512,1536]{1,0:T(8,128)(2,1)} %pad_maximum_fusion.18), channel_id=1, source_target_pairs={{0,24},{8,0},{16,8},{24,16},{1,25},{9,1},{17,9},{25,17},{2,26},{10... | collective-permute-start | bytes 4718600 | tf_op jit(solution)/shard_map/ppermute | solution.py:16
  174.4 117.1 %all-gather.18.cloned.1.call-start = ((), (), s32[]{:S(2)}) async-start(), calls=%async_computation.10 | async-start | bytes 4718592 | tf_op jit(solution)/shard_map/all_gather | solution.py:194
  175.0 238.3 %all-gather.20.cloned.1.call-start = ((), (), s32[]{:S(2)}) async-start(), calls=%async_computation.11 | async-start | bytes 3145728 | tf_op jit(solution)/shard_map/all_gather | solution.py:194
  175.1 35.4 %collective-permute-start.11 = (f32[256,1536]{1,0:T(8,128)}, f32[256,1536]{1,0:T(8,128)S(1)}, u32[]{:S(2)}, u32[]{:S(2)}) collective-permute-start(f32[256,1536]{1,0:T(8,128)} %slice_add_fusion), channel_id=1, source_target_pairs={{0,8},{8,16},{1,9},{9,17},{2,10},{10,18},{3,11},{11,19},{4,12},{12... | collective-permute-start | bytes 4718600 | tf_op jit(solution)/shard_map/ppermute | solution.py:42
  176.5 34.0 %collective-permute-start.12 = (f32[256,1536]{1,0:T(8,128)}, f32[256,1536]{1,0:T(8,128)S(1)}, u32[]{:S(2)}, u32[]{:S(2)}) collective-permute-start(f32[256,1536]{1,0:T(8,128)} %slice_add_fusion), channel_id=1, source_target_pairs={{24,16},{16,8},{25,17},{17,9},{26,18},{18,10},{27,19},{19,11},{28,... | collective-permute-start | bytes 4718600 | tf_op jit(solution)/shard_map/ppermute | solution.py:42
  214.1 44.2 %collective-permute-start.13 = (f32[256,1536]{1,0:T(8,128)}, f32[256,1536]{1,0:T(8,128)}, u32[]{:S(2)}, u32[]{:S(2)}) collective-permute-start(f32[256,1536]{1,0:T(8,128)} %get-tuple-element.99), channel_id=1, source_target_pairs={{0,8},{8,16},{16,24},{1,9},{9,17},{17,25},{2,10},{10,18},{18,26},{... | collective-permute-start | bytes 4718600 | tf_op jit(solution)/shard_map/ppermute | solution.py:42
  226.5 36.9 %collective-permute-start.14 = (f32[256,1536]{1,0:T(8,128)S(1)}, f32[256,1536]{1,0:T(8,128)}, u32[]{:S(2)}, u32[]{:S(2)}) collective-permute-start(f32[256,1536]{1,0:T(8,128)S(1)} %get-tuple-element.100), channel_id=1, source_target_pairs={{24,16},{16,8},{8,0},{25,17},{17,9},{9,1},{26,18},{18,10},{10,2},{... | collective-permute-start | bytes 4718600 | tf_op jit(solution)/shard_map/ppermute | solution.py:42
  227.8 302.7 %all-gather.22.cloned.1.call-start = ((), (), s32[]{:S(2)}) async-start(), calls=%async_computation.12 | async-start | bytes 2359296 | tf_op jit(solution)/shard_map/all_gather | solution.py:194
  279.3 66.8 %collective-permute-start.16 = (bf16[512,768]{1,0:T(8,128)(2,1)}, bf16[512,768]{1,0:T(8,128)(2,1)}, u32[]{:S(2)}, u32[]{:S(2)}) collective-permute-start(bf16[512,768]{1,0:T(8,128)(2,1)} %get-tuple-element.224), channel_id=1, source_target_pairs={{0,16},{8,24},{16,0},{24,8},{1,17},{9,25},{17,1},{25,9},{2,18},{10... | collective-permute-start | bytes 2359304 | tf_op jit(solution)/shard_map/ppermute | solution.py:16
  280.2 66.0 %collective-permute-start.17 = (bf16[512,768]{1,0:T(8,128)(2,1)}, bf16[512,768]{1,0:T(8,128)(2,1)}, u32[]{:S(2)}, u32[]{:S(2)}) collective-permute-start(bf16[512,768]{1,0:T(8,128)(2,1)} %get-tuple-element.223), channel_id=1, source_target_pairs={{0,8},{8,16},{16,24},{24,0},{1,9},{9,17},{17,25},{25,1},{2,10},{10... | collective-permute-start | bytes 2359304 | tf_op jit(solution)/shard_map/ppermute | solution.py:16
  346.1 184.4 %all-gather.24.cloned.1.call-start = ((), (), s32[]{:S(2)}) async-start(), calls=%async_computation.13 | async-start | bytes 2359296 | tf_op jit(solution)/shard_map/all_gather | solution.py:194
  349.9 180.6 %all-gather.26.cloned.1.call-start = ((), (), s32[]{:S(2)}) async-start(), calls=%async_computation.14 | async-start | bytes 2359296 | tf_op jit(solution)/shard_map/all_gather | solution.py:194
  366.0 38.4 %collective-permute-start.25 = (bf16[256,1024]{1,0:T(8,128)(2,1)}, bf16[256,1024]{1,0:T(8,128)(2,1)S(1)}, u32[]{:S(2)}, u32[]{:S(2)}) collective-permute-start(bf16[256,1024]{1,0:T(8,128)(2,1)} %param.27), channel_id=1, source_target_pairs={{0,0},{1,8},{2,16},{3,24},{8,1},{9,9},{10,17},{11,25},{16,2},{17,1... | collective-permute-start | bytes 1572872 | tf_op jit(solution)/shard_map/ppermute | solution.py:31
  382.0 28.4 %collective-permute-start.22 = (bf16[256,1024]{1,0:T(8,128)(2,1)}, bf16[256,1024]{1,0:T(8,128)(2,1)}, u32[]{:S(2)}, u32[]{:S(2)}) collective-permute-start(bf16[256,1024]{1,0:T(8,128)(2,1)} %get-tuple-element.258), channel_id=1, source_target_pairs={{16,24},{8,0},{17,25},{9,1},{18,26},{10,2},{19,27},{11,3},{20,28},... | collective-permute-start | bytes 1572872 | tf_op jit(solution)/shard_map/ppermute | solution.py:42
  383.3 147.2 %all-gather.28.cloned.1.call-start = ((), (), s32[]{:S(2)}) async-start(), calls=%async_computation.15 | async-start | bytes 2359296 | tf_op jit(solution)/shard_map/all_gather | solution.py:194
  421.3 45.1 %collective-permute-start.23 = (f32[2,256,1024]{2,1,0:T(8,128)}, f32[2,256,1024]{2,1,0:T(8,128)}, u32[]{:S(2)}, u32[]{:S(2)}) collective-permute-start(f32[2,256,1024]{2,1,0:T(8,128)} %pad_maximum_fusion.7), channel_id=1, source_target_pairs={{0,1},{1,0},{2,3},{3,2},{4,5},{5,4},{6,7},{7,6},{8,9},{9,8},{10,11... | collective-permute-start | bytes 6291464 | tf_op jit(solution)/shard_map/ppermute | solution.py:20
  421.4 227.3 %all-gather.30.cloned.1.call-start = ((), (), s32[]{:S(2)}) async-start(), calls=%async_computation.16 | async-start | bytes 4718592 | tf_op jit(solution)/shard_map/all_gather | solution.py:194
  446.6 41.3 %collective-permute-start.30 = (bf16[512,1024]{1,0:T(8,128)(2,1)S(1)}, bf16[512,1024]{1,0:T(8,128)(2,1)S(1)}, u32[]{:S(2)}, u32[]{:S(2)}) collective-permute-start(bf16[512,1024]{1,0:T(8,128)(2,1)S(1)} %pad_maximum_fusion.25), channel_id=1, source_target_pairs={{0,1},{1,0},{2,3},{3,2},{4,5},{5,4},{6,7},{7,6},{8,9},{9,8},{10,11... | collective-permute-start | bytes 3145736 | tf_op jit(solution)/shard_map/ppermute | solution.py:20
  450.7 38.9 %collective-permute-start.40 = (bf16[512,1024]{1,0:T(8,128)(2,1)S(1)}, bf16[512,1024]{1,0:T(8,128)(2,1)S(1)}, u32[]{:S(2)}, u32[]{:S(2)}) collective-permute-start(bf16[512,1024]{1,0:T(8,128)(2,1)S(1)} %pad_maximum_fusion.28), channel_id=1, source_target_pairs={{0,1},{1,0},{2,3},{3,2},{4,5},{5,4},{6,7},{7,6},{8,9},{9,8},{10,11... | collective-permute-start | bytes 3145736 | tf_op jit(solution)/shard_map/ppermute | solution.py:20
  466.4 26.4 %collective-permute-start.33 = (bf16[512,1024]{1,0:T(8,128)(2,1)S(1)}, bf16[512,1024]{1,0:T(8,128)(2,1)S(1)}, u32[]{:S(2)}, u32[]{:S(2)}) collective-permute-start(bf16[512,1024]{1,0:T(8,128)(2,1)S(1)} %pad_maximum_fusion.26), channel_id=1, source_target_pairs={{0,1},{1,0},{2,3},{3,2},{4,5},{5,4},{6,7},{7,6},{8,9},{9,8},{10,11... | collective-permute-start | bytes 3145736 | tf_op jit(solution)/shard_map/ppermute | solution.py:20
  476.5 32.7 %collective-permute-start.24 = (f32[256,1024]{1,0:T(8,128)S(1)}, f32[256,1024]{1,0:T(8,128)S(1)}, u32[]{:S(2)}, u32[]{:S(2)}) collective-permute-start(f32[256,1024]{1,0:T(8,128)S(1)} %fusion.42), channel_id=1, source_target_pairs={{0,2},{2,0},{1,3},{3,1},{4,6},{6,4},{5,7},{7,5},{8,10},{10,8},{9,1... | collective-permute-start | bytes 3145736 | tf_op jit(solution)/shard_map/ppermute | solution.py:20
  487.8 38.1 %collective-permute-start.43 = (bf16[512,1024]{1,0:T(8,128)(2,1)S(1)}, bf16[512,1024]{1,0:T(8,128)(2,1)S(1)}, u32[]{:S(2)}, u32[]{:S(2)}) collective-permute-start(bf16[512,1024]{1,0:T(8,128)(2,1)S(1)} %pad_maximum_fusion.29), channel_id=1, source_target_pairs={{0,1},{1,0},{2,3},{3,2},{4,5},{5,4},{6,7},{7,6},{8,9},{9,8},{10,11... | collective-permute-start | bytes 3145736 | tf_op jit(solution)/shard_map/ppermute | solution.py:20
  489.7 70.4 %collective-permute-start.28 = (bf16[512,1536]{1,0:T(8,128)(2,1)}, bf16[512,1536]{1,0:T(8,128)(2,1)}, u32[]{:S(2)}, u32[]{:S(2)}) collective-permute-start(bf16[512,1536]{1,0:T(8,128)(2,1)} %pad_maximum_fusion.21), channel_id=1, source_target_pairs={{0,16},{8,24},{16,0},{24,8},{1,17},{9,25},{17,1},{25,9},{2,18},{10... | collective-permute-start | bytes 4718600 | tf_op jit(solution)/shard_map/ppermute | solution.py:16
  584.7 171.7 %reduce-scatter.8.cloned.1.call-start = ((), (), s32[]{:S(2)}) async-start(), calls=%async_computation.17 | async-start | bytes 4718592 | tf_op jit(solution)/shard_map/reduce_scatter | solution.py:225
  586.1 37.6 %collective-permute-start.45 = (bf16[512,1024]{1,0:T(8,128)(2,1)S(1)}, bf16[512,1024]{1,0:T(8,128)(2,1)S(1)}, u32[]{:S(2)}, u32[]{:S(2)}) collective-permute-start(bf16[512,1024]{1,0:T(8,128)(2,1)S(1)} %pad_maximum_fusion.30), channel_id=1, source_target_pairs={{0,1},{1,0},{2,3},{3,2},{4,5},{5,4},{6,7},{7,6},{8,9},{9,8},{10,11... | collective-permute-start | bytes 3145736 | tf_op jit(solution)/shard_map/ppermute | solution.py:20
  586.5 25.9 %collective-permute-start.50 = (bf16[256,1024]{1,0:T(8,128)(2,1)}, bf16[256,1024]{1,0:T(8,128)(2,1)S(1)}, u32[]{:S(2)}, u32[]{:S(2)}) collective-permute-start(bf16[256,1024]{1,0:T(8,128)(2,1)} %collective-permute-done.49), channel_id=1, source_target_pairs={{0,2},{2,0},{1,3},{3,1},{4,6},{6,4},{5,7},{7,5},{8,10},{10,8},{9,1... | collective-permute-start | bytes 1572872 | tf_op jit(solution)/shard_map/ppermute | solution.py:20
  597.1 26.3 %collective-permute-start.56 = (bf16[256,1024]{1,0:T(8,128)(2,1)S(1)}, bf16[256,1024]{1,0:T(8,128)(2,1)S(1)}, u32[]{:S(2)}, u32[]{:S(2)}) collective-permute-start(bf16[256,1024]{1,0:T(8,128)(2,1)S(1)} %get-tuple-element.253), channel_id=1, source_target_pairs={{16,24},{8,0},{17,25},{9,1},{18,26},{10,2},{19,27},{11,3},{20,28},... | collective-permute-start | bytes 1572872 | tf_op jit(solution)/shard_map/ppermute | solution.py:42
  602.3 35.6 %collective-permute-start.48 = (bf16[512,1024]{1,0:T(8,128)(2,1)S(1)}, bf16[512,1024]{1,0:T(8,128)(2,1)S(1)}, u32[]{:S(2)}, u32[]{:S(2)}) collective-permute-start(bf16[512,1024]{1,0:T(8,128)(2,1)S(1)} %pad_maximum_fusion.31), channel_id=1, source_target_pairs={{0,1},{1,0},{2,3},{3,2},{4,5},{5,4},{6,7},{7,6},{8,9},{9,8},{10,11... | collective-permute-start | bytes 3145736 | tf_op jit(solution)/shard_map/ppermute | solution.py:20
  613.5 29.8 %collective-permute-start.51 = (bf16[512,1024]{1,0:T(8,128)(2,1)S(1)}, bf16[512,1024]{1,0:T(8,128)(2,1)S(1)}, u32[]{:S(2)}, u32[]{:S(2)}) collective-permute-start(bf16[512,1024]{1,0:T(8,128)(2,1)S(1)} %pad_maximum_fusion.32), channel_id=1, source_target_pairs={{0,1},{1,0},{2,3},{3,2},{4,5},{5,4},{6,7},{7,6},{8,9},{9,8},{10,11... | collective-permute-start | bytes 3145736 | tf_op jit(solution)/shard_map/ppermute | solution.py:20
  623.2 25.4 %collective-permute-start.55 = (bf16[512,1024]{1,0:T(8,128)(2,1)S(1)}, bf16[512,1024]{1,0:T(8,128)(2,1)}, u32[]{:S(2)}, u32[]{:S(2)}) collective-permute-start(bf16[512,1024]{1,0:T(8,128)(2,1)S(1)} %pad_maximum_fusion.33), channel_id=1, source_target_pairs={{0,1},{1,0},{2,3},{3,2},{4,5},{5,4},{6,7},{7,6},{8,9},{9,8},{10,11... | collective-permute-start | bytes 3145736 | tf_op jit(solution)/shard_map/ppermute | solution.py:20
  694.9 259.5 %reduce-scatter.10.cloned.1.call-start = ((), (), s32[]{:S(2)}) async-start(), calls=%async_computation.18 | async-start | bytes 4718592 | tf_op jit(solution)/shard_map/reduce_scatter | solution.py:225
  704.7 51.7 %collective-permute-start.70 = (f32[2,256,1024]{2,1,0:T(8,128)S(1)}, f32[2,256,1024]{2,1,0:T(8,128)}, u32[]{:S(2)}, u32[]{:S(2)}) collective-permute-start(f32[2,256,1024]{2,1,0:T(8,128)S(1)} %bitcast.303), channel_id=1, source_target_pairs={{0,1},{1,0},{2,3},{3,2},{4,5},{5,4},{6,7},{7,6},{8,9},{9,8},{10,11... | collective-permute-start | bytes 6291464 | tf_op jit(solution)/shard_map/ppermute | solution.py:20
  705.9 41.0 %collective-permute-start.62 = (bf16[1024,768]{1,0:T(8,128)(2,1)S(1)}, bf16[1024,768]{1,0:T(8,128)(2,1)}, u32[]{:S(2)}, u32[]{:S(2)}) collective-permute-start(bf16[1024,768]{1,0:T(8,128)(2,1)S(1)} %copy-done.143), channel_id=1, source_target_pairs={{0,8},{8,16},{16,24},{1,9},{9,17},{17,25},{2,10},{10,18},{18,26},{... | collective-permute-start | bytes 4718600 | tf_op jit(solution)/shard_map/ppermute | solution.py:42
  713.5 38.8 %collective-permute-start.63 = (bf16[1024,768]{1,0:T(8,128)(2,1)S(1)}, bf16[1024,768]{1,0:T(8,128)(2,1)}, u32[]{:S(2)}, u32[]{:S(2)}) collective-permute-start(bf16[1024,768]{1,0:T(8,128)(2,1)S(1)} %copy-done.143), channel_id=1, source_target_pairs={{24,16},{16,8},{8,0},{25,17},{17,9},{9,1},{26,18},{18,10},{10,2},{... | collective-permute-start | bytes 4718600 | tf_op jit(solution)/shard_map/ppermute | solution.py:42
  716.4 51.2 %collective-permute-start.66 = (f32[256,1024]{1,0:T(8,128)}, f32[256,1024]{1,0:T(8,128)}, u32[]{:S(2)}, u32[]{:S(2)}) collective-permute-start(f32[256,1024]{1,0:T(8,128)} %slice_bitcast_fusion.6), channel_id=1, source_target_pairs={{0,2},{2,0},{1,3},{3,1},{4,6},{6,4},{5,7},{7,5},{8,10},{10,8},{9,1... | collective-permute-start | bytes 3145736 | tf_op jit(solution)/shard_map/ppermute | solution.py:20
  753.3 26.4 %collective-permute-start.64 = (f32[256,1024]{1,0:T(8,128)}, f32[256,1024]{1,0:T(8,128)}, u32[]{:S(2)}, u32[]{:S(2)}) collective-permute-start(f32[256,1024]{1,0:T(8,128)} %slice_bitcast_fusion.12), channel_id=1, source_target_pairs={{0,2},{2,0},{1,3},{3,1},{4,6},{6,4},{5,7},{7,5},{8,10},{10,8},{9,1... | collective-permute-start | bytes 3145736 | tf_op jit(solution)/shard_map/ppermute | solution.py:20
  753.4 27.7 %collective-permute-start.68 = (bf16[1024,768]{1,0:T(8,128)(2,1)}, bf16[1024,768]{1,0:T(8,128)(2,1)}, u32[]{:S(2)}, u32[]{:S(2)}) collective-permute-start(bf16[1024,768]{1,0:T(8,128)(2,1)} %collective-permute-done.62), channel_id=1, source_target_pairs={{8,16},{16,24},{9,17},{17,25},{10,18},{18,26},{11,19},{19,27},{12,... | collective-permute-start | bytes 4718600 | tf_op jit(solution)/shard_map/ppermute | solution.py:42
  755.2 71.9 %collective-permute-start.69 = (bf16[1024,768]{1,0:T(8,128)(2,1)}, bf16[1024,768]{1,0:T(8,128)(2,1)}, u32[]{:S(2)}, u32[]{:S(2)}) collective-permute-start(bf16[1024,768]{1,0:T(8,128)(2,1)} %collective-permute-done.63), channel_id=1, source_target_pairs={{16,8},{8,0},{17,9},{9,1},{18,10},{10,2},{19,11},{11,3},{20,12},{1... | collective-permute-start | bytes 4718600 | tf_op jit(solution)/shard_map/ppermute | solution.py:42
  756.5 70.6 %collective-permute-start.67 = (bf16[512,1536]{1,0:T(8,128)(2,1)}, bf16[512,1536]{1,0:T(8,128)(2,1)S(1)}, u32[]{:S(2)}, u32[]{:S(2)}) collective-permute-start(bf16[512,1536]{1,0:T(8,128)(2,1)} %reduce-scatter.8.cloned.1.call-done), channel_id=1, source_target_pairs={{0,8},{8,16},{16,24},{24,0},{1,9},{9,17},{17,25},{25,1},{2,10},{10... | collective-permute-start | bytes 4718600 | tf_op jit(solution)/shard_map/ppermute | solution.py:16
  767.6 64.0 %collective-permute-start.71 = (f32[256,1024]{1,0:T(8,128)S(1)}, f32[256,1024]{1,0:T(8,128)S(1)}, u32[]{:S(2)}, u32[]{:S(2)}) collective-permute-start(f32[256,1024]{1,0:T(8,128)S(1)} %slice_bitcast_fusion.4), channel_id=1, source_target_pairs={{0,2},{2,0},{1,3},{3,1},{4,6},{6,4},{5,7},{7,5},{8,10},{10,8},{9,1... | collective-permute-start | bytes 3145736 | tf_op jit(solution)/shard_map/ppermute | solution.py:20
  831.6 31.9 %collective-permute-start.59 = (f32[2,256,1024]{2,1,0:T(8,128)}, f32[2,256,1024]{2,1,0:T(8,128)}, u32[]{:S(2)}, u32[]{:S(2)}) collective-permute-start(f32[2,256,1024]{2,1,0:T(8,128)} %bitcast.30), channel_id=1, source_target_pairs={{0,1},{1,0},{2,3},{3,2},{4,5},{5,4},{6,7},{7,6},{8,9},{9,8},{10,11... | collective-permute-start | bytes 6291464 | tf_op jit(solution)/shard_map/ppermute | solution.py:20
  867.3 34.1 %collective-permute-start.60 = (f32[256,1024]{1,0:T(8,128)}, f32[256,1024]{1,0:T(8,128)}, u32[]{:S(2)}, u32[]{:S(2)}) collective-permute-start(f32[256,1024]{1,0:T(8,128)} %slice_bitcast_fusion.8), channel_id=1, source_target_pairs={{0,2},{2,0},{1,3},{3,1},{4,6},{6,4},{5,7},{7,5},{8,10},{10,8},{9,1... | collective-permute-start | bytes 3145736 | tf_op jit(solution)/shard_map/ppermute | solution.py:20
  880.4 25.4 %collective-permute-start.75 = (f32[256,1024]{1,0:T(8,128)}, f32[256,1024]{1,0:T(8,128)S(1)}, u32[]{:S(2)}, u32[]{:S(2)}) collective-permute-start(f32[256,1024]{1,0:T(8,128)} %add.557), channel_id=1, source_target_pairs={{0,8},{8,16},{16,24},{1,9},{9,17},{17,25},{2,10},{10,18},{18,26},{... | collective-permute-start | bytes 3145736 | tf_op jit(solution)/shard_map/ppermute | solution.py:42
  912.2 166.1 %reduce-scatter.12.cloned.1.call-start = ((), (), s32[]{:S(2)}) async-start(), calls=%async_computation.19 | async-start | bytes 4718592 | tf_op jit(solution)/shard_map/reduce_scatter | solution.py:225
  913.0 165.3 %reduce-scatter.14.cloned.1.call-start = ((), (), s32[]{:S(2)}) async-start(), calls=%async_computation.20 | async-start | bytes 4718592 | tf_op jit(solution)/shard_map/reduce_scatter | solution.py:225
  924.1 217.5 %all-gather.32.cloned.1.call-start = ((), (), s32[]{:S(2)}) async-start(), calls=%async_computation.21 | async-start | bytes 9437184 | tf_op jit(solution)/shard_map/all_gather | solution.py:194
  954.4 37.3 %collective-permute-start.81 = (bf16[512,1536]{1,0:T(8,128)(2,1)}, bf16[512,1536]{1,0:T(8,128)(2,1)S(1)}, u32[]{:S(2)}, u32[]{:S(2)}) collective-permute-start(bf16[512,1536]{1,0:T(8,128)(2,1)} %reduce-scatter.10.cloned.1.call-done), channel_id=1, source_target_pairs={{0,24},{8,0},{16,8},{24,16},{1,25},{9,1},{17,9},{25,17},{2,26},{10... | collective-permute-start | bytes 4718600 | tf_op jit(solution)/shard_map/ppermute | solution.py:16
  1016.1 25.5 %collective-permute-start.83 = (f32[256,1024]{1,0:T(8,128)S(1)}, f32[256,1024]{1,0:T(8,128)S(1)}, u32[]{:S(2)}, u32[]{:S(2)}) collective-permute-start(f32[256,1024]{1,0:T(8,128)S(1)} %slice_add_fusion.4), channel_id=1, source_target_pairs={{0,8},{8,16},{1,9},{9,17},{2,10},{10,18},{3,11},{11,19},{4,12},{12... | collective-permute-start | bytes 3145736 | tf_op jit(solution)/shard_map/ppermute | solution.py:42
  1043.3 28.7 %collective-permute-start.85 = (f32[256,1024]{1,0:T(8,128)}, f32[256,1024]{1,0:T(8,128)S(1)}, u32[]{:S(2)}, u32[]{:S(2)}) collective-permute-start(f32[256,1024]{1,0:T(8,128)} %get-tuple-element.149), channel_id=1, source_target_pairs={{0,8},{8,16},{16,24},{1,9},{9,17},{17,25},{2,10},{10,18},{18,26},{... | collective-permute-start | bytes 3145736 | tf_op jit(solution)/shard_map/ppermute | solution.py:42
  1055.5 298.3 %reduce-scatter.18.cloned.1.call-start = ((), (), s32[]{:S(2)}) async-start(), calls=%async_computation.23 | async-start | bytes 3145728 | tf_op jit(solution)/shard_map/reduce_scatter | solution.py:225
  1082.1 37.7 %collective-permute-start.87 = (bf16[1024,768]{1,0:T(8,128)(2,1)}, bf16[1024,768]{1,0:T(8,128)(2,1)}, u32[]{:S(2)}, u32[]{:S(2)}) collective-permute-start(bf16[1024,768]{1,0:T(8,128)(2,1)} %get-tuple-element.222), channel_id=1, source_target_pairs={{16,24},{8,0},{17,25},{9,1},{18,26},{10,2},{19,27},{11,3},{20,28},... | collective-permute-start | bytes 4718600 | tf_op jit(solution)/shard_map/ppermute | solution.py:42
  1177.6 179.2 %reduce-scatter.16.cloned.1.call-start = ((), (), s32[]{:S(2)}) async-start(), calls=%async_computation.22 | async-start | bytes 4718592 | tf_op jit(solution)/shard_map/reduce_scatter | solution.py:225
  1186.1 174.6 %reduce-scatter.20.cloned.1.call-start = ((), (), s32[]{:S(2)}) async-start(), calls=%async_computation.24 | async-start | bytes 9437184 | tf_op jit(solution)/shard_map/reduce_scatter | solution.py:225
  1199.3 70.9 %collective-permute-start.100 = (bf16[512,1536]{1,0:T(8,128)(2,1)}, bf16[512,1536]{1,0:T(8,128)(2,1)}, u32[]{:S(2)}, u32[]{:S(2)}) collective-permute-start(bf16[512,1536]{1,0:T(8,128)(2,1)} %reduce-scatter.12.cloned.1.call-done), channel_id=1, source_target_pairs={{0,16},{8,24},{16,0},{24,8},{1,17},{9,25},{17,1},{25,9},{2,18},{10... | collective-permute-start | bytes 4718600 | tf_op jit(solution)/shard_map/ppermute | solution.py:16
  1201.0 26.2 %collective-permute-start.99 = (f32[256,1024]{1,0:T(8,128)}, f32[256,1024]{1,0:T(8,128)S(1)}, u32[]{:S(2)}, u32[]{:S(2)}) collective-permute-start(f32[256,1024]{1,0:T(8,128)} %fusion.30), channel_id=1, source_target_pairs={{0,2},{2,0},{1,3},{3,1},{4,6},{6,4},{5,7},{7,5},{8,10},{10,8},{9,1... | collective-permute-start | bytes 3145736 | tf_op jit(solution)/shard_map/ppermute | solution.py:20
  1207.2 73.2 %collective-permute-start.96 = (f32[256,1024]{1,0:T(8,128)S(1)}, f32[256,1024]{1,0:T(8,128)S(1)}, u32[]{:S(2)}, u32[]{:S(2)}) collective-permute-start(f32[256,1024]{1,0:T(8,128)S(1)} %slice_bitcast_fusion.2), channel_id=1, source_target_pairs={{0,2},{2,0},{1,3},{3,1},{4,6},{6,4},{5,7},{7,5},{8,10},{10,8},{9,1... | collective-permute-start | bytes 3145736 | tf_op jit(solution)/shard_map/ppermute | solution.py:20
  1281.2 75.5 %collective-permute-start.103 = (f32[256,1024]{1,0:T(8,128)S(1)}, f32[256,1024]{1,0:T(8,128)S(1)}, u32[]{:S(2)}, u32[]{:S(2)}) collective-permute-start(f32[256,1024]{1,0:T(8,128)S(1)} %get-tuple-element.247), channel_id=1, source_target_pairs={{0,0},{1,8},{2,16},{3,24},{8,1},{9,9},{10,17},{11,25},{16,2},{17,1... | collective-permute-start | bytes 3145736 | tf_op jit(solution)/shard_map/ppermute | solution.py:31
  1284.4 69.4 %collective-permute-start.97 = (bf16[256,1024]{1,0:T(8,128)(2,1)S(1)}, bf16[256,1024]{1,0:T(8,128)(2,1)S(1)}, u32[]{:S(2)}, u32[]{:S(2)}) collective-permute-start(bf16[256,1024]{1,0:T(8,128)(2,1)S(1)} %get-tuple-element.248), channel_id=1, source_target_pairs={{0,0},{1,8},{2,16},{3,24},{8,1},{9,9},{10,17},{11,25},{16,2},{17,1... | collective-permute-start | bytes 1572872 | tf_op jit(solution)/shard_map/ppermute | solution.py:31
  (208 other events, 3329.6 us)
Sparse Core Ops, SparseCore 0:
  10.7 46.2 all-gather.11
  63.4 46.5 all-gather.13
  174.5 47.0 all-gather.15
  223.6 44.9 all-gather.17
  270.0 33.1 all-gather.19
  346.3 27.1 all-gather.21
  375.0 27.2 all-gather.23
  403.8 27.2 all-gather.25
  432.6 27.1 all-gather.27
  584.9 47.1 all-gather.29
  695.0 45.6 reduce-scatter.7
  912.3 42.0 reduce-scatter.9
  956.6 43.3 reduce-scatter.11
  1002.2 43.3 reduce-scatter.13
  1055.6 79.6 all-gather.31
  1177.7 30.1 reduce-scatter.17
  1210.1 43.3 reduce-scatter.15
  1256.2 77.3 reduce-scatter.19

commit v4 on v3

--- a/solution.py
+++ b/solution.py
@@ -47,15 +47,28 @@
 
 
 def ring_add(blocks, held=(), held_two=()):
+    blocks, held = ring_add_first(blocks, held)
+    total = ring_add_rest(blocks, held_two)
+    if held_two:
+        return (total[0], *held, *total[1:])
+    return (total, *held) if held else total
+
+
+def ring_add_first(blocks, held=()):
     zero, one, two, three = blocks
     i = lax.axis_index("a")
     two = two + line(jnp.where(i == 0, three, one), [(0, 1), (3, 2)])
     two, *held = lax.optimization_barrier((two, *held))
+    return (zero, one, two, three), held
+
+
+def ring_add_rest(blocks, held_two=()):
+    zero, one, two, three = blocks
     one = one + line(two, [(0, 1), (1, 2)])
     three = three + line(two, [(3, 2), (2, 1)])
     one, three, *held_two = lax.optimization_barrier((one, three, *held_two))
     total = zero + line(one, [(0, 1), (1, 2), (2, 3)]) + line(three, [(3, 2), (2, 1), (1, 0)])
-    return (total, *held, *held_two) if held or held_two else total
+    return (total, *held_two) if held_two else total
 
 
 def ring_first(own):
@@ -112,28 +125,36 @@
     return jnp.concatenate(blocks, axis=1).astype(f32)
 
 
-def swapped(shards, r):
+def block_for(shards, r):
     blocks = [column_block(shard, (4 - r) % 4) for shard in shards]
-    blocks = jnp.concatenate(blocks, axis=1) if len(blocks) > 1 else blocks[0]
-    return shift(blocks, "a", 4 - r) if r else blocks
+    return jnp.concatenate(blocks, axis=1) if len(blocks) > 1 else blocks[0]
 
 
 def together(*values):
     return lax.optimization_barrier(values)
 
 
-def gather_all(own):
-    i = lax.axis_index("a")
-
-    def spread(block):
-        pair = jnp.concatenate([block, flip(block, "x")], axis=0)
-        return jnp.concatenate([pair, flip(pair, "c")], axis=0)
-
+def line_pieces(own):
     first = ring_first(own)
     second = ring_second(*first)
     far = ring_third(*second)
-    two = jnp.where(i < 2, second[1], second[0])
-    return [spread(block) for block in (own, first[1], two, first[0], far)]
+    two = jnp.where(lax.axis_index("a") < 2, second[1], second[0])
+    return [own, first[1], two, first[0], far]
+
+
+def spread_over_x(*blocks):
+    group = jnp.stack(blocks)
+    return jnp.stack([group, flip(group, "x")], axis=1)
+
+
+def spread_over_c(group):
+    group = jnp.stack([group, flip(group, "c")], axis=1)
+    return [piece.reshape(-1, group.shape[-1]) for piece in group]
+
+
+def spread_one(block):
+    pair = jnp.concatenate([block, flip(block, "x")], axis=0)
+    return jnp.concatenate([pair, flip(pair, "c")], axis=0)
 
 
 def ring_pieces(pieces):
@@ -168,16 +189,17 @@
     return near + flip(far, "x")
 
 
-def tensor_gather(own):
+def tensor_gather(own, held=()):
     size = lax.axis_size("a")
     a = lax.axis_index("a")
     t = lax.axis_index("x") * 2 + lax.axis_index("c")
-    pair = jnp.stack([own, flip(own, "x")])
+    pair, *held = together(jnp.stack([own, flip(own, "x")]), *held)
     other = flip(pair, "c")
     pieces = jnp.stack([pair[0], other[0], pair[1], other[1]])
-    return jnp.concatenate(
+    gathered = jnp.concatenate(
         [lax.dynamic_index_in_dim(pieces, ((a + r) % size) ^ t, 0, False) for r in range(size)], axis=0
     )
+    return (gathered, *held) if held else gathered
 
 
 def chunk_gains(value):
@@ -351,32 +373,47 @@
     ffn_gain = gains[:, 1].reshape(-1)
     inv_one = lax.rsqrt(ring_sum(jnp.sum(x_block * x_block, axis=1, keepdims=True)) / width + epsilon)
     normed_one = x_block * inv_one
-    hidden_block, gate_shard, up_shard = together(
-        (normed_one * attn_gain).astype(bf16), w_gate, w_up
-    )
-    near = [swapped([gate_shard, up_shard], r) for r in (1, 3)]
-    hidden_one = tensor_gather(hidden_block)
-    qkv, *near = ring_scatter(project_in(hidden_one, wqkv), near)
+    gate_up_blocks = [block_for([w_gate, w_up], r) for r in range(4)]
+    down_blocks = [block_for([w_down], r) for r in range(4)]
+    hidden_block, *gate_up_blocks = together((normed_one * attn_gain).astype(bf16), *gate_up_blocks)
+    near = [shift(gate_up_blocks[r], "a", 4 - r) for r in (1, 3)]
+    hidden_one, dy_block = together(tensor_gather(hidden_block), cotangent)
+    blocks = jnp.split(project_in(hidden_one, wqkv), 4, axis=0)
+    blocks, held = ring_add_first(blocks, (transpose_blocks(dy_block), *near))
+    dy_block, near = held[0], held[1:]
+    qkv, *dy_line = ring_add_rest(blocks, line_pieces(dy_block))
     wo = fetch(w_out)
-    zero, one, three = [fetch(piece) for piece in (swapped([w_gate, w_up], 0), *near)]
-    qkv, down_shard = together(qkv, w_down)
-    down = [swapped([down_shard], r) for r in range(4)]
+    zero, one, three = [fetch(piece) for piece in (gate_up_blocks[0], *near)]
+    values = together(qkv, *dy_line, *down_blocks)
+    qkv, dy_line, down_blocks = values[0], values[1:6], values[6:]
+    down = [shift(down_blocks[r], "a", 4 - r) for r in (1, 2, 3)]
     mixed, saved = attention_forward(qkv, segments, query_gain, key_gain, kv_heads)
-    mixed, zero, one, three, dy_block, *down = together(mixed, zero, one, three, cotangent, *down)
-    dy_block = transpose_blocks(dy_block)
-    dy_pieces = gather_all(dy_block)
-    down = [fetch(piece) for piece in down]
-    mixed_rows, gate_shard, up_shard = together(ring_gather(mixed), w_gate, w_up)
-    opposite = swapped([gate_shard, up_shard], 2)
-    resid = x_block + tensor_scatter(project_out(mixed_rows, wo))
+    values = together(
+        mixed,
+        spread_over_x(dy_line[0], dy_line[1], dy_line[3]),
+        spread_over_x(dy_line[2], dy_line[4]),
+        zero,
+        one,
+        three,
+        gate_up_blocks[2],
+        *down,
+    )
+    mixed = values[0]
+    dy_own, dy_one, dy_three = spread_over_c(values[1])
+    dy_two, dy_far = spread_over_c(values[2])
+    zero, one, three, opposite = values[3:7]
+    down = [fetch(piece) for piece in (down_blocks[0], *values[7:])]
+    values = together(ring_gather(mixed), opposite, dy_own, dy_one, dy_two, dy_three, dy_far)
+    mixed_rows, opposite, dy_pieces = values[0], values[1], values[2:]
+    dy_rows = dy_pieces[0]
+    opposite = shift(opposite, "a", 2)
+    resid, opposite = together(x_block + tensor_scatter(project_out(mixed_rows, wo)), opposite)
+    two = fetch(opposite)
     inv_two = lax.rsqrt(ring_sum(jnp.sum(resid * resid, axis=1, keepdims=True)) / width + epsilon)
     normed_two = resid * inv_two
-    values = together((normed_two * ffn_gain).astype(bf16), opposite, *down, *dy_pieces)
-    hidden_block, opposite, down, dy_pieces = values[0], values[1], values[2:6], values[6:]
-    dy_rows = dy_pieces[0]
-    two = fetch(opposite)
+    hidden_block, *down = together((normed_two * ffn_gain).astype(bf16), *down)
     columns = [zero, one, two, three]
-    hidden_pieces = gather_all(hidden_block)
+    hidden_pieces = [spread_one(piece) for piece in line_pieces(hidden_block)]
     d_act = project_all(dy_pieces, down)
     gate, up = jnp.split(project_all(hidden_pieces, columns), 2, axis=1)
     hidden_pieces = ring_pieces(hidden_pieces)
@@ -392,55 +429,61 @@
     d_gate_up, next_grad = together(d_gate_up, next_grad)
     next_grad = shift(pair_scatter(next_grad), "a", 1)
     parts.update({r: project_out(d_gate_up, columns[r]) for r in (2, 0)})
-    parts = {r: flip_half(parts[r]) for r in (3, 1, 2, 0)}
-    parts[3], *act_first = together(parts[3], *ring_first(act))
-    act_second = ring_second(*act_first)
-    parts = {r: flip_rest(parts[r]) for r in (3, 1, 2, 0)}
-    parts[3], parts[1], next_grad, *act_second = together(
-        parts[3], parts[1], next_grad, *act_second
+    parts = {r: flip_rest(flip_half(parts[r])) for r in (3, 1, 2, 0)}
+    parts[3], parts[1], next_grad, *act_first = together(
+        parts[3], parts[1], next_grad, *ring_first(act)
     )
     d_hidden_two, *grads = together(
         ring_add([parts[r] for r in range(4)]),
         *[weight_partial(hidden_pieces[r], d_gate_up) for r in (3, 2, 0)],
     )
     last_grad, far_grad, own_grad = [pair_scatter(grad) for grad in grads]
-    last_grad = shift(last_grad, "a", 3)
     ffn_gain_part = jnp.sum(d_hidden_two * normed_two, axis=0)
     e_two = d_hidden_two * ffn_gain
     stat_two = ring_sum(jnp.sum(e_two * normed_two, axis=1, keepdims=True)) / width
     d_resid = dy_block.astype(f32) + inv_two * (e_two - normed_two * stat_two)
-    d_resid_rows = tensor_gather(d_resid.astype(bf16))
-    d_mixed, last_grad = together(project_in(d_resid_rows, wo), last_grad)
-    d_mixed, far_grad, own_grad, *act_second = together(
-        ring_scatter(d_mixed), far_grad, own_grad, *act_second
-    )
+    d_resid, *act_first = together(d_resid, *act_first)
+    act_second = ring_second(*act_first)
+    d_resid_rows, *act_second = tensor_gather(d_resid.astype(bf16), act_second)
+    d_mixed, wd = together(project_in(d_resid_rows, wo), wd)
+    far_parts = jnp.split(far_grad, 4, axis=1)
+    d_mixed, grad_out, last_grad, far_parts[0], own_grad, *act_second = together(
+        ring_scatter(d_mixed),
+        weight_partial(d_resid_rows, mixed_rows),
+        last_grad,
+        shift(far_parts[0], "a", 2),
+        own_grad,
+        *act_second,
+    )
+    grad_out = pair_scatter(grad_out)
     act_third = ring_third(*act_second)
     d_qkv, query_part, key_part = attention_backward(d_mixed, saved, query_gain, key_gain)
-    d_qkv, act_third = together(d_qkv, act_third)
+    d_qkv, act_third, grad_out = together(d_qkv, act_third, grad_out)
     act_rows = jnp.concatenate(ring_order(act, *act_first, *act_second, act_third), axis=1)
-    d_qkv_rows, head_parts, grad_down, ffn_out, grad_out = together(
+    d_qkv_rows, head_parts, grad_down, ffn_out, last_grad, far_parts[1] = together(
         ring_gather(d_qkv),
         ring_sum(jnp.stack([query_part, key_part])),
         weight_partial(dy_rows, act_rows),
-        project_out(act_rows, wd),
-        weight_partial(d_resid_rows, mixed_rows),
+        flip_half(project_out(act_rows, wd)),
+        last_grad,
+        shift(far_parts[1], "a", 2),
     )
     grad_down = pair_scatter(grad_down)
-    grad_out = pair_scatter(grad_out).astype(f32)
-    block_out = transpose_blocks((resid + flip_rest(flip_half(ffn_out))).astype(bf16))
-    d_qkv_rows, far_grad = together(d_qkv_rows, far_grad)
-    d_hidden_one, far_grad = together(
-        tensor_scatter(project_out(d_qkv_rows, wqkv)), shift(far_grad, "a", 2)
-    )
+    grad_out = grad_out.astype(f32)
+    d_hidden_one, d_qkv_rows = together(project_out(d_qkv_rows, wqkv), d_qkv_rows)
+    d_hidden_one, ffn_out, last_grad, far_parts[2] = together(
+        tensor_scatter(d_hidden_one),
+        ffn_out,
+        shift(last_grad, "a", 3),
+        shift(far_parts[2], "a", 2),
+    )
+    block_out = transpose_blocks((resid + flip_rest(ffn_out)).astype(bf16))
     attn_gain_part = jnp.sum(d_hidden_one * normed_one, axis=0)
     e_one = d_hidden_one * attn_gain
     stat_one = ring_sum(jnp.sum(e_one * normed_one, axis=1, keepdims=True)) / width
     d_tokens = d_resid + inv_one * (e_one - normed_one * stat_one)
+    d_tokens, far_parts[3] = together(d_tokens, far_parts[3])
     d_tokens = transpose_blocks(d_tokens)
-    grad_gate_up = jnp.concatenate([own_grad, last_grad, far_grad, next_grad], axis=1)
-    grad_gate = plain_columns(grad_gate_up, 0, 2)
-    grad_up = plain_columns(grad_gate_up, 1, 2)
-    grad_down = plain_columns(grad_down)
     grad_qkv = weight_grad(hidden_one, d_qkv_rows)
 
     gains = jnp.concatenate(
@@ -448,6 +491,11 @@
     ).reshape(-1, head)
     gains = gains + flip(gains, "c")
     gains = gains + flip(gains, "x")
+    far_parts[3] = shift(far_parts[3], "a", 2)
+    grad_gate_up = jnp.concatenate([own_grad, last_grad, *far_parts, next_grad], axis=1)
+    grad_gate = plain_columns(grad_gate_up, 0, 2)
+    grad_up = plain_columns(grad_gate_up, 1, 2)
+    grad_down = plain_columns(grad_down)
     gains = gains + flip(gains, "b") if lax.axis_size("b") == 2 else lax.psum(gains, "b")
     chunk = attn_gain_part.shape[0]
     lane = (lax.axis_index("b") * lax.axis_size("x") + lax.axis_index("x")) * lax.axis_size(

time: 1380 us -> 1340 us (0.971)
  waiting for transfers between devices: 817 us -> 759 us
  other arithmetic: 123 us -> 145 us
  starting transfers between devices: 172 us -> 156 us
    ppermute x9 -> x12, waiting for transfers between devices: 219 us -> 165 us  [shift(): lax.ppermute(value, axis, [(i, (i + step) % size) for i in range(size)])]
    ppermute x54 -> x48, waiting for transfers between devices: 159 us -> 201 us  [flip(): lax.ppermute(value, axis, [(i, i ^ mask) for i in range(lax.axis_size(axi...]
    ppermute x4, waiting for transfers between devices: 98.3 us -> 78.2 us  [transpose_blocks(): return lax.ppermute(value, ('a', 'x', 'c'), pairs)]
    another operation x2 -> x9, other arithmetic: 2.12 us -> 19.2 us  [the longest x4 10.9 us: spread_over_x(): return jnp.stack([group, flip(group, 'x')], axis=1)]
    add x10 -> x12, other arithmetic: 20 us -> 28.3 us  [the longest x3 11.1 us: ring_add_rest(): three = three + line(two, [(3, 2), (2, 1)])]
    ppermute x54 -> x48, starting transfers between devices: 38.4 us -> 33.7 us  [flip(): lax.ppermute(value, axis, [(i, i ^ mask) for i in range(lax.axis_size(axi...]
    unnamed x311 -> x320, local copies, waits for them, and re-layouts: 34.5 us -> 32.3 us
  transfers between devices with their start and end apart: 125 -> 122, of which waited for: 60 -> 60; matrix products, arithmetic and copies ran while one was open for 21% -> 24% of each run, Pallas kernels for 0% -> 0%
where the time goes in v4:
time: 1340 us; the launch traced here: 1330 us
  waiting for transfers between devices  759 us (57%)
  starting transfers between devices  156 us (12%)
  matrix products  153 us (11%)
  other arithmetic  145 us (11%)
  local copies, waits for them, and re-layouts  96.1 us (7%)
  between operations  17.6 us (1%)
    ppermute x40, waiting for transfers between devices, line(): return lax.ppermute(value, 'a', pairs)  305 us
    ppermute x48, waiting for transfers between devices, flip(): lax.ppermute(value, axis, [(i, i ^ mask) for i in range(lax.axis_size(axi...  201 us
    ppermute x12, waiting for transfers between devices, shift(): lax.ppermute(value, axis, [(i, (i + step) % size) for i in range(size)])  165 us
    dot_general x26, matrix products, dot(): lax.dot_general(left, right, (((left_dim,), (right_dim,)), ((), ())), pre...  143 us
    ppermute x40, starting transfers between devices, line(): return lax.ppermute(value, 'a', pairs)  89.8 us
    ppermute x4, waiting for transfers between devices, transpose_blocks(): return lax.ppermute(value, ('a', 'x', 'c'), pairs)  78.2 us
    ppermute x48, starting transfers between devices, flip(): lax.ppermute(value, axis, [(i, i ^ mask) for i in range(lax.axis_size(axi...  33.7 us
    unnamed x320, local copies, waits for them, and re-layouts  32.3 us
  transfers between devices with their start and end apart: 122, of which 60 were waited for; matrix products, arithmetic and copies ran while one was open for 24% of the time, Pallas kernels for 0%

profile of v4, /device:TPU:2, one launch (start us, length us, event | category | flops | bytes accessed | tf_op | source)
XLA Modules:
  0.0 1326.5 jit_solution(870209218478916334)
XLA Ops:
  26.4 13.5 %collective-permute-done = bf16[256,1024]{1,0:T(8,128)(2,1)S(1)} collective-permute-done((bf16[256,1024]{1,0:T(8,128)(2,1)S(1)}, bf16[256,1024]{1,0:T(8,128)(2,1)S(1)}, u32[]{:S(2)}, u32[]{:S(2)}) %collective-permute-start) | collective-permute-done | bytes 524320 | tf_op jit(solution)/shard_map/ppermute | solution.py:31
  43.8 5.3 collective-permute-done.2
  49.4 10.1 collective-permute-done.6
  63.2 6.0 fusion.94
  78.1 28.3 %collective-permute-done.8 = f32[256,1536]{1,0:T(8,128)S(1)} collective-permute-done((f32[256,1536]{1,0:T(8,128)S(1)}, f32[256,1536]{1,0:T(8,128)S(1)}, u32[]{:S(2)}, u32[]{:S(2)}) %collective-permute-start.8) | collective-permute-done | bytes 1572896 | tf_op jit(solution)/shard_map/ppermute | solution.py:42
  107.8 32.4 %collective-permute-done.10 = bf16[512,1536]{1,0:T(8,128)(2,1)S(1)} collective-permute-done((bf16[512,1536]{1,0:T(8,128)(2,1)S(1)}, bf16[512,1536]{1,0:T(8,128)(2,1)S(1)}, u32[]{:S(2)}, u32[]{:S(2)}) %collective-permute-start.10) | collective-permute-done | bytes 1572896 | tf_op jit(solution)/shard_map/ppermute | solution.py:16
  140.1 36.6 %collective-permute-done.11 = bf16[512,1536]{1,0:T(8,128)(2,1)} collective-permute-done((bf16[512,1536]{1,0:T(8,128)(2,1)}, bf16[512,1536]{1,0:T(8,128)(2,1)}, u32[]{:S(2)}, u32[]{:S(2)}) %collective-permute-start.11) | collective-permute-done | bytes 1572896 | tf_op jit(solution)/shard_map/ppermute | solution.py:16
  176.7 7.6 collective-permute-done.9
  189.5 5.4 collective-permute-start.16
  194.8 6.9 collective-permute-done.14
  203.0 26.0 %collective-permute-done.16 = bf16[256,1024]{1,0:T(8,128)(2,1)} collective-permute-done((bf16[256,1024]{1,0:T(8,128)(2,1)S(1)}, bf16[256,1024]{1,0:T(8,128)(2,1)}, u32[]{:S(2)}, u32[]{:S(2)}) %collective-permute-start.16) | collective-permute-done | bytes 524320 | tf_op jit(solution)/shard_map/ppermute | solution.py:42
  238.6 19.6 %collective-permute-done.18 = bf16[256,1024]{1,0:T(8,128)(2,1)S(1)} collective-permute-done((bf16[256,1024]{1,0:T(8,128)(2,1)S(1)}, bf16[256,1024]{1,0:T(8,128)(2,1)S(1)}, u32[]{:S(2)}, u32[]{:S(2)}) %collective-permute-start.18) | collective-permute-done | bytes 524320 | tf_op jit(solution)/shard_map/ppermute | solution.py:42
  267.9 26.4 %collective-permute-done.19 = f32[256,1536]{1,0:T(8,128)S(1)} collective-permute-done((f32[256,1536]{1,0:T(8,128)}, f32[256,1536]{1,0:T(8,128)S(1)}, u32[]{:S(2)}, u32[]{:S(2)}) %collective-permute-start.19) | collective-permute-done | bytes 1572896 | tf_op jit(solution)/shard_map/ppermute | solution.py:42
  295.5 5.4 collective-permute-done.20
  345.2 23.9 %collective-permute-done.21 = bf16[3,256,1024]{2,1,0:T(8,128)(2,1)} collective-permute-done((bf16[3,256,1024]{2,1,0:T(8,128)(2,1)}, bf16[3,256,1024]{2,1,0:T(8,128)(2,1)}, u32[]{:S(2)}, u32[]{:S(2)}) %collective-permute-start.21) | collective-permute-done | bytes 1572896 | tf_op jit(solution)/shard_map/ppermute | solution.py:20
  372.5 26.6 %collective-permute-done.24 = bf16[512,768]{1,0:T(8,128)(2,1)} collective-permute-done((bf16[512,768]{1,0:T(8,128)(2,1)}, bf16[512,768]{1,0:T(8,128)(2,1)}, u32[]{:S(2)}, u32[]{:S(2)}) %collective-permute-start.24) | collective-permute-done | bytes 786464 | tf_op jit(solution)/shard_map/ppermute | solution.py:16
  403.2 9.4 collective-permute-done.26
  418.9 14.3 %collective-permute-done.29 = bf16[256,1024]{1,0:T(8,128)(2,1)S(1)} collective-permute-done((bf16[256,1024]{1,0:T(8,128)(2,1)}, bf16[256,1024]{1,0:T(8,128)(2,1)S(1)}, u32[]{:S(2)}, u32[]{:S(2)}) %collective-permute-start.29) | collective-permute-done | bytes 524320 | tf_op jit(solution)/shard_map/ppermute | solution.py:42
  435.7 13.4 %collective-permute-done.30 = bf16[256,1024]{1,0:T(8,128)(2,1)} collective-permute-done((bf16[256,1024]{1,0:T(8,128)(2,1)}, bf16[256,1024]{1,0:T(8,128)(2,1)}, u32[]{:S(2)}, u32[]{:S(2)}) %collective-permute-start.30) | collective-permute-done | bytes 524320 | tf_op jit(solution)/shard_map/ppermute | solution.py:42
  475.4 25.0 %collective-permute-done.34 = f32[256,1024]{1,0:T(8,128)} collective-permute-done((f32[256,1024]{1,0:T(8,128)}, f32[256,1024]{1,0:T(8,128)}, u32[]{:S(2)}, u32[]{:S(2)}) %collective-permute-start.34) | collective-permute-done | bytes 1048608 | tf_op jit(solution)/shard_map/ppermute | solution.py:20
  502.9 35.9 %collective-permute-done.35 = bf16[512,1536]{1,0:T(8,128)(2,1)} collective-permute-done((bf16[512,1536]{1,0:T(8,128)(2,1)}, bf16[512,1536]{1,0:T(8,128)(2,1)}, u32[]{:S(2)}, u32[]{:S(2)}) %collective-permute-start.35) | collective-permute-done | bytes 1572896 | tf_op jit(solution)/shard_map/ppermute | solution.py:16
  573.0 8.4 collective-permute-done.46
  585.7 11.1 collective-permute-done.44
  597.0 10.5 collective-permute-done.48
  610.7 5.3 fusion.99
  616.0 6.0 collective-permute-done.51
  622.3 5.3 fusion.100
  627.8 5.4 fusion.101
  633.3 11.2 add_add_fusion
  650.8 7.2 multiply_convert_fusion.2
  664.8 5.0 fusion.76
  669.8 5.0 convolution_convert_fusion.5
  692.1 7.5 collective-permute-start.60
  711.6 8.5 reduce-scatter.8.cloned.1.call-done
  721.5 6.3 fusion.103
  735.0 18.3 %collective-permute-done.56 = f32[256,1024]{1,0:T(8,128)} collective-permute-done((f32[256,1024]{1,0:T(8,128)}, f32[256,1024]{1,0:T(8,128)}, u32[]{:S(2)}, u32[]{:S(2)}) %collective-permute-start.56) | collective-permute-done | bytes 1048608 | tf_op jit(solution)/shard_map/ppermute | solution.py:20
  754.8 16.7 %collective-permute-done.61 = bf16[1024,768]{1,0:T(8,128)(2,1)} collective-permute-done((bf16[1024,768]{1,0:T(8,128)(2,1)}, bf16[1024,768]{1,0:T(8,128)(2,1)}, u32[]{:S(2)}, u32[]{:S(2)}) %collective-permute-start.61) | collective-permute-done | bytes 1572896 | tf_op jit(solution)/shard_map/ppermute | solution.py:42
  775.6 19.1 %collective-permute-done.64 = f32[256,1024]{1,0:T(8,128)S(1)} collective-permute-done((f32[256,1024]{1,0:T(8,128)S(1)}, f32[256,1024]{1,0:T(8,128)S(1)}, u32[]{:S(2)}, u32[]{:S(2)}) %collective-permute-start.64) | collective-permute-done | bytes 1048608 | tf_op jit(solution)/shard_map/ppermute | solution.py:42
  797.6 5.0 collective-permute-start.65
  802.6 5.0 convolution_convert_fusion.2
  815.5 7.1 collective-permute-done.65
  825.0 6.6 collective-permute-start.67
  833.3 6.3 convolution_convert_fusion.3
  839.6 7.8 convolution_convert_fusion.4
  850.8 5.1 collective-permute-done.68
  863.4 5.4 collective-permute-done.70
  874.0 7.5 collective-permute-done.71
  882.7 20.4 %collective-permute-done.73 = bf16[1024,768]{1,0:T(8,128)(2,1)S(1)} collective-permute-done((bf16[1024,768]{1,0:T(8,128)(2,1)}, bf16[1024,768]{1,0:T(8,128)(2,1)S(1)}, u32[]{:S(2)}, u32[]{:S(2)}) %collective-permute-start.73) | collective-permute-done | bytes 1572896 | tf_op jit(solution)/shard_map/ppermute | solution.py:42
  919.1 22.6 %collective-permute-done.75 = f32[256,1024]{1,0:T(8,128)S(1)} collective-permute-done((f32[256,1024]{1,0:T(8,128)S(1)}, f32[256,1024]{1,0:T(8,128)S(1)}, u32[]{:S(2)}, u32[]{:S(2)}) %collective-permute-start.75) | collective-permute-done | bytes 1048608 | tf_op jit(solution)/shard_map/ppermute | solution.py:42
  943.1 5.4 collective-permute-start.76
  951.0 18.5 %collective-permute-done.76 = f32[256,1024]{1,0:T(8,128)} collective-permute-done((f32[256,1024]{1,0:T(8,128)S(1)}, f32[256,1024]{1,0:T(8,128)}, u32[]{:S(2)}, u32[]{:S(2)}) %collective-permute-start.76) | collective-permute-done | bytes 1048608 | tf_op jit(solution)/shard_map/ppermute | solution.py:42
  973.5 6.6 collective-permute-start.78
  992.6 11.3 collective-permute-done.78
  1008.2 13.7 %collective-permute-done.80 = bf16[512,384]{1,0:T(8,128)(2,1)} collective-permute-done((bf16[512,384]{1,0:T(8,128)(2,1)}, bf16[512,384]{1,0:T(8,128)(2,1)}, u32[]{:S(2)}, u32[]{:S(2)}) %collective-permute-start.80) | collective-permute-done | bytes 393248 | tf_op jit(solution)/shard_map/ppermute | solution.py:16
  1069.1 14.7 %collective-permute-done.87 = f32[2,128]{1,0:T(2,128)S(1)} collective-permute-done((f32[2,128]{1,0:T(2,128)S(1)}, f32[2,128]{1,0:T(2,128)S(1)}, u32[]{:S(2)}, u32[]{:S(2)}) %collective-permute-start.87) | collective-permute-done | bytes 1056 | tf_op jit(solution)/shard_map/ppermute | solution.py:20
  1090.0 9.9 fusion.21
  1102.4 10.2 collective-permute-done.85
  1116.5 10.8 convolution_convert_fusion
  1164.8 20.2 %collective-permute-done.92 = f32[256,1024]{1,0:T(8,128)} collective-permute-done((f32[256,1024]{1,0:T(8,128)}, f32[256,1024]{1,0:T(8,128)}, u32[]{:S(2)}, u32[]{:S(2)}) %collective-permute-start.92) | collective-permute-done | bytes 1048608 | tf_op jit(solution)/shard_map/ppermute | solution.py:20
  1186.8 19.3 %collective-permute-done.94 = bf16[512,384]{1,0:T(8,128)(2,1)S(1)} collective-permute-done((bf16[512,384]{1,0:T(8,128)(2,1)S(1)}, bf16[512,384]{1,0:T(8,128)(2,1)S(1)}, u32[]{:S(2)}, u32[]{:S(2)}) %collective-permute-start.94) | collective-permute-done | bytes 393248 | tf_op jit(solution)/shard_map/ppermute | solution.py:16
  1218.7 14.4 %collective-permute-done.102 = f32[18,128]{1,0:T(8,128)S(1)} collective-permute-done((f32[18,128]{1,0:T(8,128)S(1)}, f32[18,128]{1,0:T(8,128)S(1)}, u32[]{:S(2)}, u32[]{:S(2)}) %collective-permute-start.102) | collective-permute-done | bytes 9248 | tf_op jit(solution)/shard_map/ppermute | solution.py:20
  1234.3 5.8 collective-permute-start.99
  1251.2 45.9 %collective-permute-done.99 = f32[256,1024]{1,0:T(8,128)S(1)} collective-permute-done((f32[256,1024]{1,0:T(8,128)S(1)}, f32[256,1024]{1,0:T(8,128)S(1)}, u32[]{:S(2)}, u32[]{:S(2)}) %collective-permute-start.99) | collective-permute-done | bytes 1048608 | tf_op jit(solution)/shard_map/ppermute | solution.py:31
  1297.1 11.2 collective-permute-done.96
  (739 shorter events, 457.4 us)
Async XLA Ops:
  7.2 56.0 %all-gather.12.cloned.1.call-start = ((), (), s32[]{:S(2)}) async-start(), calls=%async_computation.7 | async-start | bytes 4718592 | tf_op jit(solution)/shard_map/all_gather | solution.py:216
  10.7 29.3 %collective-permute-start = (bf16[256,1024]{1,0:T(8,128)(2,1)S(1)}, bf16[256,1024]{1,0:T(8,128)(2,1)S(1)}, u32[]{:S(2)}, u32[]{:S(2)}) collective-permute-start(bf16[256,1024]{1,0:T(8,128)(2,1)S(1)} %copy-done.148), channel_id=1, source_target_pairs={{0,0},{1,8},{2,16},{3,24},{8,1},{9,9},{10,17},{11,25},{16,2},{17,1... | collective-permute-start | bytes 1572872 | tf_op jit(solution)/shard_map/ppermute | solution.py:31
  15.2 357.3 %all-gather.14.cloned.1.call-start = ((), (), s32[]{:S(2)}) async-start(), calls=%async_computation.8 | async-start | bytes 4718592 | tf_op jit(solution)/shard_map/all_gather | solution.py:216
  59.8 312.7 %all-gather.16.cloned.1.call-start = ((), (), s32[]{:S(2)}) async-start(), calls=%async_computation.9 | async-start | bytes 4718592 | tf_op jit(solution)/shard_map/all_gather | solution.py:216
  69.4 37.0 %collective-permute-start.8 = (f32[256,1536]{1,0:T(8,128)S(1)}, f32[256,1536]{1,0:T(8,128)S(1)}, u32[]{:S(2)}, u32[]{:S(2)}) collective-permute-start(f32[256,1536]{1,0:T(8,128)S(1)} %slice_select_fusion), channel_id=1, source_target_pairs={{0,8},{24,16},{1,9},{25,17},{2,10},{26,18},{3,11},{27,19},{4,12},{... | collective-permute-start | bytes 4718600 | tf_op jit(solution)/shard_map/ppermute | solution.py:42
  71.9 68.2 %collective-permute-start.10 = (bf16[512,1536]{1,0:T(8,128)(2,1)S(1)}, bf16[512,1536]{1,0:T(8,128)(2,1)S(1)}, u32[]{:S(2)}, u32[]{:S(2)}) collective-permute-start(bf16[512,1536]{1,0:T(8,128)(2,1)S(1)} %copy-done.76), channel_id=1, source_target_pairs={{0,24},{8,0},{16,8},{24,16},{1,25},{9,1},{17,9},{25,17},{2,26},{10... | collective-permute-start | bytes 4718600 | tf_op jit(solution)/shard_map/ppermute | solution.py:16
  75.5 101.3 %collective-permute-start.11 = (bf16[512,1536]{1,0:T(8,128)(2,1)}, bf16[512,1536]{1,0:T(8,128)(2,1)}, u32[]{:S(2)}, u32[]{:S(2)}) collective-permute-start(bf16[512,1536]{1,0:T(8,128)(2,1)} %pad_maximum_fusion.20), channel_id=1, source_target_pairs={{0,8},{8,16},{16,24},{24,0},{1,9},{9,17},{17,25},{25,1},{2,10},{10... | collective-permute-start | bytes 4718600 | tf_op jit(solution)/shard_map/ppermute | solution.py:16
  75.5 108.9 %collective-permute-start.9 = (bf16[256,1024]{1,0:T(8,128)(2,1)S(1)}, bf16[256,1024]{1,0:T(8,128)(2,1)S(1)}, u32[]{:S(2)}, u32[]{:S(2)}) collective-permute-start(bf16[256,1024]{1,0:T(8,128)(2,1)S(1)} %copy-done.149), channel_id=1, source_target_pairs={{0,0},{1,8},{2,16},{3,24},{8,1},{9,9},{10,17},{11,25},{16,2},{17,1... | collective-permute-start | bytes 1572872 | tf_op jit(solution)/shard_map/ppermute | solution.py:31
  184.4 188.1 %all-gather.18.cloned.1.call-start = ((), (), s32[]{:S(2)}) async-start(), calls=%async_computation.10 | async-start | bytes 4718592 | tf_op jit(solution)/shard_map/all_gather | solution.py:216
  184.9 275.0 %all-gather.20.cloned.1.call-start = ((), (), s32[]{:S(2)}) async-start(), calls=%async_computation.11 | async-start | bytes 3145728 | tf_op jit(solution)/shard_map/all_gather | solution.py:216
  185.0 49.0 %collective-permute-start.12 = (f32[256,1536]{1,0:T(8,128)}, f32[256,1536]{1,0:T(8,128)S(1)}, u32[]{:S(2)}, u32[]{:S(2)}) collective-permute-start(f32[256,1536]{1,0:T(8,128)} %slice_add_fusion), channel_id=1, source_target_pairs={{0,8},{8,16},{1,9},{9,17},{2,10},{10,18},{3,11},{11,19},{4,12},{12... | collective-permute-start | bytes 4718600 | tf_op jit(solution)/shard_map/ppermute | solution.py:42
  186.4 47.6 %collective-permute-start.13 = (f32[256,1536]{1,0:T(8,128)}, f32[256,1536]{1,0:T(8,128)}, u32[]{:S(2)}, u32[]{:S(2)}) collective-permute-start(f32[256,1536]{1,0:T(8,128)} %slice_add_fusion), channel_id=1, source_target_pairs={{24,16},{16,8},{25,17},{17,9},{26,18},{18,10},{27,19},{19,11},{28,... | collective-permute-start | bytes 4718600 | tf_op jit(solution)/shard_map/ppermute | solution.py:42
  189.5 39.5 %collective-permute-start.16 = (bf16[256,1024]{1,0:T(8,128)(2,1)S(1)}, bf16[256,1024]{1,0:T(8,128)(2,1)}, u32[]{:S(2)}, u32[]{:S(2)}) collective-permute-start(bf16[256,1024]{1,0:T(8,128)(2,1)S(1)} %collective-permute-done.9), channel_id=1, source_target_pairs={{0,8},{8,16},{16,24},{1,9},{9,17},{17,25},{2,10},{10,18},{18,26},{... | collective-permute-start | bytes 1572872 | tf_op jit(solution)/shard_map/ppermute | solution.py:42
  201.7 28.8 %collective-permute-start.15 = (bf16[256,1024]{1,0:T(8,128)(2,1)S(1)}, bf16[256,1024]{1,0:T(8,128)(2,1)}, u32[]{:S(2)}, u32[]{:S(2)}) collective-permute-start(bf16[256,1024]{1,0:T(8,128)(2,1)S(1)} %collective-permute-done.14), channel_id=1, source_target_pairs={{16,8},{8,0},{17,9},{9,1},{18,10},{10,2},{19,11},{11,3},{20,12},{1... | collective-permute-start | bytes 1572872 | tf_op jit(solution)/shard_map/ppermute | solution.py:42
  259.0 35.3 %collective-permute-start.19 = (f32[256,1536]{1,0:T(8,128)}, f32[256,1536]{1,0:T(8,128)S(1)}, u32[]{:S(2)}, u32[]{:S(2)}) collective-permute-start(f32[256,1536]{1,0:T(8,128)} %get-tuple-element.132), channel_id=1, source_target_pairs={{0,8},{8,16},{16,24},{1,9},{9,17},{17,25},{2,10},{10,18},{18,26},{... | collective-permute-start | bytes 4718600 | tf_op jit(solution)/shard_map/ppermute | solution.py:42
  260.5 40.3 %collective-permute-start.20 = (f32[256,1536]{1,0:T(8,128)}, f32[256,1536]{1,0:T(8,128)}, u32[]{:S(2)}, u32[]{:S(2)}) collective-permute-start(f32[256,1536]{1,0:T(8,128)} %get-tuple-element.133), channel_id=1, source_target_pairs={{24,16},{16,8},{8,0},{25,17},{17,9},{9,1},{26,18},{18,10},{10,2},{... | collective-permute-start | bytes 4718600 | tf_op jit(solution)/shard_map/ppermute | solution.py:42
  261.9 286.9 %all-gather.22.cloned.1.call-start = ((), (), s32[]{:S(2)}) async-start(), calls=%async_computation.12 | async-start | bytes 2359296 | tf_op jit(solution)/shard_map/all_gather | solution.py:216
  309.5 33.9 %collective-permute-start.22 = (bf16[2,256,1024]{2,1,0:T(8,128)(2,1)}, bf16[2,256,1024]{2,1,0:T(8,128)(2,1)}, u32[]{:S(2)}, u32[]{:S(2)}) collective-permute-start(bf16[2,256,1024]{2,1,0:T(8,128)(2,1)} %get-tuple-element.327), channel_id=1, source_target_pairs={{0,2},{2,0},{1,3},{3,1},{4,6},{6,4},{5,7},{7,5},{8,10},{10,8},{9,1... | collective-permute-start | bytes 3145736 | tf_op jit(solution)/shard_map/ppermute | solution.py:20
  312.5 56.6 %collective-permute-start.21 = (bf16[3,256,1024]{2,1,0:T(8,128)(2,1)}, bf16[3,256,1024]{2,1,0:T(8,128)(2,1)}, u32[]{:S(2)}, u32[]{:S(2)}) collective-permute-start(bf16[3,256,1024]{2,1,0:T(8,128)(2,1)} %get-tuple-element.313), channel_id=1, source_target_pairs={{0,2},{2,0},{1,3},{3,1},{4,6},{6,4},{5,7},{7,5},{8,10},{10,8},{9,1... | collective-permute-start | bytes 4718600 | tf_op jit(solution)/shard_map/ppermute | solution.py:20
  326.6 45.9 %collective-permute-start.23 = (bf16[512,768]{1,0:T(8,128)(2,1)}, bf16[512,768]{1,0:T(8,128)(2,1)}, u32[]{:S(2)}, u32[]{:S(2)}) collective-permute-start(bf16[512,768]{1,0:T(8,128)(2,1)} %get-tuple-element.149), channel_id=1, source_target_pairs={{0,24},{8,0},{16,8},{24,16},{1,25},{9,1},{17,9},{25,17},{2,26},{10... | collective-permute-start | bytes 2359304 | tf_op jit(solution)/shard_map/ppermute | solution.py:16
  329.7 69.4 %collective-permute-start.24 = (bf16[512,768]{1,0:T(8,128)(2,1)}, bf16[512,768]{1,0:T(8,128)(2,1)}, u32[]{:S(2)}, u32[]{:S(2)}) collective-permute-start(bf16[512,768]{1,0:T(8,128)(2,1)} %get-tuple-element.150), channel_id=1, source_target_pairs={{0,16},{8,24},{16,0},{24,8},{1,17},{9,25},{17,1},{25,9},{2,18},{10... | collective-permute-start | bytes 2359304 | tf_op jit(solution)/shard_map/ppermute | solution.py:16
  330.7 68.4 %collective-permute-start.25 = (bf16[512,768]{1,0:T(8,128)(2,1)}, bf16[512,768]{1,0:T(8,128)(2,1)}, u32[]{:S(2)}, u32[]{:S(2)}) collective-permute-start(bf16[512,768]{1,0:T(8,128)(2,1)} %get-tuple-element.151), channel_id=1, source_target_pairs={{0,8},{8,16},{16,24},{24,0},{1,9},{9,17},{17,25},{25,1},{2,10},{10... | collective-permute-start | bytes 2359304 | tf_op jit(solution)/shard_map/ppermute | solution.py:16
  399.1 56.3 %collective-permute-start.31 = (bf16[3,2,256,1024]{3,2,0,1:T(8,128)(2,1)}, bf16[3,2,256,1024]{3,2,0,1:T(8,128)(2,1)}, u32[]{:S(2)}, u32[]{:S(2)}) collective-permute-start(bf16[3,2,256,1024]{3,2,0,1:T(8,128)(2,1)} %pad_maximum_fusion.1), channel_id=1, source_target_pairs={{0,1},{1,0},{2,3},{3,2},{4,5},{5,4},{6,7},{7,6},{8,9},{9,8},{10,11... | collective-permute-start | bytes 9437192 | tf_op jit(solution)/shard_map/ppermute | solution.py:20
  402.9 49.0 %collective-permute-start.32 = (bf16[2,2,256,1024]{3,2,0,1:T(8,128)(2,1)S(1)}, bf16[2,2,256,1024]{3,2,0,1:T(8,128)(2,1)}, u32[]{:S(2)}, u32[]{:S(2)}) collective-permute-start(bf16[2,2,256,1024]{3,2,0,1:T(8,128)(2,1)S(1)} %pad_maximum_fusion.9), channel_id=1, source_target_pairs={{0,1},{1,0},{2,3},{3,2},{4,5},{5,4},{6,7},{7,6},{8,9},{9,8},{10,11... | collective-permute-start | bytes 6291464 | tf_op jit(solution)/shard_map/ppermute | solution.py:20
  403.2 145.6 %all-gather.24.cloned.1.call-start = ((), (), s32[]{:S(2)}) async-start(), calls=%async_computation.13 | async-start | bytes 2359296 | tf_op jit(solution)/shard_map/all_gather | solution.py:216
  435.6 113.2 %all-gather.26.cloned.1.call-start = ((), (), s32[]{:S(2)}) async-start(), calls=%async_computation.14 | async-start | bytes 2359296 | tf_op jit(solution)/shard_map/all_gather | solution.py:216
  467.4 81.5 %all-gather.28.cloned.1.call-start = ((), (), s32[]{:S(2)}) async-start(), calls=%async_computation.15 | async-start | bytes 2359296 | tf_op jit(solution)/shard_map/all_gather | solution.py:216
  467.9 70.9 %collective-permute-start.35 = (bf16[512,1536]{1,0:T(8,128)(2,1)}, bf16[512,1536]{1,0:T(8,128)(2,1)}, u32[]{:S(2)}, u32[]{:S(2)}) collective-permute-start(bf16[512,1536]{1,0:T(8,128)(2,1)} %pad_maximum_fusion.19), channel_id=1, source_target_pairs={{0,16},{8,24},{16,0},{24,8},{1,17},{9,25},{17,1},{25,9},{2,18},{10... | collective-permute-start | bytes 4718600 | tf_op jit(solution)/shard_map/ppermute | solution.py:16
  475.3 158.0 %all-gather.30.cloned.1.call-start = ((), (), s32[]{:S(2)}) async-start(), calls=%async_computation.16 | async-start | bytes 4718592 | tf_op jit(solution)/shard_map/all_gather | solution.py:216
  547.2 172.9 %reduce-scatter.8.cloned.1.call-start = ((), (), s32[]{:S(2)}) async-start(), calls=%async_computation.17 | async-start | bytes 4718592 | tf_op jit(solution)/shard_map/reduce_scatter | solution.py:247
  570.7 38.7 %collective-permute-start.39 = (bf16[512,1024]{1,0:T(8,128)(2,1)S(1)}, bf16[512,1024]{1,0:T(8,128)(2,1)S(1)}, u32[]{:S(2)}, u32[]{:S(2)}) collective-permute-start(bf16[512,1024]{1,0:T(8,128)(2,1)S(1)} %pad_maximum_fusion.26), channel_id=1, source_target_pairs={{0,1},{1,0},{2,3},{3,2},{4,5},{5,4},{6,7},{7,6},{8,9},{9,8},{10,11... | collective-permute-start | bytes 3145736 | tf_op jit(solution)/shard_map/ppermute | solution.py:20
  581.4 26.3 %collective-permute-start.50 = (bf16[256,1024]{1,0:T(8,128)(2,1)S(1)}, bf16[256,1024]{1,0:T(8,128)(2,1)S(1)}, u32[]{:S(2)}, u32[]{:S(2)}) collective-permute-start(bf16[256,1024]{1,0:T(8,128)(2,1)S(1)} %get-tuple-element.322), channel_id=1, source_target_pairs={{16,24},{8,0},{17,25},{9,1},{18,26},{10,2},{19,27},{11,3},{20,28},... | collective-permute-start | bytes 1572872 | tf_op jit(solution)/shard_map/ppermute | solution.py:42
  585.6 36.6 %collective-permute-start.42 = (bf16[512,1024]{1,0:T(8,128)(2,1)S(1)}, bf16[512,1024]{1,0:T(8,128)(2,1)S(1)}, u32[]{:S(2)}, u32[]{:S(2)}) collective-permute-start(bf16[512,1024]{1,0:T(8,128)(2,1)S(1)} %pad_maximum_fusion.27), channel_id=1, source_target_pairs={{0,1},{1,0},{2,3},{3,2},{4,5},{5,4},{6,7},{7,6},{8,9},{9,8},{10,11... | collective-permute-start | bytes 3145736 | tf_op jit(solution)/shard_map/ppermute | solution.py:20
  596.9 30.8 %collective-permute-start.45 = (bf16[512,1024]{1,0:T(8,128)(2,1)S(1)}, bf16[512,1024]{1,0:T(8,128)(2,1)S(1)}, u32[]{:S(2)}, u32[]{:S(2)}) collective-permute-start(bf16[512,1024]{1,0:T(8,128)(2,1)S(1)} %pad_maximum_fusion.28), channel_id=1, source_target_pairs={{0,1},{1,0},{2,3},{3,2},{4,5},{5,4},{6,7},{7,6},{8,9},{9,8},{10,11... | collective-permute-start | bytes 3145736 | tf_op jit(solution)/shard_map/ppermute | solution.py:20
  607.6 25.6 %collective-permute-start.49 = (bf16[512,1024]{1,0:T(8,128)(2,1)S(1)}, bf16[512,1024]{1,0:T(8,128)(2,1)}, u32[]{:S(2)}, u32[]{:S(2)}) collective-permute-start(bf16[512,1024]{1,0:T(8,128)(2,1)S(1)} %pad_maximum_fusion.29), channel_id=1, source_target_pairs={{0,1},{1,0},{2,3},{3,2},{4,5},{5,4},{6,7},{7,6},{8,9},{9,8},{10,11... | collective-permute-start | bytes 3145736 | tf_op jit(solution)/shard_map/ppermute | solution.py:20
  674.9 240.7 %all-gather.32.cloned.1.call-start = ((), (), s32[]{:S(2)}) async-start(), calls=%async_computation.18 | async-start | bytes 9437184 | tf_op jit(solution)/shard_map/all_gather | solution.py:216
  692.1 290.9 %reduce-scatter.12.cloned.1.call-start = ((), (), s32[]{:S(2)}) async-start(), calls=%async_computation.20 | async-start | bytes 4718592 | tf_op jit(solution)/shard_map/reduce_scatter | solution.py:247
  692.1 62.7 %collective-permute-start.60 = (bf16[1024,768]{1,0:T(8,128)(2,1)}, bf16[1024,768]{1,0:T(8,128)(2,1)}, u32[]{:S(2)}, u32[]{:S(2)}) collective-permute-start(bf16[1024,768]{1,0:T(8,128)(2,1)} %get-tuple-element.252), channel_id=1, source_target_pairs={{0,8},{8,16},{16,24},{1,9},{9,17},{17,25},{2,10},{10,18},{18,26},{... | collective-permute-start | bytes 4718600 | tf_op jit(solution)/shard_map/ppermute | solution.py:42
  699.6 71.9 %collective-permute-start.61 = (bf16[1024,768]{1,0:T(8,128)(2,1)}, bf16[1024,768]{1,0:T(8,128)(2,1)}, u32[]{:S(2)}, u32[]{:S(2)}) collective-permute-start(bf16[1024,768]{1,0:T(8,128)(2,1)} %get-tuple-element.252), channel_id=1, source_target_pairs={{24,16},{16,8},{8,0},{25,17},{17,9},{9,1},{26,18},{18,10},{10,2},{... | collective-permute-start | bytes 4718600 | tf_op jit(solution)/shard_map/ppermute | solution.py:42
  704.6 26.3 %collective-permute-start.58 = (f32[256,1024]{1,0:T(8,128)}, f32[256,1024]{1,0:T(8,128)S(1)}, u32[]{:S(2)}, u32[]{:S(2)}) collective-permute-start(f32[256,1024]{1,0:T(8,128)} %slice_bitcast_fusion.4), channel_id=1, source_target_pairs={{0,2},{2,0},{1,3},{3,1},{4,6},{6,4},{5,7},{7,5},{8,10},{10,8},{9,1... | collective-permute-start | bytes 3145736 | tf_op jit(solution)/shard_map/ppermute | solution.py:20
  710.7 42.7 %collective-permute-start.56 = (f32[256,1024]{1,0:T(8,128)}, f32[256,1024]{1,0:T(8,128)}, u32[]{:S(2)}, u32[]{:S(2)}) collective-permute-start(f32[256,1024]{1,0:T(8,128)} %slice_bitcast_fusion.6), channel_id=1, source_target_pairs={{0,2},{2,0},{1,3},{3,1},{4,6},{6,4},{5,7},{7,5},{8,10},{10,8},{9,1... | collective-permute-start | bytes 3145736 | tf_op jit(solution)/shard_map/ppermute | solution.py:20
  720.1 51.5 %collective-permute-start.59 = (bf16[512,1536]{1,0:T(8,128)(2,1)}, bf16[512,1536]{1,0:T(8,128)(2,1)S(1)}, u32[]{:S(2)}, u32[]{:S(2)}) collective-permute-start(bf16[512,1536]{1,0:T(8,128)(2,1)} %reduce-scatter.8.cloned.1.call-done), channel_id=1, source_target_pairs={{0,8},{8,16},{16,24},{24,0},{1,9},{9,17},{17,25},{25,1},{2,10},{10... | collective-permute-start | bytes 4718600 | tf_op jit(solution)/shard_map/ppermute | solution.py:16
  731.8 43.7 %collective-permute-start.63 = (f32[256,1024]{1,0:T(8,128)S(1)}, f32[256,1024]{1,0:T(8,128)S(1)}, u32[]{:S(2)}, u32[]{:S(2)}) collective-permute-start(f32[256,1024]{1,0:T(8,128)S(1)} %slice_bitcast_fusion.2), channel_id=1, source_target_pairs={{0,2},{2,0},{1,3},{3,1},{4,6},{6,4},{5,7},{7,5},{8,10},{10,8},{9,1... | collective-permute-start | bytes 3145736 | tf_op jit(solution)/shard_map/ppermute | solution.py:20
  775.6 32.1 %collective-permute-start.53 = (f32[2,256,1024]{2,1,0:T(8,128)}, f32[2,256,1024]{2,1,0:T(8,128)}, u32[]{:S(2)}, u32[]{:S(2)}) collective-permute-start(f32[2,256,1024]{2,1,0:T(8,128)} %bitcast.48), channel_id=1, source_target_pairs={{0,1},{1,0},{2,3},{3,2},{4,5},{5,4},{6,7},{7,6},{8,9},{9,8},{10,11... | collective-permute-start | bytes 6291464 | tf_op jit(solution)/shard_map/ppermute | solution.py:20
  811.4 36.0 %collective-permute-start.54 = (f32[256,1024]{1,0:T(8,128)}, f32[256,1024]{1,0:T(8,128)S(1)}, u32[]{:S(2)}, u32[]{:S(2)}) collective-permute-start(f32[256,1024]{1,0:T(8,128)} %slice_bitcast_fusion.8), channel_id=1, source_target_pairs={{0,2},{2,0},{1,3},{3,1},{4,6},{6,4},{5,7},{7,5},{8,10},{10,8},{9,1... | collective-permute-start | bytes 3145736 | tf_op jit(solution)/shard_map/ppermute | solution.py:20
  825.0 25.8 %collective-permute-start.67 = (f32[256,1024]{1,0:T(8,128)}, f32[256,1024]{1,0:T(8,128)}, u32[]{:S(2)}, u32[]{:S(2)}) collective-permute-start(f32[256,1024]{1,0:T(8,128)} %add.557), channel_id=1, source_target_pairs={{0,8},{8,16},{16,24},{1,9},{9,17},{17,25},{2,10},{10,18},{18,26},{... | collective-permute-start | bytes 3145736 | tf_op jit(solution)/shard_map/ppermute | solution.py:42
  858.2 150.1 %reduce-scatter.10.cloned.1.call-start = ((), (), s32[]{:S(2)}) async-start(), calls=%async_computation.19 | async-start | bytes 4718592 | tf_op jit(solution)/shard_map/reduce_scatter | solution.py:247
  858.7 149.5 %reduce-scatter.14.cloned.1.call-start = ((), (), s32[]{:S(2)}) async-start(), calls=%async_computation.21 | async-start | bytes 4718592 | tf_op jit(solution)/shard_map/reduce_scatter | solution.py:247
  870.8 32.3 %collective-permute-start.73 = (bf16[1024,768]{1,0:T(8,128)(2,1)}, bf16[1024,768]{1,0:T(8,128)(2,1)S(1)}, u32[]{:S(2)}, u32[]{:S(2)}) collective-permute-start(bf16[1024,768]{1,0:T(8,128)(2,1)} %collective-permute-done.61), channel_id=1, source_target_pairs={{16,8},{8,0},{17,9},{9,1},{18,10},{10,2},{19,11},{11,3},{20,12},{1... | collective-permute-start | bytes 4718600 | tf_op jit(solution)/shard_map/ppermute | solution.py:42
  904.3 157.5 %reduce-scatter.16.cloned.1.call-start = ((), (), s32[]{:S(2)}) async-start(), calls=%async_computation.22 | async-start | bytes 3145728 | tf_op jit(solution)/shard_map/reduce_scatter | solution.py:247
  943.1 26.4 %collective-permute-start.76 = (f32[256,1024]{1,0:T(8,128)S(1)}, f32[256,1024]{1,0:T(8,128)}, u32[]{:S(2)}, u32[]{:S(2)}) collective-permute-start(f32[256,1024]{1,0:T(8,128)S(1)} %slice_add_fusion.4), channel_id=1, source_target_pairs={{0,8},{8,16},{1,9},{9,17},{2,10},{10,18},{3,11},{11,19},{4,12},{12... | collective-permute-start | bytes 3145736 | tf_op jit(solution)/shard_map/ppermute | solution.py:42
  973.5 30.4 %collective-permute-start.78 = (f32[256,1024]{1,0:T(8,128)}, f32[256,1024]{1,0:T(8,128)S(1)}, u32[]{:S(2)}, u32[]{:S(2)}) collective-permute-start(f32[256,1024]{1,0:T(8,128)} %get-tuple-element.200), channel_id=1, source_target_pairs={{0,8},{8,16},{16,24},{1,9},{9,17},{17,25},{2,10},{10,18},{18,26},{... | collective-permute-start | bytes 3145736 | tf_op jit(solution)/shard_map/ppermute | solution.py:42
  980.1 26.0 %collective-permute-start.79 = (f32[256,1024]{1,0:T(8,128)}, f32[256,1024]{1,0:T(8,128)}, u32[]{:S(2)}, u32[]{:S(2)}) collective-permute-start(f32[256,1024]{1,0:T(8,128)} %get-tuple-element.201), channel_id=1, source_target_pairs={{24,16},{16,8},{8,0},{25,17},{17,9},{9,1},{26,18},{18,10},{10,2},{... | collective-permute-start | bytes 3145736 | tf_op jit(solution)/shard_map/ppermute | solution.py:42
  985.7 36.3 %collective-permute-start.80 = (bf16[512,384]{1,0:T(8,128)(2,1)}, bf16[512,384]{1,0:T(8,128)(2,1)}, u32[]{:S(2)}, u32[]{:S(2)}) collective-permute-start(bf16[512,384]{1,0:T(8,128)(2,1)} %get-tuple-element.307), channel_id=1, source_target_pairs={{0,16},{8,24},{16,0},{24,8},{1,17},{9,25},{17,1},{25,9},{2,18},{10... | collective-permute-start | bytes 1179656 | tf_op jit(solution)/shard_map/ppermute | solution.py:16
  1022.0 286.3 %reduce-scatter.18.cloned.1.call-start = ((), (), s32[]{:S(2)}) async-start(), calls=%async_computation.23 | async-start | bytes 4718592 | tf_op jit(solution)/shard_map/reduce_scatter | solution.py:247
  1025.8 36.1 %collective-permute-start.81 = (bf16[1024,768]{1,0:T(8,128)(2,1)}, bf16[1024,768]{1,0:T(8,128)(2,1)}, u32[]{:S(2)}, u32[]{:S(2)}) collective-permute-start(bf16[1024,768]{1,0:T(8,128)(2,1)} %get-tuple-element.281), channel_id=1, source_target_pairs={{16,24},{8,0},{17,25},{9,1},{18,26},{10,2},{19,27},{11,3},{20,28},... | collective-permute-start | bytes 4718600 | tf_op jit(solution)/shard_map/ppermute | solution.py:42
  1069.1 67.8 %collective-permute-start.90 = (bf16[512,384]{1,0:T(8,128)(2,1)}, bf16[512,384]{1,0:T(8,128)(2,1)S(1)}, u32[]{:S(2)}, u32[]{:S(2)}) collective-permute-start(bf16[512,384]{1,0:T(8,128)(2,1)} %get-tuple-element.306), channel_id=1, source_target_pairs={{0,16},{8,24},{16,0},{24,8},{1,17},{9,25},{17,1},{25,9},{2,18},{10... | collective-permute-start | bytes 1179656 | tf_op jit(solution)/shard_map/ppermute | solution.py:16
  1148.5 163.8 %reduce-scatter.20.cloned.1.call-start = ((), (), s32[]{:S(2)}) async-start(), calls=%async_computation.24 | async-start | bytes 9437184 | tf_op jit(solution)/shard_map/reduce_scatter | solution.py:247
  1151.1 55.0 %collective-permute-start.93 = (bf16[512,1536]{1,0:T(8,128)(2,1)}, bf16[512,1536]{1,0:T(8,128)(2,1)}, u32[]{:S(2)}, u32[]{:S(2)}) collective-permute-start(bf16[512,1536]{1,0:T(8,128)(2,1)} %reduce-scatter.10.cloned.1.call-done), channel_id=1, source_target_pairs={{0,24},{8,0},{16,8},{24,16},{1,25},{9,1},{17,9},{25,17},{2,26},{10... | collective-permute-start | bytes 4718600 | tf_op jit(solution)/shard_map/ppermute | solution.py:16
  1158.9 26.1 %collective-permute-start.92 = (f32[256,1024]{1,0:T(8,128)}, f32[256,1024]{1,0:T(8,128)}, u32[]{:S(2)}, u32[]{:S(2)}) collective-permute-start(f32[256,1024]{1,0:T(8,128)} %fusion.33), channel_id=1, source_target_pairs={{0,2},{2,0},{1,3},{3,1},{4,6},{6,4},{5,7},{7,5},{8,10},{10,8},{9,1... | collective-permute-start | bytes 3145736 | tf_op jit(solution)/shard_map/ppermute | solution.py:20
  1161.2 44.9 %collective-permute-start.94 = (bf16[512,384]{1,0:T(8,128)(2,1)S(1)}, bf16[512,384]{1,0:T(8,128)(2,1)S(1)}, u32[]{:S(2)}, u32[]{:S(2)}) collective-permute-start(bf16[512,384]{1,0:T(8,128)(2,1)S(1)} %copy-done.108), channel_id=1, source_target_pairs={{0,16},{8,24},{16,0},{24,8},{1,17},{9,25},{17,1},{25,9},{2,18},{10... | collective-permute-start | bytes 1179656 | tf_op jit(solution)/shard_map/ppermute | solution.py:16
  1206.9 35.4 %collective-permute-start.95 = (f32[256,1024]{1,0:T(8,128)S(1)}, f32[256,1024]{1,0:T(8,128)S(1)}, u32[]{:S(2)}, u32[]{:S(2)}) collective-permute-start(f32[256,1024]{1,0:T(8,128)S(1)} %slice_bitcast_fusion.12), channel_id=1, source_target_pairs={{0,2},{2,0},{1,3},{3,1},{4,6},{6,4},{5,7},{7,5},{8,10},{10,8},{9,1... | collective-permute-start | bytes 3145736 | tf_op jit(solution)/shard_map/ppermute | solution.py:20
  1234.3 62.8 %collective-permute-start.99 = (f32[256,1024]{1,0:T(8,128)S(1)}, f32[256,1024]{1,0:T(8,128)S(1)}, u32[]{:S(2)}, u32[]{:S(2)}) collective-permute-start(f32[256,1024]{1,0:T(8,128)S(1)} %fusion.26), channel_id=1, source_target_pairs={{0,0},{1,8},{2,16},{3,24},{8,1},{9,9},{10,17},{11,25},{16,2},{17,1... | collective-permute-start | bytes 3145736 | tf_op jit(solution)/shard_map/ppermute | solution.py:31
  1242.6 65.7 %collective-permute-start.96 = (bf16[256,1024]{1,0:T(8,128)(2,1)S(1)}, bf16[256,1024]{1,0:T(8,128)(2,1)S(1)}, u32[]{:S(2)}, u32[]{:S(2)}) collective-permute-start(bf16[256,1024]{1,0:T(8,128)(2,1)S(1)} %fusion.49), channel_id=1, source_target_pairs={{0,0},{1,8},{2,16},{3,24},{8,1},{9,9},{10,17},{11,25},{16,2},{17,1... | collective-permute-start | bytes 1572872 | tf_op jit(solution)/shard_map/ppermute | solution.py:31
  (208 other events, 3395.3 us)
Sparse Core Ops, SparseCore 0:
  15.3 44.2 all-gather.11
  61.8 44.8 all-gather.13
  184.5 46.7 all-gather.15
  232.7 44.9 all-gather.17
  279.1 33.1 all-gather.19
  403.3 28.4 all-gather.21
  435.8 27.9 all-gather.23
  467.5 25.2 all-gather.25
  494.4 27.2 all-gather.27
  547.3 45.4 all-gather.29
  675.0 45.0 reduce-scatter.7
  722.1 80.3 all-gather.31
  858.2 41.4 reduce-scatter.11
  901.9 43.3 reduce-scatter.9
  947.4 43.3 reduce-scatter.13
  1022.1 30.1 reduce-scatter.15
  1148.6 42.8 reduce-scatter.17
  1194.3 77.3 reduce-scatter.19

commit v5 on v4

--- a/solution.py
+++ b/solution.py
@@ -458,11 +458,12 @@
     grad_out = pair_scatter(grad_out)
     act_third = ring_third(*act_second)
     d_qkv, query_part, key_part = attention_backward(d_mixed, saved, query_gain, key_gain)
-    d_qkv, act_third, grad_out = together(d_qkv, act_third, grad_out)
+    d_qkv, act_third, grad_out, far_parts[3] = together(
+        d_qkv, act_third, grad_out, shift(far_parts[3], "a", 2)
+    )
     act_rows = jnp.concatenate(ring_order(act, *act_first, *act_second, act_third), axis=1)
-    d_qkv_rows, head_parts, grad_down, ffn_out, last_grad, far_parts[1] = together(
+    d_qkv_rows, grad_down, ffn_out, last_grad, far_parts[1] = together(
         ring_gather(d_qkv),
-        ring_sum(jnp.stack([query_part, key_part])),
         weight_partial(dy_rows, act_rows),
         flip_half(project_out(act_rows, wd)),
         last_grad,
@@ -480,18 +481,20 @@
     block_out = transpose_blocks((resid + flip_rest(ffn_out)).astype(bf16))
     attn_gain_part = jnp.sum(d_hidden_one * normed_one, axis=0)
     e_one = d_hidden_one * attn_gain
-    stat_one = ring_sum(jnp.sum(e_one * normed_one, axis=1, keepdims=True)) / width
+    stat_one = jnp.sum(e_one * normed_one, axis=1)
+    rows = stat_one.shape[0]
+    sums = ring_sum(jnp.concatenate([stat_one, query_part, key_part]))
+    stat_one = sums[:rows, None] / width
+    head_parts = sums[rows:]
     d_tokens = d_resid + inv_one * (e_one - normed_one * stat_one)
-    d_tokens, far_parts[3] = together(d_tokens, far_parts[3])
     d_tokens = transpose_blocks(d_tokens)
     grad_qkv = weight_grad(hidden_one, d_qkv_rows)
 
     gains = jnp.concatenate(
-        [attn_gain_part, ffn_gain_part, head_parts.reshape(-1)]
+        [attn_gain_part, ffn_gain_part, head_parts]
     ).reshape(-1, head)
     gains = gains + flip(gains, "c")
     gains = gains + flip(gains, "x")
-    far_parts[3] = shift(far_parts[3], "a", 2)
     grad_gate_up = jnp.concatenate([own_grad, last_grad, *far_parts, next_grad], axis=1)
     grad_gate = plain_columns(grad_gate_up, 0, 2)
     grad_up = plain_columns(grad_gate_up, 1, 2)

time: 1340 us -> 1330 us (level)
  waiting for transfers between devices: 759 us -> 730 us
  starting transfers between devices: 156 us -> 175 us
    ppermute x48 -> x46, waiting for transfers between devices: 201 us -> 177 us  [flip(): lax.ppermute(value, axis, [(i, i ^ mask) for i in range(lax.axis_size(axi...]
    ppermute x12, starting transfers between devices: 15.9 us -> 31.4 us  [shift(): lax.ppermute(value, axis, [(i, (i + step) % size) for i in range(size)])]
    ppermute x48 -> x46, starting transfers between devices: 33.7 us -> 29.4 us  [flip(): lax.ppermute(value, axis, [(i, i ^ mask) for i in range(lax.axis_size(axi...]
  transfers between devices with their start and end apart: 122 -> 120, of which waited for: 60 -> 60; matrix products, arithmetic and copies ran while one was open for 24% -> 25% of each run, Pallas kernels for 0% -> 0%
where the time goes in v5:
time: 1330 us; the launch traced here: 1320 us
  waiting for transfers between devices  730 us (55%)
  starting transfers between devices  175 us (13%)
  matrix products  153 us (12%)
  other arithmetic  144 us (11%)
  local copies, waits for them, and re-layouts  99.3 us (7%)
  between operations  17.5 us (1%)
    ppermute x40, waiting for transfers between devices, line(): return lax.ppermute(value, 'a', pairs)  314 us
    ppermute x46, waiting for transfers between devices, flip(): lax.ppermute(value, axis, [(i, i ^ mask) for i in range(lax.axis_size(axi...  177 us
    ppermute x12, waiting for transfers between devices, shift(): lax.ppermute(value, axis, [(i, (i + step) % size) for i in range(size)])  160 us
    dot_general x26, matrix products, dot(): lax.dot_general(left, right, (((left_dim,), (right_dim,)), ((), ())), pre...  143 us
    ppermute x40, starting transfers between devices, line(): return lax.ppermute(value, 'a', pairs)  90.5 us
    ppermute x4, waiting for transfers between devices, transpose_blocks(): return lax.ppermute(value, ('a', 'x', 'c'), pairs)  68.1 us
    unnamed x320, local copies, waits for them, and re-layouts  33.5 us
    ppermute x12, starting transfers between devices, shift(): lax.ppermute(value, axis, [(i, (i + step) % size) for i in range(size)])  31.4 us
  transfers between devices with their start and end apart: 120, of which 60 were waited for; matrix products, arithmetic and copies ran while one was open for 25% of the time, Pallas kernels for 0%

profile of v5, /device:TPU:2, one launch (start us, length us, event | category | flops | bytes accessed | tf_op | source)
XLA Modules:
  0.0 1319.2 jit_solution(3319501789422037910)
XLA Ops:
  26.4 13.5 %collective-permute-done = bf16[256,1024]{1,0:T(8,128)(2,1)S(1)} collective-permute-done((bf16[256,1024]{1,0:T(8,128)(2,1)S(1)}, bf16[256,1024]{1,0:T(8,128)(2,1)S(1)}, u32[]{:S(2)}, u32[]{:S(2)}) %collective-permute-start) | collective-permute-done | bytes 524320 | tf_op jit(solution)/shard_map/ppermute | solution.py:31
  43.8 5.3 collective-permute-done.2
  49.4 10.1 collective-permute-done.6
  63.2 6.0 fusion.95
  78.1 28.3 %collective-permute-done.8 = f32[256,1536]{1,0:T(8,128)S(1)} collective-permute-done((f32[256,1536]{1,0:T(8,128)S(1)}, f32[256,1536]{1,0:T(8,128)S(1)}, u32[]{:S(2)}, u32[]{:S(2)}) %collective-permute-start.8) | collective-permute-done | bytes 1572896 | tf_op jit(solution)/shard_map/ppermute | solution.py:42
  107.8 32.4 %collective-permute-done.10 = bf16[512,1536]{1,0:T(8,128)(2,1)S(1)} collective-permute-done((bf16[512,1536]{1,0:T(8,128)(2,1)S(1)}, bf16[512,1536]{1,0:T(8,128)(2,1)S(1)}, u32[]{:S(2)}, u32[]{:S(2)}) %collective-permute-start.10) | collective-permute-done | bytes 1572896 | tf_op jit(solution)/shard_map/ppermute | solution.py:16
  140.1 36.6 %collective-permute-done.11 = bf16[512,1536]{1,0:T(8,128)(2,1)} collective-permute-done((bf16[512,1536]{1,0:T(8,128)(2,1)}, bf16[512,1536]{1,0:T(8,128)(2,1)}, u32[]{:S(2)}, u32[]{:S(2)}) %collective-permute-start.11) | collective-permute-done | bytes 1572896 | tf_op jit(solution)/shard_map/ppermute | solution.py:16
  176.7 7.6 collective-permute-done.9
  189.5 5.3 collective-permute-start.16
  194.8 6.9 collective-permute-done.14
  203.0 26.1 %collective-permute-done.16 = bf16[256,1024]{1,0:T(8,128)(2,1)} collective-permute-done((bf16[256,1024]{1,0:T(8,128)(2,1)S(1)}, bf16[256,1024]{1,0:T(8,128)(2,1)}, u32[]{:S(2)}, u32[]{:S(2)}) %collective-permute-start.16) | collective-permute-done | bytes 524320 | tf_op jit(solution)/shard_map/ppermute | solution.py:42
  238.6 19.6 %collective-permute-done.18 = bf16[256,1024]{1,0:T(8,128)(2,1)S(1)} collective-permute-done((bf16[256,1024]{1,0:T(8,128)(2,1)S(1)}, bf16[256,1024]{1,0:T(8,128)(2,1)S(1)}, u32[]{:S(2)}, u32[]{:S(2)}) %collective-permute-start.18) | collective-permute-done | bytes 524320 | tf_op jit(solution)/shard_map/ppermute | solution.py:42
  268.0 26.4 %collective-permute-done.19 = f32[256,1536]{1,0:T(8,128)S(1)} collective-permute-done((f32[256,1536]{1,0:T(8,128)}, f32[256,1536]{1,0:T(8,128)S(1)}, u32[]{:S(2)}, u32[]{:S(2)}) %collective-permute-start.19) | collective-permute-done | bytes 1572896 | tf_op jit(solution)/shard_map/ppermute | solution.py:42
  295.5 5.4 collective-permute-done.20
  345.2 23.9 %collective-permute-done.21 = bf16[3,256,1024]{2,1,0:T(8,128)(2,1)} collective-permute-done((bf16[3,256,1024]{2,1,0:T(8,128)(2,1)}, bf16[3,256,1024]{2,1,0:T(8,128)(2,1)}, u32[]{:S(2)}, u32[]{:S(2)}) %collective-permute-start.21) | collective-permute-done | bytes 1572896 | tf_op jit(solution)/shard_map/ppermute | solution.py:20
  372.5 26.6 %collective-permute-done.24 = bf16[512,768]{1,0:T(8,128)(2,1)} collective-permute-done((bf16[512,768]{1,0:T(8,128)(2,1)}, bf16[512,768]{1,0:T(8,128)(2,1)}, u32[]{:S(2)}, u32[]{:S(2)}) %collective-permute-start.24) | collective-permute-done | bytes 786464 | tf_op jit(solution)/shard_map/ppermute | solution.py:16
  403.2 9.4 collective-permute-done.26
  418.9 14.3 %collective-permute-done.29 = bf16[256,1024]{1,0:T(8,128)(2,1)S(1)} collective-permute-done((bf16[256,1024]{1,0:T(8,128)(2,1)}, bf16[256,1024]{1,0:T(8,128)(2,1)S(1)}, u32[]{:S(2)}, u32[]{:S(2)}) %collective-permute-start.29) | collective-permute-done | bytes 524320 | tf_op jit(solution)/shard_map/ppermute | solution.py:42
  435.7 13.4 %collective-permute-done.30 = bf16[256,1024]{1,0:T(8,128)(2,1)} collective-permute-done((bf16[256,1024]{1,0:T(8,128)(2,1)}, bf16[256,1024]{1,0:T(8,128)(2,1)}, u32[]{:S(2)}, u32[]{:S(2)}) %collective-permute-start.30) | collective-permute-done | bytes 524320 | tf_op jit(solution)/shard_map/ppermute | solution.py:42
  475.4 25.1 %collective-permute-done.34 = f32[256,1024]{1,0:T(8,128)} collective-permute-done((f32[256,1024]{1,0:T(8,128)}, f32[256,1024]{1,0:T(8,128)}, u32[]{:S(2)}, u32[]{:S(2)}) %collective-permute-start.34) | collective-permute-done | bytes 1048608 | tf_op jit(solution)/shard_map/ppermute | solution.py:20
  502.9 35.9 %collective-permute-done.35 = bf16[512,1536]{1,0:T(8,128)(2,1)} collective-permute-done((bf16[512,1536]{1,0:T(8,128)(2,1)}, bf16[512,1536]{1,0:T(8,128)(2,1)}, u32[]{:S(2)}, u32[]{:S(2)}) %collective-permute-start.35) | collective-permute-done | bytes 1572896 | tf_op jit(solution)/shard_map/ppermute | solution.py:16
  573.0 8.4 collective-permute-done.46
  585.7 11.1 collective-permute-done.44
  597.0 10.5 collective-permute-done.48
  610.8 5.3 fusion.100
  616.0 6.0 collective-permute-done.51
  622.3 5.3 fusion.101
  627.8 5.4 fusion.102
  633.3 11.2 add_add_fusion
  650.8 7.2 multiply_convert_fusion.2
  664.8 5.0 fusion.76
  669.8 5.0 convolution_convert_fusion.5
  692.1 7.5 collective-permute-start.60
  711.6 8.5 reduce-scatter.8.cloned.1.call-done
  721.5 6.3 fusion.104
  735.1 18.3 %collective-permute-done.56 = f32[256,1024]{1,0:T(8,128)} collective-permute-done((f32[256,1024]{1,0:T(8,128)}, f32[256,1024]{1,0:T(8,128)}, u32[]{:S(2)}, u32[]{:S(2)}) %collective-permute-start.56) | collective-permute-done | bytes 1048608 | tf_op jit(solution)/shard_map/ppermute | solution.py:20
  754.8 16.7 %collective-permute-done.61 = bf16[1024,768]{1,0:T(8,128)(2,1)} collective-permute-done((bf16[1024,768]{1,0:T(8,128)(2,1)}, bf16[1024,768]{1,0:T(8,128)(2,1)}, u32[]{:S(2)}, u32[]{:S(2)}) %collective-permute-start.61) | collective-permute-done | bytes 1572896 | tf_op jit(solution)/shard_map/ppermute | solution.py:42
  775.5 19.1 %collective-permute-done.64 = f32[256,1024]{1,0:T(8,128)S(1)} collective-permute-done((f32[256,1024]{1,0:T(8,128)S(1)}, f32[256,1024]{1,0:T(8,128)S(1)}, u32[]{:S(2)}, u32[]{:S(2)}) %collective-permute-start.64) | collective-permute-done | bytes 1048608 | tf_op jit(solution)/shard_map/ppermute | solution.py:42
  797.6 5.0 collective-permute-start.65
  815.5 7.1 collective-permute-done.65
  825.0 6.6 collective-permute-start.67
  833.4 6.2 convolution_convert_fusion.3
  839.6 7.8 convolution_convert_fusion.4
  850.7 5.1 collective-permute-done.68
  863.4 5.4 collective-permute-done.70
  874.0 7.5 collective-permute-done.71
  882.7 20.4 %collective-permute-done.73 = bf16[1024,768]{1,0:T(8,128)(2,1)S(1)} collective-permute-done((bf16[1024,768]{1,0:T(8,128)(2,1)}, bf16[1024,768]{1,0:T(8,128)(2,1)S(1)}, u32[]{:S(2)}, u32[]{:S(2)}) %collective-permute-start.73) | collective-permute-done | bytes 1572896 | tf_op jit(solution)/shard_map/ppermute | solution.py:42
  919.1 22.6 %collective-permute-done.75 = f32[256,1024]{1,0:T(8,128)S(1)} collective-permute-done((f32[256,1024]{1,0:T(8,128)S(1)}, f32[256,1024]{1,0:T(8,128)S(1)}, u32[]{:S(2)}, u32[]{:S(2)}) %collective-permute-start.75) | collective-permute-done | bytes 1048608 | tf_op jit(solution)/shard_map/ppermute | solution.py:42
  943.1 5.4 collective-permute-start.76
  950.9 18.5 %collective-permute-done.76 = f32[256,1024]{1,0:T(8,128)} collective-permute-done((f32[256,1024]{1,0:T(8,128)S(1)}, f32[256,1024]{1,0:T(8,128)}, u32[]{:S(2)}, u32[]{:S(2)}) %collective-permute-start.76) | collective-permute-done | bytes 1048608 | tf_op jit(solution)/shard_map/ppermute | solution.py:42
  973.5 6.6 collective-permute-start.78
  992.6 11.4 collective-permute-done.78
  1008.2 13.9 %collective-permute-start.82 = (bf16[512,384]{1,0:T(8,128)(2,1)}, bf16[512,384]{1,0:T(8,128)(2,1)}, u32[]{:S(2)}, u32[]{:S(2)}) collective-permute-start(bf16[512,384]{1,0:T(8,128)(2,1)} %get-tuple-element.302), channel_id=1, source_target_pairs={{0,16},{8,24},{16,0},{24,8},{1,17},{9,25},{17,1},{25,9},{2,18},{10... | collective-permute-start | bytes 1179656 | tf_op jit(solution)/shard_map/ppermute | solution.py:16
  1022.2 11.0 collective-permute-done.80
  1079.8 7.4 collective-permute-done.83
  1094.3 9.9 fusion.21
  1114.4 10.8 convolution_convert_fusion
  1129.4 12.4 collective-permute-done.87
  1150.0 5.0 convolution_convert_fusion.1
  1170.0 21.0 %collective-permute-done.91 = f32[256,1024]{1,0:T(8,128)} collective-permute-done((f32[256,1024]{1,0:T(8,128)}, f32[256,1024]{1,0:T(8,128)}, u32[]{:S(2)}, u32[]{:S(2)}) %collective-permute-start.91) | collective-permute-done | bytes 1048608 | tf_op jit(solution)/shard_map/ppermute | solution.py:20
  1192.8 17.7 %collective-permute-done.93 = bf16[512,384]{1,0:T(8,128)(2,1)S(1)} collective-permute-done((bf16[512,384]{1,0:T(8,128)(2,1)S(1)}, bf16[512,384]{1,0:T(8,128)(2,1)S(1)}, u32[]{:S(2)}, u32[]{:S(2)}) %collective-permute-start.93) | collective-permute-done | bytes 393248 | tf_op jit(solution)/shard_map/ppermute | solution.py:16
  1238.8 11.1 collective-permute-start.95
  1254.1 37.0 %collective-permute-done.98 = f32[256,1024]{1,0:T(8,128)S(1)} collective-permute-done((f32[256,1024]{1,0:T(8,128)S(1)}, f32[256,1024]{1,0:T(8,128)S(1)}, u32[]{:S(2)}, u32[]{:S(2)}) %collective-permute-start.98) | collective-permute-done | bytes 1048608 | tf_op jit(solution)/shard_map/ppermute | solution.py:31
  1291.1 10.0 collective-permute-done.95
  (734 shorter events, 463.8 us)
Async XLA Ops:
  7.2 56.0 %all-gather.12.cloned.1.call-start = ((), (), s32[]{:S(2)}) async-start(), calls=%async_computation.7 | async-start | bytes 4718592 | tf_op jit(solution)/shard_map/all_gather | solution.py:216
  10.7 29.3 %collective-permute-start = (bf16[256,1024]{1,0:T(8,128)(2,1)S(1)}, bf16[256,1024]{1,0:T(8,128)(2,1)S(1)}, u32[]{:S(2)}, u32[]{:S(2)}) collective-permute-start(bf16[256,1024]{1,0:T(8,128)(2,1)S(1)} %copy-done.148), channel_id=1, source_target_pairs={{0,0},{1,8},{2,16},{3,24},{8,1},{9,9},{10,17},{11,25},{16,2},{17,1... | collective-permute-start | bytes 1572872 | tf_op jit(solution)/shard_map/ppermute | solution.py:31
  15.2 357.3 %all-gather.14.cloned.1.call-start = ((), (), s32[]{:S(2)}) async-start(), calls=%async_computation.8 | async-start | bytes 4718592 | tf_op jit(solution)/shard_map/all_gather | solution.py:216
  59.8 312.7 %all-gather.16.cloned.1.call-start = ((), (), s32[]{:S(2)}) async-start(), calls=%async_computation.9 | async-start | bytes 4718592 | tf_op jit(solution)/shard_map/all_gather | solution.py:216
  69.4 37.0 %collective-permute-start.8 = (f32[256,1536]{1,0:T(8,128)S(1)}, f32[256,1536]{1,0:T(8,128)S(1)}, u32[]{:S(2)}, u32[]{:S(2)}) collective-permute-start(f32[256,1536]{1,0:T(8,128)S(1)} %slice_select_fusion), channel_id=1, source_target_pairs={{0,8},{24,16},{1,9},{25,17},{2,10},{26,18},{3,11},{27,19},{4,12},{... | collective-permute-start | bytes 4718600 | tf_op jit(solution)/shard_map/ppermute | solution.py:42
  71.9 68.2 %collective-permute-start.10 = (bf16[512,1536]{1,0:T(8,128)(2,1)S(1)}, bf16[512,1536]{1,0:T(8,128)(2,1)S(1)}, u32[]{:S(2)}, u32[]{:S(2)}) collective-permute-start(bf16[512,1536]{1,0:T(8,128)(2,1)S(1)} %copy-done.77), channel_id=1, source_target_pairs={{0,24},{8,0},{16,8},{24,16},{1,25},{9,1},{17,9},{25,17},{2,26},{10... | collective-permute-start | bytes 4718600 | tf_op jit(solution)/shard_map/ppermute | solution.py:16
  75.4 101.3 %collective-permute-start.11 = (bf16[512,1536]{1,0:T(8,128)(2,1)}, bf16[512,1536]{1,0:T(8,128)(2,1)}, u32[]{:S(2)}, u32[]{:S(2)}) collective-permute-start(bf16[512,1536]{1,0:T(8,128)(2,1)} %pad_maximum_fusion.20), channel_id=1, source_target_pairs={{0,8},{8,16},{16,24},{24,0},{1,9},{9,17},{17,25},{25,1},{2,10},{10... | collective-permute-start | bytes 4718600 | tf_op jit(solution)/shard_map/ppermute | solution.py:16
  75.4 108.9 %collective-permute-start.9 = (bf16[256,1024]{1,0:T(8,128)(2,1)S(1)}, bf16[256,1024]{1,0:T(8,128)(2,1)S(1)}, u32[]{:S(2)}, u32[]{:S(2)}) collective-permute-start(bf16[256,1024]{1,0:T(8,128)(2,1)S(1)} %copy-done.149), channel_id=1, source_target_pairs={{0,0},{1,8},{2,16},{3,24},{8,1},{9,9},{10,17},{11,25},{16,2},{17,1... | collective-permute-start | bytes 1572872 | tf_op jit(solution)/shard_map/ppermute | solution.py:31
  184.4 188.1 %all-gather.18.cloned.1.call-start = ((), (), s32[]{:S(2)}) async-start(), calls=%async_computation.10 | async-start | bytes 4718592 | tf_op jit(solution)/shard_map/all_gather | solution.py:216
  184.9 275.0 %all-gather.20.cloned.1.call-start = ((), (), s32[]{:S(2)}) async-start(), calls=%async_computation.11 | async-start | bytes 3145728 | tf_op jit(solution)/shard_map/all_gather | solution.py:216
  185.0 49.0 %collective-permute-start.12 = (f32[256,1536]{1,0:T(8,128)}, f32[256,1536]{1,0:T(8,128)S(1)}, u32[]{:S(2)}, u32[]{:S(2)}) collective-permute-start(f32[256,1536]{1,0:T(8,128)} %slice_add_fusion), channel_id=1, source_target_pairs={{0,8},{8,16},{1,9},{9,17},{2,10},{10,18},{3,11},{11,19},{4,12},{12... | collective-permute-start | bytes 4718600 | tf_op jit(solution)/shard_map/ppermute | solution.py:42
  186.4 47.6 %collective-permute-start.13 = (f32[256,1536]{1,0:T(8,128)}, f32[256,1536]{1,0:T(8,128)}, u32[]{:S(2)}, u32[]{:S(2)}) collective-permute-start(f32[256,1536]{1,0:T(8,128)} %slice_add_fusion), channel_id=1, source_target_pairs={{24,16},{16,8},{25,17},{17,9},{26,18},{18,10},{27,19},{19,11},{28,... | collective-permute-start | bytes 4718600 | tf_op jit(solution)/shard_map/ppermute | solution.py:42
  189.5 39.6 %collective-permute-start.16 = (bf16[256,1024]{1,0:T(8,128)(2,1)S(1)}, bf16[256,1024]{1,0:T(8,128)(2,1)}, u32[]{:S(2)}, u32[]{:S(2)}) collective-permute-start(bf16[256,1024]{1,0:T(8,128)(2,1)S(1)} %collective-permute-done.9), channel_id=1, source_target_pairs={{0,8},{8,16},{16,24},{1,9},{9,17},{17,25},{2,10},{10,18},{18,26},{... | collective-permute-start | bytes 1572872 | tf_op jit(solution)/shard_map/ppermute | solution.py:42
  201.7 28.8 %collective-permute-start.15 = (bf16[256,1024]{1,0:T(8,128)(2,1)S(1)}, bf16[256,1024]{1,0:T(8,128)(2,1)}, u32[]{:S(2)}, u32[]{:S(2)}) collective-permute-start(bf16[256,1024]{1,0:T(8,128)(2,1)S(1)} %collective-permute-done.14), channel_id=1, source_target_pairs={{16,8},{8,0},{17,9},{9,1},{18,10},{10,2},{19,11},{11,3},{20,12},{1... | collective-permute-start | bytes 1572872 | tf_op jit(solution)/shard_map/ppermute | solution.py:42
  259.0 35.3 %collective-permute-start.19 = (f32[256,1536]{1,0:T(8,128)}, f32[256,1536]{1,0:T(8,128)S(1)}, u32[]{:S(2)}, u32[]{:S(2)}) collective-permute-start(f32[256,1536]{1,0:T(8,128)} %get-tuple-element.130), channel_id=1, source_target_pairs={{0,8},{8,16},{16,24},{1,9},{9,17},{17,25},{2,10},{10,18},{18,26},{... | collective-permute-start | bytes 4718600 | tf_op jit(solution)/shard_map/ppermute | solution.py:42
  260.6 40.3 %collective-permute-start.20 = (f32[256,1536]{1,0:T(8,128)}, f32[256,1536]{1,0:T(8,128)}, u32[]{:S(2)}, u32[]{:S(2)}) collective-permute-start(f32[256,1536]{1,0:T(8,128)} %get-tuple-element.131), channel_id=1, source_target_pairs={{24,16},{16,8},{8,0},{25,17},{17,9},{9,1},{26,18},{18,10},{10,2},{... | collective-permute-start | bytes 4718600 | tf_op jit(solution)/shard_map/ppermute | solution.py:42
  261.9 286.9 %all-gather.22.cloned.1.call-start = ((), (), s32[]{:S(2)}) async-start(), calls=%async_computation.12 | async-start | bytes 2359296 | tf_op jit(solution)/shard_map/all_gather | solution.py:216
  309.4 33.9 %collective-permute-start.22 = (bf16[2,256,1024]{2,1,0:T(8,128)(2,1)}, bf16[2,256,1024]{2,1,0:T(8,128)(2,1)}, u32[]{:S(2)}, u32[]{:S(2)}) collective-permute-start(bf16[2,256,1024]{2,1,0:T(8,128)(2,1)} %get-tuple-element.323), channel_id=1, source_target_pairs={{0,2},{2,0},{1,3},{3,1},{4,6},{6,4},{5,7},{7,5},{8,10},{10,8},{9,1... | collective-permute-start | bytes 3145736 | tf_op jit(solution)/shard_map/ppermute | solution.py:20
  312.5 56.6 %collective-permute-start.21 = (bf16[3,256,1024]{2,1,0:T(8,128)(2,1)}, bf16[3,256,1024]{2,1,0:T(8,128)(2,1)}, u32[]{:S(2)}, u32[]{:S(2)}) collective-permute-start(bf16[3,256,1024]{2,1,0:T(8,128)(2,1)} %get-tuple-element.309), channel_id=1, source_target_pairs={{0,2},{2,0},{1,3},{3,1},{4,6},{6,4},{5,7},{7,5},{8,10},{10,8},{9,1... | collective-permute-start | bytes 4718600 | tf_op jit(solution)/shard_map/ppermute | solution.py:20
  326.5 45.9 %collective-permute-start.23 = (bf16[512,768]{1,0:T(8,128)(2,1)}, bf16[512,768]{1,0:T(8,128)(2,1)}, u32[]{:S(2)}, u32[]{:S(2)}) collective-permute-start(bf16[512,768]{1,0:T(8,128)(2,1)} %get-tuple-element.147), channel_id=1, source_target_pairs={{0,24},{8,0},{16,8},{24,16},{1,25},{9,1},{17,9},{25,17},{2,26},{10... | collective-permute-start | bytes 2359304 | tf_op jit(solution)/shard_map/ppermute | solution.py:16
  329.7 69.4 %collective-permute-start.24 = (bf16[512,768]{1,0:T(8,128)(2,1)}, bf16[512,768]{1,0:T(8,128)(2,1)}, u32[]{:S(2)}, u32[]{:S(2)}) collective-permute-start(bf16[512,768]{1,0:T(8,128)(2,1)} %get-tuple-element.148), channel_id=1, source_target_pairs={{0,16},{8,24},{16,0},{24,8},{1,17},{9,25},{17,1},{25,9},{2,18},{10... | collective-permute-start | bytes 2359304 | tf_op jit(solution)/shard_map/ppermute | solution.py:16
  330.7 68.4 %collective-permute-start.25 = (bf16[512,768]{1,0:T(8,128)(2,1)}, bf16[512,768]{1,0:T(8,128)(2,1)}, u32[]{:S(2)}, u32[]{:S(2)}) collective-permute-start(bf16[512,768]{1,0:T(8,128)(2,1)} %get-tuple-element.149), channel_id=1, source_target_pairs={{0,8},{8,16},{16,24},{24,0},{1,9},{9,17},{17,25},{25,1},{2,10},{10... | collective-permute-start | bytes 2359304 | tf_op jit(solution)/shard_map/ppermute | solution.py:16
  399.1 56.4 %collective-permute-start.31 = (bf16[3,2,256,1024]{3,2,0,1:T(8,128)(2,1)}, bf16[3,2,256,1024]{3,2,0,1:T(8,128)(2,1)}, u32[]{:S(2)}, u32[]{:S(2)}) collective-permute-start(bf16[3,2,256,1024]{3,2,0,1:T(8,128)(2,1)} %pad_maximum_fusion.1), channel_id=1, source_target_pairs={{0,1},{1,0},{2,3},{3,2},{4,5},{5,4},{6,7},{7,6},{8,9},{9,8},{10,11... | collective-permute-start | bytes 9437192 | tf_op jit(solution)/shard_map/ppermute | solution.py:20
  402.8 49.1 %collective-permute-start.32 = (bf16[2,2,256,1024]{3,2,0,1:T(8,128)(2,1)S(1)}, bf16[2,2,256,1024]{3,2,0,1:T(8,128)(2,1)}, u32[]{:S(2)}, u32[]{:S(2)}) collective-permute-start(bf16[2,2,256,1024]{3,2,0,1:T(8,128)(2,1)S(1)} %pad_maximum_fusion.9), channel_id=1, source_target_pairs={{0,1},{1,0},{2,3},{3,2},{4,5},{5,4},{6,7},{7,6},{8,9},{9,8},{10,11... | collective-permute-start | bytes 6291464 | tf_op jit(solution)/shard_map/ppermute | solution.py:20
  403.1 145.7 %all-gather.24.cloned.1.call-start = ((), (), s32[]{:S(2)}) async-start(), calls=%async_computation.13 | async-start | bytes 2359296 | tf_op jit(solution)/shard_map/all_gather | solution.py:216
  435.6 113.2 %all-gather.26.cloned.1.call-start = ((), (), s32[]{:S(2)}) async-start(), calls=%async_computation.14 | async-start | bytes 2359296 | tf_op jit(solution)/shard_map/all_gather | solution.py:216
  467.4 81.5 %all-gather.28.cloned.1.call-start = ((), (), s32[]{:S(2)}) async-start(), calls=%async_computation.15 | async-start | bytes 2359296 | tf_op jit(solution)/shard_map/all_gather | solution.py:216
  467.9 70.9 %collective-permute-start.35 = (bf16[512,1536]{1,0:T(8,128)(2,1)}, bf16[512,1536]{1,0:T(8,128)(2,1)}, u32[]{:S(2)}, u32[]{:S(2)}) collective-permute-start(bf16[512,1536]{1,0:T(8,128)(2,1)} %pad_maximum_fusion.19), channel_id=1, source_target_pairs={{0,16},{8,24},{16,0},{24,8},{1,17},{9,25},{17,1},{25,9},{2,18},{10... | collective-permute-start | bytes 4718600 | tf_op jit(solution)/shard_map/ppermute | solution.py:16
  475.3 158.0 %all-gather.30.cloned.1.call-start = ((), (), s32[]{:S(2)}) async-start(), calls=%async_computation.16 | async-start | bytes 4718592 | tf_op jit(solution)/shard_map/all_gather | solution.py:216
  547.2 172.9 %reduce-scatter.8.cloned.1.call-start = ((), (), s32[]{:S(2)}) async-start(), calls=%async_computation.17 | async-start | bytes 4718592 | tf_op jit(solution)/shard_map/reduce_scatter | solution.py:247
  570.7 38.7 %collective-permute-start.39 = (bf16[512,1024]{1,0:T(8,128)(2,1)S(1)}, bf16[512,1024]{1,0:T(8,128)(2,1)S(1)}, u32[]{:S(2)}, u32[]{:S(2)}) collective-permute-start(bf16[512,1024]{1,0:T(8,128)(2,1)S(1)} %pad_maximum_fusion.26), channel_id=1, source_target_pairs={{0,1},{1,0},{2,3},{3,2},{4,5},{5,4},{6,7},{7,6},{8,9},{9,8},{10,11... | collective-permute-start | bytes 3145736 | tf_op jit(solution)/shard_map/ppermute | solution.py:20
  581.4 26.3 %collective-permute-start.50 = (bf16[256,1024]{1,0:T(8,128)(2,1)S(1)}, bf16[256,1024]{1,0:T(8,128)(2,1)S(1)}, u32[]{:S(2)}, u32[]{:S(2)}) collective-permute-start(bf16[256,1024]{1,0:T(8,128)(2,1)S(1)} %get-tuple-element.318), channel_id=1, source_target_pairs={{16,24},{8,0},{17,25},{9,1},{18,26},{10,2},{19,27},{11,3},{20,28},... | collective-permute-start | bytes 1572872 | tf_op jit(solution)/shard_map/ppermute | solution.py:42
  585.6 36.6 %collective-permute-start.42 = (bf16[512,1024]{1,0:T(8,128)(2,1)S(1)}, bf16[512,1024]{1,0:T(8,128)(2,1)S(1)}, u32[]{:S(2)}, u32[]{:S(2)}) collective-permute-start(bf16[512,1024]{1,0:T(8,128)(2,1)S(1)} %pad_maximum_fusion.27), channel_id=1, source_target_pairs={{0,1},{1,0},{2,3},{3,2},{4,5},{5,4},{6,7},{7,6},{8,9},{9,8},{10,11... | collective-permute-start | bytes 3145736 | tf_op jit(solution)/shard_map/ppermute | solution.py:20
  596.8 30.8 %collective-permute-start.45 = (bf16[512,1024]{1,0:T(8,128)(2,1)S(1)}, bf16[512,1024]{1,0:T(8,128)(2,1)S(1)}, u32[]{:S(2)}, u32[]{:S(2)}) collective-permute-start(bf16[512,1024]{1,0:T(8,128)(2,1)S(1)} %pad_maximum_fusion.28), channel_id=1, source_target_pairs={{0,1},{1,0},{2,3},{3,2},{4,5},{5,4},{6,7},{7,6},{8,9},{9,8},{10,11... | collective-permute-start | bytes 3145736 | tf_op jit(solution)/shard_map/ppermute | solution.py:20
  674.9 240.7 %all-gather.32.cloned.1.call-start = ((), (), s32[]{:S(2)}) async-start(), calls=%async_computation.18 | async-start | bytes 9437184 | tf_op jit(solution)/shard_map/all_gather | solution.py:216
  692.0 291.0 %reduce-scatter.12.cloned.1.call-start = ((), (), s32[]{:S(2)}) async-start(), calls=%async_computation.20 | async-start | bytes 4718592 | tf_op jit(solution)/shard_map/reduce_scatter | solution.py:247
  692.1 62.7 %collective-permute-start.60 = (bf16[1024,768]{1,0:T(8,128)(2,1)}, bf16[1024,768]{1,0:T(8,128)(2,1)}, u32[]{:S(2)}, u32[]{:S(2)}) collective-permute-start(bf16[1024,768]{1,0:T(8,128)(2,1)} %get-tuple-element.248), channel_id=1, source_target_pairs={{0,8},{8,16},{16,24},{1,9},{9,17},{17,25},{2,10},{10,18},{18,26},{... | collective-permute-start | bytes 4718600 | tf_op jit(solution)/shard_map/ppermute | solution.py:42
  699.5 71.9 %collective-permute-start.61 = (bf16[1024,768]{1,0:T(8,128)(2,1)}, bf16[1024,768]{1,0:T(8,128)(2,1)}, u32[]{:S(2)}, u32[]{:S(2)}) collective-permute-start(bf16[1024,768]{1,0:T(8,128)(2,1)} %get-tuple-element.248), channel_id=1, source_target_pairs={{24,16},{16,8},{8,0},{25,17},{17,9},{9,1},{26,18},{18,10},{10,2},{... | collective-permute-start | bytes 4718600 | tf_op jit(solution)/shard_map/ppermute | solution.py:42
  704.5 26.3 %collective-permute-start.58 = (f32[256,1024]{1,0:T(8,128)}, f32[256,1024]{1,0:T(8,128)S(1)}, u32[]{:S(2)}, u32[]{:S(2)}) collective-permute-start(f32[256,1024]{1,0:T(8,128)} %slice_bitcast_fusion.4), channel_id=1, source_target_pairs={{0,2},{2,0},{1,3},{3,1},{4,6},{6,4},{5,7},{7,5},{8,10},{10,8},{9,1... | collective-permute-start | bytes 3145736 | tf_op jit(solution)/shard_map/ppermute | solution.py:20
  710.7 42.7 %collective-permute-start.56 = (f32[256,1024]{1,0:T(8,128)}, f32[256,1024]{1,0:T(8,128)}, u32[]{:S(2)}, u32[]{:S(2)}) collective-permute-start(f32[256,1024]{1,0:T(8,128)} %slice_bitcast_fusion.6), channel_id=1, source_target_pairs={{0,2},{2,0},{1,3},{3,1},{4,6},{6,4},{5,7},{7,5},{8,10},{10,8},{9,1... | collective-permute-start | bytes 3145736 | tf_op jit(solution)/shard_map/ppermute | solution.py:20
  720.1 51.4 %collective-permute-start.59 = (bf16[512,1536]{1,0:T(8,128)(2,1)}, bf16[512,1536]{1,0:T(8,128)(2,1)S(1)}, u32[]{:S(2)}, u32[]{:S(2)}) collective-permute-start(bf16[512,1536]{1,0:T(8,128)(2,1)} %reduce-scatter.8.cloned.1.call-done), channel_id=1, source_target_pairs={{0,8},{8,16},{16,24},{24,0},{1,9},{9,17},{17,25},{25,1},{2,10},{10... | collective-permute-start | bytes 4718600 | tf_op jit(solution)/shard_map/ppermute | solution.py:16
  731.8 43.7 %collective-permute-start.63 = (f32[256,1024]{1,0:T(8,128)S(1)}, f32[256,1024]{1,0:T(8,128)S(1)}, u32[]{:S(2)}, u32[]{:S(2)}) collective-permute-start(f32[256,1024]{1,0:T(8,128)S(1)} %slice_bitcast_fusion.2), channel_id=1, source_target_pairs={{0,2},{2,0},{1,3},{3,1},{4,6},{6,4},{5,7},{7,5},{8,10},{10,8},{9,1... | collective-permute-start | bytes 3145736 | tf_op jit(solution)/shard_map/ppermute | solution.py:20
  775.5 32.0 %collective-permute-start.53 = (f32[2,256,1024]{2,1,0:T(8,128)}, f32[2,256,1024]{2,1,0:T(8,128)}, u32[]{:S(2)}, u32[]{:S(2)}) collective-permute-start(f32[2,256,1024]{2,1,0:T(8,128)} %bitcast.48), channel_id=1, source_target_pairs={{0,1},{1,0},{2,3},{3,2},{4,5},{5,4},{6,7},{7,6},{8,9},{9,8},{10,11... | collective-permute-start | bytes 6291464 | tf_op jit(solution)/shard_map/ppermute | solution.py:20
  811.4 36.1 %collective-permute-start.54 = (f32[256,1024]{1,0:T(8,128)}, f32[256,1024]{1,0:T(8,128)S(1)}, u32[]{:S(2)}, u32[]{:S(2)}) collective-permute-start(f32[256,1024]{1,0:T(8,128)} %slice_bitcast_fusion.8), channel_id=1, source_target_pairs={{0,2},{2,0},{1,3},{3,1},{4,6},{6,4},{5,7},{7,5},{8,10},{10,8},{9,1... | collective-permute-start | bytes 3145736 | tf_op jit(solution)/shard_map/ppermute | solution.py:20
  825.0 25.8 %collective-permute-start.67 = (f32[256,1024]{1,0:T(8,128)}, f32[256,1024]{1,0:T(8,128)}, u32[]{:S(2)}, u32[]{:S(2)}) collective-permute-start(f32[256,1024]{1,0:T(8,128)} %add.551), channel_id=1, source_target_pairs={{0,8},{8,16},{16,24},{1,9},{9,17},{17,25},{2,10},{10,18},{18,26},{... | collective-permute-start | bytes 3145736 | tf_op jit(solution)/shard_map/ppermute | solution.py:42
  858.1 164.0 %reduce-scatter.10.cloned.1.call-start = ((), (), s32[]{:S(2)}) async-start(), calls=%async_computation.19 | async-start | bytes 4718592 | tf_op jit(solution)/shard_map/reduce_scatter | solution.py:247
  858.7 163.4 %reduce-scatter.14.cloned.1.call-start = ((), (), s32[]{:S(2)}) async-start(), calls=%async_computation.21 | async-start | bytes 4718592 | tf_op jit(solution)/shard_map/reduce_scatter | solution.py:247
  870.8 32.3 %collective-permute-start.73 = (bf16[1024,768]{1,0:T(8,128)(2,1)}, bf16[1024,768]{1,0:T(8,128)(2,1)S(1)}, u32[]{:S(2)}, u32[]{:S(2)}) collective-permute-start(bf16[1024,768]{1,0:T(8,128)(2,1)} %collective-permute-done.61), channel_id=1, source_target_pairs={{16,8},{8,0},{17,9},{9,1},{18,10},{10,2},{19,11},{11,3},{20,12},{1... | collective-permute-start | bytes 4718600 | tf_op jit(solution)/shard_map/ppermute | solution.py:42
  904.3 168.3 %reduce-scatter.16.cloned.1.call-start = ((), (), s32[]{:S(2)}) async-start(), calls=%async_computation.22 | async-start | bytes 3145728 | tf_op jit(solution)/shard_map/reduce_scatter | solution.py:247
  943.1 26.4 %collective-permute-start.76 = (f32[256,1024]{1,0:T(8,128)S(1)}, f32[256,1024]{1,0:T(8,128)}, u32[]{:S(2)}, u32[]{:S(2)}) collective-permute-start(f32[256,1024]{1,0:T(8,128)S(1)} %slice_add_fusion.4), channel_id=1, source_target_pairs={{0,8},{8,16},{1,9},{9,17},{2,10},{10,18},{3,11},{11,19},{4,12},{12... | collective-permute-start | bytes 3145736 | tf_op jit(solution)/shard_map/ppermute | solution.py:42
  973.5 30.4 %collective-permute-start.78 = (f32[256,1024]{1,0:T(8,128)}, f32[256,1024]{1,0:T(8,128)S(1)}, u32[]{:S(2)}, u32[]{:S(2)}) collective-permute-start(f32[256,1024]{1,0:T(8,128)} %get-tuple-element.198), channel_id=1, source_target_pairs={{0,8},{8,16},{16,24},{1,9},{9,17},{17,25},{2,10},{10,18},{18,26},{... | collective-permute-start | bytes 3145736 | tf_op jit(solution)/shard_map/ppermute | solution.py:42
  980.1 26.0 %collective-permute-start.79 = (f32[256,1024]{1,0:T(8,128)}, f32[256,1024]{1,0:T(8,128)}, u32[]{:S(2)}, u32[]{:S(2)}) collective-permute-start(f32[256,1024]{1,0:T(8,128)} %get-tuple-element.199), channel_id=1, source_target_pairs={{24,16},{16,8},{8,0},{25,17},{17,9},{9,1},{26,18},{18,10},{10,2},{... | collective-permute-start | bytes 3145736 | tf_op jit(solution)/shard_map/ppermute | solution.py:42
  985.7 47.5 %collective-permute-start.80 = (bf16[512,384]{1,0:T(8,128)(2,1)}, bf16[512,384]{1,0:T(8,128)(2,1)}, u32[]{:S(2)}, u32[]{:S(2)}) collective-permute-start(bf16[512,384]{1,0:T(8,128)(2,1)} %get-tuple-element.303), channel_id=1, source_target_pairs={{0,16},{8,24},{16,0},{24,8},{1,17},{9,25},{17,1},{25,9},{2,18},{10... | collective-permute-start | bytes 1179656 | tf_op jit(solution)/shard_map/ppermute | solution.py:16
  1008.2 62.2 %collective-permute-start.82 = (bf16[512,384]{1,0:T(8,128)(2,1)}, bf16[512,384]{1,0:T(8,128)(2,1)}, u32[]{:S(2)}, u32[]{:S(2)}) collective-permute-start(bf16[512,384]{1,0:T(8,128)(2,1)} %get-tuple-element.302), channel_id=1, source_target_pairs={{0,16},{8,24},{16,0},{24,8},{1,17},{9,25},{17,1},{25,9},{2,18},{10... | collective-permute-start | bytes 1179656 | tf_op jit(solution)/shard_map/ppermute | solution.py:16
  1033.2 267.9 %reduce-scatter.18.cloned.1.call-start = ((), (), s32[]{:S(2)}) async-start(), calls=%async_computation.23 | async-start | bytes 4718592 | tf_op jit(solution)/shard_map/reduce_scatter | solution.py:247
  1037.0 35.6 %collective-permute-start.81 = (bf16[1024,768]{1,0:T(8,128)(2,1)}, bf16[1024,768]{1,0:T(8,128)(2,1)}, u32[]{:S(2)}, u32[]{:S(2)}) collective-permute-start(bf16[1024,768]{1,0:T(8,128)(2,1)} %get-tuple-element.277), channel_id=1, source_target_pairs={{16,24},{8,0},{17,25},{9,1},{18,26},{10,2},{19,27},{11,3},{20,28},... | collective-permute-start | bytes 4718600 | tf_op jit(solution)/shard_map/ppermute | solution.py:42
  1106.7 36.8 %collective-permute-start.89 = (bf16[512,384]{1,0:T(8,128)(2,1)S(1)}, bf16[512,384]{1,0:T(8,128)(2,1)}, u32[]{:S(2)}, u32[]{:S(2)}) collective-permute-start(bf16[512,384]{1,0:T(8,128)(2,1)S(1)} %copy-done.111), channel_id=1, source_target_pairs={{0,16},{8,24},{16,0},{24,8},{1,17},{9,25},{17,1},{25,9},{2,18},{10... | collective-permute-start | bytes 1179656 | tf_op jit(solution)/shard_map/ppermute | solution.py:16
  1112.9 29.0 %collective-permute-start.87 = (bf16[256,1536]{1,0:T(8,128)(2,1)}, bf16[256,1536]{1,0:T(8,128)(2,1)}, u32[]{:S(2)}, u32[]{:S(2)}) collective-permute-start(bf16[256,1536]{1,0:T(8,128)(2,1)} %get-tuple-element.307), channel_id=1, source_target_pairs={{16,24},{8,0},{17,25},{9,1},{18,26},{10,2},{19,27},{11,3},{20,28},... | collective-permute-start | bytes 2359304 | tf_op jit(solution)/shard_map/ppermute | solution.py:42
  1155.1 150.0 %reduce-scatter.20.cloned.1.call-start = ((), (), s32[]{:S(2)}) async-start(), calls=%async_computation.24 | async-start | bytes 9437184 | tf_op jit(solution)/shard_map/reduce_scatter | solution.py:247
  1157.7 52.8 %collective-permute-start.92 = (bf16[512,1536]{1,0:T(8,128)(2,1)}, bf16[512,1536]{1,0:T(8,128)(2,1)}, u32[]{:S(2)}, u32[]{:S(2)}) collective-permute-start(bf16[512,1536]{1,0:T(8,128)(2,1)} %reduce-scatter.10.cloned.1.call-done), channel_id=1, source_target_pairs={{0,24},{8,0},{16,8},{24,16},{1,25},{9,1},{17,9},{25,17},{2,26},{10... | collective-permute-start | bytes 4718600 | tf_op jit(solution)/shard_map/ppermute | solution.py:16
  1166.7 43.8 %collective-permute-start.93 = (bf16[512,384]{1,0:T(8,128)(2,1)S(1)}, bf16[512,384]{1,0:T(8,128)(2,1)S(1)}, u32[]{:S(2)}, u32[]{:S(2)}) collective-permute-start(bf16[512,384]{1,0:T(8,128)(2,1)S(1)} %copy-done.110), channel_id=1, source_target_pairs={{0,16},{8,24},{16,0},{24,8},{1,17},{9,25},{17,1},{25,9},{2,18},{10... | collective-permute-start | bytes 1179656 | tf_op jit(solution)/shard_map/ppermute | solution.py:16
  1211.7 26.8 %collective-permute-start.94 = (f32[256,1024]{1,0:T(8,128)S(1)}, f32[256,1024]{1,0:T(8,128)S(1)}, u32[]{:S(2)}, u32[]{:S(2)}) collective-permute-start(f32[256,1024]{1,0:T(8,128)S(1)} %slice_bitcast_fusion.12), channel_id=1, source_target_pairs={{0,2},{2,0},{1,3},{3,1},{4,6},{6,4},{5,7},{7,5},{8,10},{10,8},{9,1... | collective-permute-start | bytes 3145736 | tf_op jit(solution)/shard_map/ppermute | solution.py:20
  1228.2 62.9 %collective-permute-start.98 = (f32[256,1024]{1,0:T(8,128)S(1)}, f32[256,1024]{1,0:T(8,128)S(1)}, u32[]{:S(2)}, u32[]{:S(2)}) collective-permute-start(f32[256,1024]{1,0:T(8,128)S(1)} %fusion.26), channel_id=1, source_target_pairs={{0,0},{1,8},{2,16},{3,24},{8,1},{9,9},{10,17},{11,25},{16,2},{17,1... | collective-permute-start | bytes 3145736 | tf_op jit(solution)/shard_map/ppermute | solution.py:31
  1238.8 62.2 %collective-permute-start.95 = (bf16[256,1024]{1,0:T(8,128)(2,1)S(1)}, bf16[256,1024]{1,0:T(8,128)(2,1)S(1)}, u32[]{:S(2)}, u32[]{:S(2)}) collective-permute-start(bf16[256,1024]{1,0:T(8,128)(2,1)S(1)} %fusion.49), channel_id=1, source_target_pairs={{0,0},{1,8},{2,16},{3,24},{8,1},{9,9},{10,17},{11,25},{16,2},{17,1... | collective-permute-start | bytes 1572872 | tf_op jit(solution)/shard_map/ppermute | solution.py:31
  (206 other events, 3408.0 us)
Sparse Core Ops, SparseCore 0:
  15.3 44.2 all-gather.11
  61.8 44.8 all-gather.13
  184.5 46.7 all-gather.15
  232.7 44.9 all-gather.17
  279.1 33.1 all-gather.19
  403.3 28.4 all-gather.21
  435.7 27.9 all-gather.23
  467.5 25.2 all-gather.25
  494.4 27.2 all-gather.27
  547.3 45.4 all-gather.29
  675.0 45.0 reduce-scatter.7
  722.1 80.3 all-gather.31
  858.2 41.5 reduce-scatter.11
  901.9 43.3 reduce-scatter.9
  947.5 43.3 reduce-scatter.13
  1033.3 29.8 reduce-scatter.15
  1155.2 41.0 reduce-scatter.17
  1199.0 77.2 reduce-scatter.19
